TPU v7x, 256 devices: a whole 4x4x8 slice. The times are simulated.
256 devices in a mesh: work: 32 (over y, x, core), tile: 8 (over z).
Axes of the slice: x: 4, y: 4, z: 8, core: 2. Of those that a mesh axis runs over, the one named last changes fastest.
Arguments:
- block_coords: float32 [32768, 3, 128], P(('work', 'tile')), may hold values from -6 to 6
- block_visibilities: float32 [32768, 4, 128], P(('work', 'tile')), may hold values from -6 to 6
- subgrid_of_block: int32 [32768], P(('work', 'tile')), may hold values from 0 to 511, as said below
- live_blocks: int32 [256], P(('work', 'tile')), may hold values from 96 to 128, as said below
- corners: int32 [512, 2], replicated, may hold values from 0 to 4064, as said below
- channel_scale: float32 [2], replicated, may hold values from 0.85 to 1.15
Outputs:
- uv_grid: float32 [4, 512, 4096], P(None, 'tile', 'work')
Inputs may be any that keep to these rules, and one draw needn't show every extreme that they name: `subgrid_of_block`: subgrid s belongs to the strip of worker s // 16. Among the 128 blocks of one device at most 16 belong to subgrids of one worker, and some worker gets exactly 16 blocks from every device. Device d in the order of the axes work, tile holds the blocks d * 128 to (d + 1) * 128 - 1; its first live_blocks[d] blocks are live, the others take no part. Some device has all its blocks live. Subgrid s covers rows corners[s, 0] to corners[s, 0] + 31 of the window, and columns corners[s, 1] to corners[s, 1] + 31, all inside columns 128 (s // 16) to 128 (s // 16 + 1) - 1.
All inputs are finite; a program needn't handle non-finite values.
Results may differ from a plain program's by a relative error of at most 0.0003.
Values sent between devices are 32-bit elements; how exact they have to be, the bound alone decides.
No kernel may reach another device: no remote copies, remote signals or barrier semaphores. Data moves between devices by JAX's collectives and lax.ppermute only.
A program may use at most 192 MiB of HBM per device.

v0:
```python
import math

import jax
import jax.numpy as jnp
from jax import lax
from jax.sharding import PartitionSpec as P

CH = 2
SUB = 32
ROWS = 128
TR = 64
GCW = 128
SUBW = 16


two_pi = 2.0 * math.pi
highest = lax.Precision.HIGHEST


def cut_along(value, dim, length):
    lengths = value.shape
    blocks = value.reshape(*lengths[:dim], length, lengths[dim] // length, *lengths[dim + 1 :])
    return jnp.moveaxis(blocks, dim, 0)


def sent_and_summed(value, axis, dim):
    blocks = cut_along(value, dim, lax.axis_size(axis))
    arrived = lax.all_to_all(blocks, axis, split_axis=0, concat_axis=0, tiled=True)
    return arrived.sum(axis=0)


def pixel_offsets():
    return (jnp.arange(SUB, dtype=jnp.float32) - SUB // 2) / SUB


def block_pictures(coords, waves, channel_scale):
    offsets = pixel_offsets()
    squares = offsets * offsets
    layers = []
    for channel in range(CH):
        factor = channel_scale[channel]
        first_coord = coords[:, 0, :] * factor
        second_coord = coords[:, 1, :] * factor
        depth_coord = coords[:, 2, :] * factor
        depth_term = depth_coord[:, None, :] * squares[None, :, None]
        phase_first = two_pi * (first_coord[:, None, :] * offsets[None, :, None] + depth_term)
        phase_second = two_pi * (second_coord[:, None, :] * offsets[None, :, None] + depth_term)
        wave_real = waves[:, 2 * channel, :][:, None, :]
        wave_imag = waves[:, 2 * channel + 1, :][:, None, :]
        cosine_first = jnp.cos(phase_first)
        sine_first = jnp.sin(phase_first)
        cosine_second = jnp.cos(phase_second)
        sine_second = jnp.sin(phase_second)
        left_side = jnp.concatenate(
            [
                wave_real * cosine_first - wave_imag * sine_first,
                wave_real * sine_first + wave_imag * cosine_first,
            ],
            axis=2,
        )
        right_real = jnp.concatenate([cosine_second, -sine_second], axis=2)
        right_imag = jnp.concatenate([sine_second, cosine_second], axis=2)
        right_side = jnp.concatenate([right_real, right_imag], axis=1)
        layers.append(jnp.einsum("nxk,njk->nxj", left_side, right_side, precision=highest))
    return jnp.stack(layers, axis=1)


def transform_matrix():
    offsets = jnp.arange(SUB, dtype=jnp.int32)
    taper_values = jnp.sin(jnp.pi * (offsets.astype(jnp.float32) + 0.5) / SUB) ** 2
    product = offsets[:, None] * offsets[None, :] % SUB
    angles = two_pi * product.astype(jnp.float32) / SUB
    real_part = taper_values[:, None] * jnp.cos(angles)
    imag_part = -taper_values[:, None] * jnp.sin(angles)
    upper = jnp.concatenate([real_part, imag_part], axis=1)
    lower = jnp.concatenate([-imag_part, real_part], axis=1)
    return jnp.concatenate([upper, lower], axis=0)


def to_spectrum(pictures):
    amount = pictures.shape[0]
    matrix = transform_matrix()
    first = jnp.einsum("ncxj,jq->ncxq", pictures, matrix, precision=highest)
    first = first.reshape(amount, CH, SUB, 2, SUB)
    second = jnp.einsum(
        "ncxpl,pxqk->ncqkl", first, matrix.reshape(2, SUB, 2, SUB), precision=highest
    )
    return (second * (1.0 / (ROWS * SUB))).reshape(amount, 2 * CH, SUB, SUB)


def place_dense(spectra, row_start, col_start, height, width):
    offsets = jnp.arange(SUB, dtype=jnp.int32)
    row_cells = jnp.arange(height, dtype=jnp.int32)
    col_cells = jnp.arange(width, dtype=jnp.int32)
    row_map = (
        row_cells[None, :, None] == row_start[:, None, None] + offsets[None, None, :]
    ).astype(jnp.float32)
    col_map = (
        col_start[:, None, None] + offsets[None, :, None] == col_cells[None, None, :]
    ).astype(jnp.float32)
    widened = jnp.einsum("spkl,slj->spkj", spectra, col_map, precision=highest)
    return jnp.einsum("sik,spkj->pij", row_map, widened, precision=highest)


def merge_pictures(selector, pictures):
    slots = pictures.shape[0]
    merged = jnp.dot(selector, pictures.reshape(slots, CH * SUB * 2 * SUB), precision=highest)
    return merged.reshape(SUBW, CH, SUB, 2 * SUB)


def local(block_coords, block_visibilities, subgrid_of_block, live_blocks, corners, channel_scale):
    workers = lax.axis_size("work")
    tiles = lax.axis_size("tile")
    worker = lax.axis_index("work")
    blocks = block_coords.shape[0]
    capacity = 4 * blocks // workers
    position = jnp.arange(blocks, dtype=jnp.int32)
    owner = jnp.where(position < live_blocks[0], subgrid_of_block // SUBW, workers)
    earlier = (owner[:, None] == owner[None, :]) & (position[None, :] < position[:, None])
    before = jnp.sum(earlier.astype(jnp.int32), axis=1)
    target = owner * capacity + before
    payload = jnp.concatenate([block_coords, block_visibilities], axis=1)
    slot_ids = jnp.arange(workers * capacity, dtype=jnp.int32)
    matches = slot_ids[:, None] == target[None, :]
    dispatch = matches.astype(jnp.float32)
    send_data = jnp.dot(
        dispatch, payload.reshape(blocks, payload.shape[1] * payload.shape[2]), precision=highest
    )
    send_labels = jnp.sum(jnp.where(matches, subgrid_of_block[None, :] + 1, 0), axis=1) - 1
    send_data = send_data.reshape(workers, capacity, payload.shape[1], payload.shape[2])
    send_labels = send_labels.reshape(workers, capacity)
    payloads = lax.all_to_all(send_data, "work", split_axis=0, concat_axis=0, tiled=True)
    labels = lax.all_to_all(send_labels, "work", split_axis=0, concat_axis=0, tiled=True)
    leading = payloads.shape[0]
    items = payloads.shape[1]
    flat = payloads.reshape(leading * items, payloads.shape[2], payloads.shape[3])
    pictures = block_pictures(flat[:, 0:3, :], flat[:, 3:, :], channel_scale)
    pictures, got_labels = (pictures.reshape(leading, items, CH, SUB, 2 * SUB), labels)
    slots = pictures.shape[0] * pictures.shape[1]
    pictures = pictures.reshape(slots, CH, SUB, 2 * SUB)
    local_labels = got_labels.reshape(slots) - worker * SUBW
    local_corners = lax.dynamic_slice_in_dim(corners, worker * SUBW, SUBW, 0)
    col_corners = local_corners[:, 1] - worker * GCW
    subgrid_ids = jnp.arange(SUBW, dtype=jnp.int32)
    height = TR * tiles
    selector = (subgrid_ids[:, None] == local_labels[None, :]).astype(jnp.float32)
    merged = merge_pictures(selector, pictures)
    spectra = to_spectrum(merged)
    strip = place_dense(spectra, local_corners[:, 0], col_corners, height, GCW)
    uv_grid = sent_and_summed(strip, "tile", 1)
    return uv_grid


def solution(mesh):
    return jax.shard_map(
        local,
        mesh=mesh,
        in_specs=(
            P(("work", "tile"), None, None),
            P(("work", "tile"), None, None),
            P(("work", "tile")),
            P(("work", "tile")),
            P(),
            P(),
        ),
        out_specs=P(None, "tile", "work"),
        check_vma=False,
    )
```

profile of v0, /device:TPU:2, one launch (start us, length us, event | category | flops | bytes accessed | tf_op | source)
XLA Modules:
  0.0 327.8 jit_solution(4615039110082349473)
XLA Ops:
  0.7 0.7 broadcast_add_fusion.1
  1.7 0.7 sub.60
  2.4 7.6 %all-to-all-start = ((s32[32,1,16]{2,1,0:T(1,128)}), s32[32,1,16]{2,1,0:T(1,128)S(1)}, u32[]{:S(2)}, u32[]{:S(2)}) async-start(s32[32,1,16]{2,1,0:T(1,128)} %bitcast.2), calls=%async_computation | async-start | bytes 32768 | tf_op jit(solution)/shard_map/all_to_all | solution.py:133
  10.0 1.1 copy.33
  11.1 1.1 copy.32
  12.2 2.2 fusion.59
  14.3 1.8 all-to-all-done
  16.1 5.6 %all-to-all-start.1 = ((f32[32,16,7,128]{3,1,2,0:T(8,128)}), f32[32,16,7,128]{3,1,2,0:T(8,128)S(1)}, u32[]{:S(2)}, u32[]{:S(2)}) async-start(f32[32,16,7,128]{3,1,2,0:T(8,128)} %fusion.59), calls=%async_computation.1 | async-start | bytes 3670016 | tf_op jit(solution)/shard_map/all_to_all | solution.py:132
  22.3 1.4 fusion.87
  23.9 22.9 %all-to-all-done.1 = f32[32,16,7,128]{3,1,2,0:T(8,128)S(1)} async-done(((f32[32,16,7,128]{3,1,2,0:T(8,128)}), f32[32,16,7,128]{3,1,2,0:T(8,128)S(1)}, u32[]{:S(2)}, u32[]{:S(2)}) %all-to-all-start.1) | async-done | bytes 1835040 | tf_op jit(solution)/shard_map/all_to_all | solution.py:132
  46.9 1.5 slice_bitcast_fusion.3
  48.4 133.7 %multiply_subtract_fusion.1 = (f32[512,32,128]{2,1,0:T(8,128)}, f32[512,32,128]{2,1,0:T(8,128)}, f32[512,32,128]{2,1,0:T(8,128)}, f32[512,32,128]{2,1,0:T(8,128)...) fusion(f32[512,128]{1,0:T(8,128)S(1)} %get-tuple-element.12, ...), kind=kLoop, calls=%fused_computation.42 | loop fusion | flops 58720256 | bytes 86507776 | tf_op jit(solution)/shard_map/sub | solution.py:56
  182.1 35.7 %fusion.41 = f32[512,1,32,64]{3,2,0,1:T(8,128)} fusion(f32[512,32,128]{2,1,0:T(8,128)} %get-tuple-element.26, f32[512,32,128]{2,1,0:T(8,128)} %get-tuple-element.25, f32[512,32,128]{2,1,0:T(8,128)} %get-tuple-element.27, f32[512,32,128]{2,1,0:T(8,128)} %get-tuple-element.16, f32[512,32,128]{2,1,0:T(8,128)} %get-tuple-element.15), kind=kOutput, calls=%fused_computation.46 | convolution fusion | flops 3250585600 | bytes 46137344 | tf_op jit(solution)/shard_map/nxk,njk->nxj/dot_general | solution.py:64
  217.9 35.7 %fusion.36 = f32[512,1,32,64]{3,2,0,1:T(8,128)} fusion(f32[512,32,128]{2,1,0:T(8,128)} %get-tuple-element.34, f32[512,32,128]{2,1,0:T(8,128)} %get-tuple-element.35, f32[512,32,128]{2,1,0:T(8,128)} %get-tuple-element.33, f32[512,32,128]{2,1,0:T(8,128)} %get-tuple-element.36, f32[512,32,128]{2,1,0:T(8,128)} %get-tuple-element.37), kind=kOutput, calls=%fused_computation.45 | convolution fusion | flops 3250585600 | bytes 46137344 | tf_op jit(solution)/shard_map/nxk,njk->nxj/dot_general | solution.py:64
  253.6 11.8 %pad_maximum_fusion = f32[512,2,32,64]{3,2,0,1:T(8,128)} fusion(f32[512,1,32,64]{3,2,0,1:T(8,128)} %fusion.36, f32[512,1,32,64]{3,2,0,1:T(8,128)} %fusion.41), kind=kLoop, calls=%fused_computation.22 | loop fusion | flops 2097152 | bytes 16777216 | tf_op jit(solution)/shard_map/stack | solution.py:65
  265.3 12.7 %copy.35 = f32[512,2,32,64]{0,3,2,1:T(8,128)} copy(f32[512,2,32,64]{3,2,0,1:T(8,128)} %pad_maximum_fusion) | data formatting | bytes 16777216 | tf_op jit(solution)/shard_map/stack | solution.py:65
  278.1 7.5 %fusion.26 = f32[16,2,32,64]{3,0,2,1:T(8,128)S(1)} fusion(f32[512,2,32,64]{0,3,2,1:T(8,128)} %copy.35, s32[512]{0:T(512)S(1)} %sub.63), kind=kOutput, calls=%fused_computation.31 | convolution fusion | flops 402661376 | bytes 8652800 | tf_op jit(solution)/shard_map/dot_general | solution.py:107
  285.6 0.7 fusion.56
  286.3 0.6 reshape.146
  286.9 1.1 fusion.49
  288.0 0.7 fusion.51
  288.7 1.2 convolution_bitcast_fusion
  290.3 36.7 %all_to_all.16 = f32[8,4,64,128]{3,2,1,0:T(8,128)S(1)} all-to-all(f32[8,4,64,128]{3,2,1,0:T(8,128)S(1)} %copy.42), channel_id=1, replica_groups=mesh['work'=32,'tile'=8] {'tile'}, dimensions={0} | all-to-all | bytes 2097152 | tf_op jit(solution)/shard_map/all_to_all | solution.py:28
  327.1 0.7 reduce_sum.29
  (25 shorter events, 1.7 us)
Async XLA Ops:
  0.0 22.2 %copy-start = (s32[512,2]{0,1:T(2,128)S(1)}, s32[512,2]{0,1:T(2,128)}, u32[]{:S(2)}) copy-start(s32[512,2]{0,1:T(2,128)} %param.10) | copy-start | bytes 12292
  2.4 13.7 %all-to-all-start = ((s32[32,1,16]{2,1,0:T(1,128)}), s32[32,1,16]{2,1,0:T(1,128)S(1)}, u32[]{:S(2)}, u32[]{:S(2)}) async-start(s32[32,1,16]{2,1,0:T(1,128)} %bitcast.2), calls=%async_computation | async-start | bytes 32768 | tf_op jit(solution)/shard_map/all_to_all | solution.py:133
  16.1 30.7 %all-to-all-start.1 = ((f32[32,16,7,128]{3,1,2,0:T(8,128)}), f32[32,16,7,128]{3,1,2,0:T(8,128)S(1)}, u32[]{:S(2)}, u32[]{:S(2)}) async-start(f32[32,16,7,128]{3,1,2,0:T(8,128)} %fusion.59), calls=%async_computation.1 | async-start | bytes 3670016 | tf_op jit(solution)/shard_map/all_to_all | solution.py:132
  285.6 42.2 %copy-start.1 = (s32[512,2]{0,1:T(2,128)S(1)}, s32[512,2]{0,1:T(2,128)}, u32[]{:S(2)}) copy-start(s32[512,2]{0,1:T(2,128)} %param.10) | copy-start | bytes 12292
where the time goes:
time: 329 us; the launch traced here: 328 us
  other arithmetic  149 us (45%)
  matrix products  84.7 us (26%)
  blocking collectives  36.7 us (11%)
  waiting for transfers between devices  24.6 us (7%)
  local copies, waits for them, and re-layouts  18.4 us (6%)
  starting transfers between devices  13.2 us (4%)
    sub x1, other arithmetic, block_pictures(): wave_real * cosine_first - wave_imag * sine_first  134 us
    dot_general x2, matrix products, block_pictures(): jnp.einsum('nxk,njk->nxj', left_side, right_side, precision=highest)  71.4 us
    all_to_all x1, blocking collectives, sent_and_summed(): lax.all_to_all(blocks, axis, split_axis=0, concat_axis=0, tiled=True)  36.7 us
    all_to_all x1, waiting for transfers between devices, local(): lax.all_to_all(send_data, 'work', split_axis=0, concat_axis=0, tiled=True)  22.9 us
    another operation x1, local copies, waits for them, and re-layouts, block_pictures(): return jnp.stack(layers, axis=1)  12.7 us
    another operation x1, other arithmetic, block_pictures(): return jnp.stack(layers, axis=1)  11.8 us
    all_to_all x1, starting transfers between devices, local(): lax.all_to_all(send_labels, 'work', split_axis=0, concat_axis=0, tiled=True)  7.62 us
    dot_general x1, matrix products, merge_pictures(): jnp.dot(selector, pictures.reshape(slots, CH * SUB * 2 * SUB), precision=...  7.5 us
  transfers between devices with their start and end apart: 2, of which 2 were waited for; matrix products, arithmetic and copies ran while one was open for 2% of the time, Pallas kernels for 0%

commit v1 on v0

v1 whole, which is shorter than its diff:
```python
import functools
import math

import jax
import jax.numpy as jnp
import numpy as np
from jax import lax
from jax.experimental import pallas as pl
from jax.experimental.pallas import tpu as pltpu
from jax.sharding import PartitionSpec as P

CH = 2
SUB = 32
HALF = SUB // 2
ROWS = 128
TR = 64
GCW = 128
SUBW = 16
FIELDS = 3 + 2 * CH
TERMS = 4 * HALF

NT = (((1,), (1,)), ((), ()))


def pack_kernel(label_ref, live_ref, coords_ref, waves_ref, out_ref, count_ref):
    workers, capacity = out_ref.shape[0], SUBW
    out_ref[...] = jnp.zeros_like(out_ref)

    def clear(worker, carry):
        count_ref[worker] = 0
        return carry

    lax.fori_loop(0, workers, clear, 0)
    lane = lax.broadcasted_iota(jnp.int32, (1, ROWS), 1)

    def move(block, carry):
        label = label_ref[block]
        worker = label // SUBW
        slot = count_ref[worker]
        count_ref[worker] = slot + 1
        for field in range(3):
            out_ref[worker, pl.ds(field * capacity + slot, 1), :] = coords_ref[
                field, pl.ds(block, 1), :
            ]
        for field in range(2 * CH):
            out_ref[worker, pl.ds((3 + field) * capacity + slot, 1), :] = waves_ref[
                block, pl.ds(field, 1), :
            ]
        row = pl.ds(FIELDS * capacity, 1)
        inside = (label - worker * SUBW).astype(jnp.float32)
        out_ref[worker, row, :] = jnp.where(lane == slot, inside, out_ref[worker, row, :])
        return carry

    lax.fori_loop(0, live_ref[0], move, 0)


def pack(labels, live, coords, waves, workers):
    smem = pl.BlockSpec(memory_space=pltpu.SMEM)
    vmem = pl.BlockSpec(memory_space=pltpu.VMEM)
    return pl.pallas_call(
        pack_kernel,
        name="pack",
        out_shape=jax.ShapeDtypeStruct((workers, FIELDS * SUBW + 8, ROWS), jnp.float32),
        in_specs=[smem, smem, vmem, vmem],
        out_specs=vmem,
        scratch_shapes=[pltpu.SMEM((workers,), jnp.int32)],
    )(labels, live, coords, waves)


def sin_cos(theta, sin_terms, cos_terms):
    square = theta * theta
    sine = jnp.full_like(theta, (-1.0) ** (sin_terms - 1) / math.factorial(2 * sin_terms - 1))
    for n in range(sin_terms - 2, -1, -1):
        sine = sine * square + (-1.0) ** n / math.factorial(2 * n + 1)
    cosine = jnp.full_like(theta, (-1.0) ** (cos_terms - 1) / math.factorial(2 * cos_terms - 2))
    for n in range(cos_terms - 2, -1, -1):
        cosine = cosine * square + (-1.0) ** n / math.factorial(2 * n)
    return cosine, sine * theta


def times(a, b):
    return a[0] * b[0] - a[1] * b[1], a[0] * b[1] + a[1] * b[0]


def split(value):
    high = value.astype(jnp.bfloat16)
    low = (value - high.astype(jnp.float32)).astype(jnp.bfloat16)
    return high, low


def picture_kernel(
    label_ref, scale_ref, corner_ref, x_ref, mix_ref, spread_ref, out_ref, sums, left, right, strip
):
    step = pl.program_id(0)
    capacity = SUBW

    @pl.when(step == 0)
    def _():
        sums[...] = jnp.zeros_like(sums)
        strip[...] = jnp.zeros_like(strip)

    def field(index):
        return x_ref[0, index * capacity : (index + 1) * capacity, :]

    u, v, w = field(0), field(1), field(2)
    for ch in range(CH):
        factor = scale_ref[ch]
        first = u * factor * (2.0 * math.pi / (2 * SUB))
        second = v * factor * (2.0 * math.pi / (2 * SUB))
        depth = w * factor * (2.0 * math.pi / (SUB * SUB))
        along_u = sin_cos(first - depth * 0.5, 5, 6)
        along_v = sin_cos(second - depth * 0.5, 5, 6)
        turn = sin_cos(depth * 2.0, 4, 4)
        start = sin_cos(depth - (first + second), 7, 8)
        step_u = times(along_u, along_u)
        step_v = times(along_v, along_v)
        wave = times((field(3 + 2 * ch), field(4 + 2 * ch)), start)
        chirp = turn
        grown = turn
        for k in range(HALF):
            if k > 1:
                grown = times(grown, turn)
                chirp = times(chirp, grown)
            if k > 0:
                along_u = times(along_u, step_u)
                along_v = times(along_v, step_v)
            scaled = times(wave, chirp) if k > 0 else wave

            def put(ref, kind, value):
                ref[ch, pl.ds((kind * HALF + k) * capacity, capacity), :] = value

            put(left, 0, scaled[0] * along_u[0])
            put(left, 1, scaled[1] * along_u[0])
            put(left, 2, scaled[0] * along_u[1])
            put(left, 3, scaled[1] * along_u[1])
            if k > 0:
                put(right, 0, chirp[0] * along_v[0])
                put(right, 1, chirp[1] * along_v[0])
                put(right, 2, chirp[0] * along_v[1])
                put(right, 3, chirp[1] * along_v[1])
            else:
                put(right, 0, along_v[0])
                put(right, 1, jnp.zeros_like(u))
                put(right, 2, along_v[1])
                put(right, 3, jnp.zeros_like(u))
    for slot in range(capacity):
        label = label_ref[step * capacity + slot]
        for ch in range(CH):
            left_high, left_low = split(left[ch, pl.ds(slot, TERMS, stride=capacity), :])
            right_high, right_low = split(right[ch, pl.ds(slot, TERMS, stride=capacity), :])
            sums[label, ch] += lax.dot_general(
                jnp.concatenate([left_high, left_high, left_low], axis=1),
                jnp.concatenate([right_high, right_low, right_high], axis=1),
                NT,
                preferred_element_type=jnp.float32,
            )

    @pl.when(step == pl.num_programs(0) - 1)
    def _():
        for subgrid in range(SUBW):
            shift = corner_ref[subgrid, 1]
            spread_real = pltpu.roll(spread_ref[0], shift, 1)
            spread_imag = pltpu.roll(spread_ref[1], shift, 1)
            spread = jnp.concatenate([spread_real, spread_imag], axis=1)
            for ch in range(CH):
                wide = jnp.dot(
                    sums[subgrid, ch],
                    spread,
                    precision=lax.Precision.HIGHEST,
                    preferred_element_type=jnp.float32,
                )
                spectrum = jnp.dot(
                    mix_ref[...],
                    jnp.concatenate([wide[:, :GCW], wide[:, GCW:]], axis=0),
                    precision=lax.Precision.HIGHEST,
                    preferred_element_type=jnp.float32,
                )
                rows = pl.ds(corner_ref[subgrid, 0], SUB)
                strip[2 * ch, rows, :] += spectrum[:SUB]
                strip[2 * ch + 1, rows, :] += spectrum[SUB:]
        for tile in range(out_ref.shape[0]):
            for plane in range(2 * CH):
                out_ref[tile, plane] = strip[plane, tile * TR : (tile + 1) * TR, :]


def transform_tables():
    k = np.arange(SUB)[:, None]
    h = np.arange(HALF)[None, :]

    def tapered(x):
        return np.sin(np.pi * (x + 0.5) / SUB) ** 2 * np.exp(-2j * np.pi * k * x / SUB)

    upper, lower = tapered(HALF + h), tapered(HALF - 1 - h)
    even, odd = upper + lower, upper - lower
    table = np.concatenate([even, 1j * even, 1j * odd, -odd], axis=1)
    real, imag = table.real, table.imag
    mix = np.concatenate(
        [np.concatenate([real, -imag], axis=1), np.concatenate([imag, real], axis=1)], axis=0
    ) / (ROWS * SUB)
    spread = np.zeros((2, TERMS, GCW))
    spread[0, :, :SUB] = real.T
    spread[1, :, :SUB] = imag.T
    return mix.astype(np.float32), spread.astype(np.float32)


def picture_strip(labels, scale, corners, arrived, tiles):
    sources = arrived.shape[0]
    mix, spread = transform_tables()
    return pl.pallas_call(
        picture_kernel,
        name="pictures",
        out_shape=jax.ShapeDtypeStruct((tiles, 2 * CH, TR, GCW), jnp.float32),
        grid_spec=pltpu.PrefetchScalarGridSpec(
            num_scalar_prefetch=3,
            grid=(sources,),
            in_specs=[
                pl.BlockSpec((1, arrived.shape[1], ROWS), lambda i, *_: (i, 0, 0)),
                pl.BlockSpec(mix.shape, lambda i, *_: (0, 0)),
                pl.BlockSpec(spread.shape, lambda i, *_: (0, 0, 0)),
            ],
            out_specs=pl.BlockSpec((tiles, 2 * CH, TR, GCW), lambda i, *_: (0, 0, 0, 0)),
            scratch_shapes=[
                pltpu.VMEM((SUBW, CH, TERMS, TERMS), jnp.float32),
                pltpu.VMEM((CH, TERMS * SUBW, ROWS), jnp.float32),
                pltpu.VMEM((CH, TERMS * SUBW, ROWS), jnp.float32),
                pltpu.VMEM((2 * CH, TR * tiles, GCW), jnp.float32),
            ],
        ),
        compiler_params=pltpu.CompilerParams(dimension_semantics=("arbitrary",)),
    )(labels, scale, corners, arrived, jnp.asarray(mix), jnp.asarray(spread))


def local(block_coords, block_visibilities, subgrid_of_block, live_blocks, corners, channel_scale):
    workers = lax.axis_size("work")
    tiles = lax.axis_size("tile")
    worker = lax.axis_index("work")
    coords = jnp.swapaxes(block_coords, 0, 1)
    packed = pack(subgrid_of_block, live_blocks, coords, block_visibilities, workers)
    arrived = lax.all_to_all(packed, "work", split_axis=0, concat_axis=0, tiled=True)
    labels = arrived[:, FIELDS * SUBW, :SUBW].astype(jnp.int32).reshape(workers * SUBW)
    local_corners = lax.dynamic_slice_in_dim(corners, worker * SUBW, SUBW, 0)
    local_corners = local_corners - jnp.stack([0 * worker, worker * GCW])[None, :]
    strip = picture_strip(labels, channel_scale, local_corners, arrived, tiles)
    gathered = lax.all_to_all(strip, "tile", split_axis=0, concat_axis=0, tiled=True)
    return gathered.sum(axis=0)


def solution(mesh):
    return jax.shard_map(
        local,
        mesh=mesh,
        in_specs=(
            P(("work", "tile"), None, None),
            P(("work", "tile"), None, None),
            P(("work", "tile")),
            P(("work", "tile")),
            P(),
            P(),
        ),
        out_specs=P(None, "tile", "work"),
        check_vma=False,
    )
```

time: 329 us -> 134 us (0.41)
  other arithmetic: 149 us -> 1.45 us
  matrix products: 84.7 us -> 0 us
  Pallas kernels: 0 us -> 60.3 us
  local copies, waits for them, and re-layouts: 18.4 us -> 1.39 us
  starting transfers between devices: 13.2 us -> 7.37 us
    sub x3 -> x1, other arithmetic: 134 us -> 0.6 us  [local(): local_corners - jnp.stack([0 * worker, worker * GCW])[None, :]]
    dot_general x8 -> x0, matrix products: 84.7 us -> none  [the longest x2 71.4 us: block_pictures(): jnp.einsum('nxk,njk->nxj', left_side, right_side, precision=highest)]
    pallas_call x0 -> x2, Pallas kernels: none -> 60.3 us  [the longest x1 55.2 us: picture_strip(): pl.pallas_call(picture_kernel, name='pictures', out_shape=jax.ShapeDtypeS...]
    another operation x1 -> x0, local copies, waits for them, and re-layouts: 12.7 us -> none  [block_pictures(): return jnp.stack(layers, axis=1)]
    another operation x1, other arithmetic: 11.8 us -> 0.07 us  [local(): jnp.stack([0 * worker, worker * GCW])[None, :]]
    all_to_all x2 -> x1, starting transfers between devices: 13.2 us -> 7.37 us  [local(): lax.all_to_all(packed, 'work', split_axis=0, concat_axis=0, tiled=True)]
    all_to_all x2 -> x1, waiting for transfers between devices: 24.6 us -> 25.6 us  [local(): lax.all_to_all(packed, 'work', split_axis=0, concat_axis=0, tiled=True)]
  transfers between devices with their start and end apart: 2 -> 1, of which waited for: 2 -> 1; matrix products, arithmetic and copies ran while one was open for 2% -> 1% of each run, Pallas kernels for 0% -> 0%
where the time goes in v1:
time: 134 us
  Pallas kernels  60.3 us (45%)
  blocking collectives  36.7 us (27%)
  waiting for transfers between devices  25.6 us (19%)
  starting transfers between devices  7.37 us (6%)
  other arithmetic  1.45 us (1%)
  local copies, waits for them, and re-layouts  1.39 us (1%)
    pallas_call x1, Pallas kernels, picture_strip(): pl.pallas_call(picture_kernel, name='pictures', out_shape=jax.ShapeDtypeS...  55.2 us
    all_to_all x1, blocking collectives, local(): lax.all_to_all(strip, 'tile', split_axis=0, concat_axis=0, tiled=True)  36.7 us
    all_to_all x1, waiting for transfers between devices, local(): lax.all_to_all(packed, 'work', split_axis=0, concat_axis=0, tiled=True)  25.6 us
    all_to_all x1, starting transfers between devices, local(): lax.all_to_all(packed, 'work', split_axis=0, concat_axis=0, tiled=True)  7.37 us
    pallas_call x1, Pallas kernels, pack(): pl.pallas_call(pack_kernel, name='pack', out_shape=jax.ShapeDtypeStruct((...  5.08 us
  transfers between devices with their start and end apart: 1, of which 1 were waited for; matrix products, arithmetic and copies ran while one was open for 1% of the time, Pallas kernels for 0%

profile of v1, /device:TPU:2, one launch (start us, length us, event | category | flops | bytes accessed | tf_op | source)
XLA Modules:
  0.0 133.5 jit_solution(8699033293064428918)
XLA Ops:
  0.0 0.0 copy-start
  0.7 5.1 %pack.1 = f32[32,120,128]{2,1,0:T(8,128)} custom-call(s32[128]{0:T(128)} %label_ref.1, s32[1]{0:T(128)S(6)} %copy.12.live_ref, f32[3,128,128]{2,1,0:T(8,128)} %bitcast.2, f32[128,4,128]{2,1,0:T(4,128)} %waves_ref.1), custom_call_target="tpu_custom_call" | custom-call | tf_op jit(solution)/shard_map/pack/pallas_call | solution.py:60
  5.8 7.4 %all-to-all-start = ((f32[32,120,128]{2,1,0:T(8,128)}), f32[32,120,128]{2,1,0:T(8,128)S(1)}, u32[]{:S(2)}, u32[]{:S(2)}) async-start(f32[32,120,128]{2,1,0:T(8,128)} %pack.1), calls=%async_computation | async-start | bytes 3932160 | tf_op jit(solution)/shard_map/all_to_all | solution.py:239
  13.1 0.0 copy-done
  13.1 0.1 constant_dynamic-slice_fusion
  13.2 0.1 copy.11
  13.3 0.1 pad_add_fusion
  13.4 0.6 broadcast_subtract_fusion.corner_ref
  14.0 25.6 %all-to-all-done.x_ref = f32[32,120,128]{2,1,0:T(8,128)S(1)} async-done(((f32[32,120,128]{2,1,0:T(8,128)}), f32[32,120,128]{2,1,0:T(8,128)S(1)}, u32[]{:S(2)}, u32[]{:S(2)}) %all-to-all-start) | async-done | bytes 1966112 | tf_op jit(solution)/shard_map/all_to_all | solution.py:239
  39.6 0.0 copy-start.1
  39.6 0.1 fusion
  39.7 0.8 convert_element_type.8.label_ref
  40.4 0.5 copy-done.1
  40.9 55.2 %pictures.1 = f32[8,4,64,128]{3,2,1,0:T(8,128)} custom-call(s32[512]{0:T(512)} %convert_element_type.8.label_ref, f32[2]{0:T(128)} %scale_ref.1, s32[16,2]{1,0:T(8,128)} %broadcast_subtract_fusion.corner_ref, f32[32,120,128]{2,1,0:T(8,128)} %copy-done.1, f32[64,128]{1,0:T(8,128)} %constant.22.clone.mix_ref, f32[2,64,128]{2,1,0:T(8,128)} %constant.23.clone.spread_ref), custom_call_target="tpu_custom_call" | custom-call | tf_op jit(solution)/shard_map/pictures/pallas_call | solution.py:209
  96.1 36.7 %all_to_all.10 = f32[8,4,64,128]{3,2,1,0:T(8,128)S(1)} all-to-all(f32[8,4,64,128]{3,2,1,0:T(8,128)} %pictures.1), channel_id=1, replica_groups=mesh['work'=32,'tile'=8] {'tile'}, dimensions={0} | all-to-all | bytes 2097152 | tf_op jit(solution)/shard_map/all_to_all | solution.py:244
  132.8 0.7 reduce_sum.9
Async XLA Ops:
  0.0 13.1 %copy-start = (s32[512,2]{0,1:T(2,128)S(1)}, s32[512,2]{0,1:T(2,128)}, u32[]{:S(2)}) copy-start(s32[512,2]{0,1:T(2,128)} %param.12) | copy-start | bytes 12292
  5.8 33.9 %all-to-all-start = ((f32[32,120,128]{2,1,0:T(8,128)}), f32[32,120,128]{2,1,0:T(8,128)S(1)}, u32[]{:S(2)}, u32[]{:S(2)}) async-start(f32[32,120,128]{2,1,0:T(8,128)} %pack.1), calls=%async_computation | async-start | bytes 3932160 | tf_op jit(solution)/shard_map/all_to_all | solution.py:239
  39.6 1.3 copy-start.1

commit v2 on v1

v2 whole, which is shorter than its diff:
```python
import functools
import math

import jax
import jax.numpy as jnp
import numpy as np
from jax import lax
from jax.experimental import pallas as pl
from jax.experimental.pallas import tpu as pltpu
from jax.sharding import PartitionSpec as P

CH = 2
SUB = 32
HALF = SUB // 2
ROWS = 128
TR = 64
GCW = 128
SUBW = 16
FIELDS = 3 + 2 * CH
TERMS = 4 * HALF
GROUP = 8
UNROLL = 8

def pack_kernel(label_ref, live_ref, coords_ref, waves_ref, out_ref, count_ref):
    workers, capacity = out_ref.shape[0], SUBW
    out_ref[...] = jnp.zeros_like(out_ref)

    def clear(worker, carry):
        count_ref[worker] = 0
        return carry

    lax.fori_loop(0, workers, clear, 0)
    lane = lax.broadcasted_iota(jnp.int32, (1, ROWS), 1)

    live = live_ref[0]

    def move(group, carry):
        for offset in range(UNROLL):
            block = group * UNROLL + offset
            label = label_ref[block]
            worker = label // SUBW
            slot = count_ref[worker]
            count_ref[worker] = slot + 1
            kept = jnp.where(block < live, 1.0, 0.0)
            for field in range(3):
                out_ref[worker, pl.ds(field * capacity + slot, 1), :] = coords_ref[
                    field, pl.ds(block, 1), :
                ]
            for field in range(2 * CH):
                out_ref[worker, pl.ds((3 + field) * capacity + slot, 1), :] = (
                    waves_ref[block, pl.ds(field, 1), :] * kept
                )
            row = pl.ds(FIELDS * capacity, 1)
            inside = (label - worker * SUBW).astype(jnp.float32)
            out_ref[worker, row, :] = jnp.where(lane == slot, inside, out_ref[worker, row, :])
        return carry

    lax.fori_loop(0, label_ref.shape[0] // UNROLL, move, 0)


def pack(labels, live, coords, waves, workers):
    smem = pl.BlockSpec(memory_space=pltpu.SMEM)
    vmem = pl.BlockSpec(memory_space=pltpu.VMEM)
    return pl.pallas_call(
        pack_kernel,
        name="pack",
        out_shape=jax.ShapeDtypeStruct((workers, FIELDS * SUBW + 8, ROWS), jnp.float32),
        in_specs=[smem, smem, vmem, vmem],
        out_specs=vmem,
        scratch_shapes=[pltpu.SMEM((workers,), jnp.int32)],
    )(labels, live, coords, waves)


def series(square, first, count):
    terms = [(-1.0) ** n / math.factorial(2 * n + first) for n in range(count)]
    total = square * terms[-1] + terms[-2]
    for term in terms[-3::-1]:
        total = total * square + term
    return total


def sin_cos(theta, sin_terms, cos_terms):
    square = theta * theta
    return series(square, 0, cos_terms), series(square, 1, sin_terms) * theta


def times(a, b):
    return a[0] * b[0] - a[1] * b[1], a[0] * b[1] + a[1] * b[0]


def split(value):
    high = value.astype(jnp.bfloat16)
    low = (value - high.astype(jnp.float32)).astype(jnp.bfloat16)
    return high, low


def advance(current, previous, twice_sine):
    return (
        previous[0] - twice_sine * current[1],
        previous[1] + twice_sine * current[0],
    )


def factor_rows(fields, factor, put_left, put_right):
    u, v, w = fields[:3]
    first = u * (factor * (2.0 * math.pi / (2 * SUB)))
    second = v * (factor * (2.0 * math.pi / (2 * SUB)))
    depth = w * (factor * (math.pi / (SUB * SUB)))
    along_u = sin_cos(first - depth, 5, 5)
    along_v = sin_cos(second - depth, 5, 5)
    turn = sin_cos(depth * 4.0, 3, 3)
    twice_u = along_u[0] * along_u[1] * 4.0
    twice_v = along_v[0] * along_v[1] * 4.0
    twice_w = turn[1] * 2.0
    both = times(along_u, along_v)
    wave = times(fields[3:], (both[0], -both[1]))
    before_u = (along_u[0], -along_u[1])
    before_v = (along_v[0], -along_v[1])
    zero = jnp.zeros_like(u)
    chirp = before_grown = (jnp.ones_like(u), zero)
    grown = turn
    for k in range(HALF):
        if k > 0:
            if k > 1:
                grown, before_grown = advance(grown, before_grown, twice_w), grown
                chirp = times(chirp, grown)
            else:
                chirp = turn
            wave = times(wave, grown)
            along_u, before_u = advance(along_u, before_u, twice_u), along_u
            along_v, before_v = advance(along_v, before_v, twice_v), along_v
        put_left(0, k, wave[0] * along_u[0])
        put_left(1, k, wave[1] * along_u[0])
        put_left(2, k, wave[0] * along_u[1])
        put_left(3, k, wave[1] * along_u[1])
        put_right(0, k, chirp[0] * along_v[0] if k > 0 else along_v[0])
        put_right(1, k, chirp[1] * along_v[0] if k > 0 else zero)
        put_right(2, k, chirp[0] * along_v[1] if k > 0 else along_v[1])
        put_right(3, k, chirp[1] * along_v[1] if k > 0 else zero)


def product(left, right, contract):
    left_high, left_low = split(left)
    right_high, right_low = split(right)
    return lax.dot_general(
        jnp.concatenate([left_high, left_high, left_low], axis=1),
        jnp.concatenate([right_high, right_low, right_high], axis=contract),
        (((1,), (contract,)), ((), ())),
        preferred_element_type=jnp.float32,
    )


def picture_kernel(
    label_ref,
    scale_ref,
    corner_ref,
    tile_ref,
    x_ref,
    mix_ref,
    spread_ref,
    out_ref,
    left,
    right,
    strip,
    *sums,
):
    step = pl.program_id(0)
    capacity = SUBW
    tiles = out_ref.shape[0]

    @pl.when(step == 0)
    def _():
        for ch in range(CH):
            sums[ch][...] = jnp.zeros_like(sums[ch])
        strip[...] = jnp.zeros_like(strip)

    def factors(group, ch):
        def field(index):
            start = index * capacity + group * GROUP
            return x_ref[0, start : start + GROUP, :]

        def put(ref, kind, k, value):
            ref[ch, group, pl.ds((kind * HALF + k) * GROUP, GROUP), :] = value

        chosen = [field(index) for index in (0, 1, 2, 3 + 2 * ch, 4 + 2 * ch)]
        factor_rows(
            chosen, scale_ref[ch], functools.partial(put, left), functools.partial(put, right)
        )

    def gather(group, ch):
        for slot in range(GROUP):
            label = label_ref[step * capacity + group * GROUP + slot]
            rows = pl.ds(slot, TERMS, stride=GROUP)
            sums[ch][label] += product(left[ch, group, rows, :], right[ch, group, rows, :], 1)

    units = [(group, ch) for group in range(capacity // GROUP) for ch in range(CH)]
    factors(*units[0])
    for unit, following in zip(units[:-1], units[1:]):
        factors(*following)
        gather(*unit)
    gather(*units[-1])

    @pl.when(step == pl.num_programs(0) - 1)
    def _():
        for subgrid in range(SUBW):
            shift = corner_ref[subgrid, 1]
            spread_real = pltpu.roll(spread_ref[0], shift, 1)
            spread_imag = pltpu.roll(spread_ref[1], shift, 1)
            spread = jnp.concatenate([spread_real, spread_imag], axis=1)
            rows = pl.ds(corner_ref[subgrid, 0], SUB)
            for ch in range(CH):
                wide = product(sums[ch][subgrid], spread, 0)
                stacked = jnp.concatenate([wide[:, :GCW], wide[:, GCW:]], axis=0)
                spectrum = product(mix_ref[...], stacked, 0)
                strip[2 * ch, rows, :] += spectrum[:SUB]
                strip[2 * ch + 1, rows, :] += spectrum[SUB:]
        for distance in range(tiles):
            tile = lax.rem(tile_ref[0] + distance, tiles)
            for plane in range(2 * CH):
                out_ref[distance, plane] = strip[
                    plane, pl.ds(pl.multiple_of(tile * TR, TR), TR), :
                ]


def transform_tables():
    k = np.arange(SUB)[:, None]
    h = np.arange(HALF)[None, :]

    def tapered(x):
        return np.sin(np.pi * (x + 0.5) / SUB) ** 2 * np.exp(-2j * np.pi * k * x / SUB)

    upper, lower = tapered(HALF + h), tapered(HALF - 1 - h)
    even, odd = upper + lower, upper - lower
    table = np.concatenate([even, 1j * even, 1j * odd, -odd], axis=1)
    real, imag = table.real, table.imag
    mix = np.concatenate(
        [np.concatenate([real, -imag], axis=1), np.concatenate([imag, real], axis=1)], axis=0
    ) / (ROWS * SUB)
    spread = np.zeros((2, TERMS, GCW))
    spread[0, :, :SUB] = real.T
    spread[1, :, :SUB] = imag.T
    return mix.astype(np.float32), spread.astype(np.float32)


def picture_strip(labels, scale, corners, tile, arrived, tiles):
    sources = arrived.shape[0]
    mix, spread = transform_tables()
    return pl.pallas_call(
        picture_kernel,
        name="pictures",
        out_shape=jax.ShapeDtypeStruct((tiles, 2 * CH, TR, GCW), jnp.float32),
        grid_spec=pltpu.PrefetchScalarGridSpec(
            num_scalar_prefetch=4,
            grid=(sources,),
            in_specs=[
                pl.BlockSpec((1, arrived.shape[1], ROWS), lambda i, *_: (i, 0, 0)),
                pl.BlockSpec(mix.shape, lambda i, *_: (0, 0)),
                pl.BlockSpec(spread.shape, lambda i, *_: (0, 0, 0)),
            ],
            out_specs=pl.BlockSpec((tiles, 2 * CH, TR, GCW), lambda i, *_: (0, 0, 0, 0)),
            scratch_shapes=[
                pltpu.VMEM((CH, SUBW // GROUP, TERMS * GROUP, ROWS), jnp.float32),
                pltpu.VMEM((CH, SUBW // GROUP, TERMS * GROUP, ROWS), jnp.float32),
                pltpu.VMEM((2 * CH, TR * tiles, GCW), jnp.float32),
            ]
            + [pltpu.VMEM((SUBW, TERMS, TERMS), jnp.float32)] * CH,
        ),
        compiler_params=pltpu.CompilerParams(dimension_semantics=("arbitrary",)),
    )(labels, scale, corners, tile, arrived, jnp.asarray(mix), jnp.asarray(spread))


def summed_around(parts, axis):
    size = lax.axis_size(axis)
    far = size // 2
    up = [(i, (i + 1) % size) for i in range(size)]
    down = [(i, (i - 1) % size) for i in range(size)]
    rising = lax.ppermute(parts[far, :CH], axis, up)
    falling = lax.ppermute(parts[far, CH:], axis, down)
    for distance in range(far - 1, 0, -1):
        near, opposite = parts[distance], parts[size - distance]
        if distance == far - 1:
            rising = jnp.concatenate([near[:CH] + rising, near[CH:]])
            falling = jnp.concatenate([opposite[:CH], opposite[CH:] + falling])
        else:
            rising, falling = near + rising, opposite + falling
        rising = lax.ppermute(rising, axis, up)
        falling = lax.ppermute(falling, axis, down)
    return parts[0] + rising + falling


def local(block_coords, block_visibilities, subgrid_of_block, live_blocks, corners, channel_scale):
    workers = lax.axis_size("work")
    tiles = lax.axis_size("tile")
    worker = lax.axis_index("work")
    coords = jnp.swapaxes(block_coords, 0, 1)
    packed = pack(subgrid_of_block, live_blocks, coords, block_visibilities, workers)
    arrived = lax.all_to_all(packed, "work", split_axis=0, concat_axis=0, tiled=True)
    labels = arrived[:, FIELDS * SUBW, :SUBW].astype(jnp.int32).reshape(workers * SUBW)
    local_corners = lax.dynamic_slice_in_dim(corners, worker * SUBW, SUBW, 0)
    local_corners = local_corners - jnp.stack([0 * worker, worker * GCW])[None, :]
    tile = lax.axis_index("tile").astype(jnp.int32).reshape(1)
    parts = picture_strip(labels, channel_scale, local_corners, tile, arrived, tiles)
    return summed_around(parts, "tile")


def solution(mesh):
    return jax.shard_map(
        local,
        mesh=mesh,
        in_specs=(
            P(("work", "tile"), None, None),
            P(("work", "tile"), None, None),
            P(("work", "tile")),
            P(("work", "tile")),
            P(),
            P(),
        ),
        out_specs=P(None, "tile", "work"),
        check_vma=False,
    )
```

time: 134 us -> 121 us (0.903)
  the two profiles are of different devices: /device:TPU:2 before, /device:TPU:96 now
where the time goes in v2:
time: 121 us
  waiting for transfers between devices  49.9 us (41%)
  Pallas kernels  47.1 us (39%)
  starting transfers between devices  17.2 us (14%)
  other arithmetic  3.3 us (3%)
  local copies, waits for them, and re-layouts  2.46 us (2%)
    pallas_call x1, Pallas kernels, picture_strip(): pl.pallas_call(picture_kernel, name='pictures', out_shape=jax.ShapeDtypeS...  43.2 us
    all_to_all x1, waiting for transfers between devices, local(): lax.all_to_all(packed, 'work', split_axis=0, concat_axis=0, tiled=True)  27.6 us
    ppermute x3, waiting for transfers between devices, summed_around(): falling = lax.ppermute(falling, axis, down)  9.1 us
    ppermute x3, waiting for transfers between devices, summed_around(): rising = lax.ppermute(rising, axis, up)  7.67 us
    all_to_all x1, starting transfers between devices, local(): lax.all_to_all(packed, 'work', split_axis=0, concat_axis=0, tiled=True)  7.32 us
    ppermute x3, starting transfers between devices, summed_around(): rising = lax.ppermute(rising, axis, up)  4.6 us
    pallas_call x1, Pallas kernels, pack(): pl.pallas_call(pack_kernel, name='pack', out_shape=jax.ShapeDtypeStruct((...  3.91 us
    ppermute x1, waiting for transfers between devices, summed_around(): falling = lax.ppermute(parts[far, CH:], axis, down)  3.57 us
  transfers between devices with their start and end apart: 9, of which 7 were waited for; matrix products, arithmetic and copies ran while one was open for 1% of the time, Pallas kernels for 0%

profile of v2, /device:TPU:96, one launch (start us, length us, event | category | flops | bytes accessed | tf_op | source)
XLA Modules:
  0.0 120.7 jit_solution(9160441295473112191)
XLA Ops:
  0.7 3.9 %pack.1 = f32[32,120,128]{2,1,0:T(8,128)} custom-call(s32[128]{0:T(128)} %label_ref.1, s32[1]{0:T(128)S(6)} %copy.12.live_ref, f32[3,128,128]{2,1,0:T(8,128)} %bitcast.41, f32[128,4,128]{2,1,0:T(4,128)} %waves_ref.1), custom_call_target="tpu_custom_call" | custom-call | tf_op jit(solution)/shard_map/pack/pallas_call | solution.py:64
  4.6 7.3 %all-to-all-start = ((f32[32,120,128]{2,1,0:T(8,128)}), f32[32,120,128]{2,1,0:T(8,128)S(1)}, u32[]{:S(2)}, u32[]{:S(2)}) async-start(f32[32,120,128]{2,1,0:T(8,128)} %pack.1), calls=%async_computation | async-start | bytes 3932160 | tf_op jit(solution)/shard_map/all_to_all | solution.py:297
  12.0 0.1 copy.11
  12.2 0.6 broadcast_subtract_fusion.corner_ref
  12.8 27.6 %all-to-all-done.x_ref = f32[32,120,128]{2,1,0:T(8,128)S(1)} async-done(((f32[32,120,128]{2,1,0:T(8,128)}), f32[32,120,128]{2,1,0:T(8,128)S(1)}, u32[]{:S(2)}, u32[]{:S(2)}) %all-to-all-start) | async-done | bytes 1966112 | tf_op jit(solution)/shard_map/all_to_all | solution.py:297
  40.5 0.8 convert_element_type.8.label_ref
  41.3 0.4 copy-done.1
  41.7 43.2 %pictures.1 = f32[8,4,64,128]{3,2,1,0:T(8,128)} custom-call(s32[512]{0:T(512)} %convert_element_type.8.label_ref, f32[2]{0:T(128)} %scale_ref.1, s32[16,2]{1,0:T(8,128)} %broadcast_subtract_fusion.corner_ref, s32[1]{0:T(128)} %bitcast.2.tile_ref, f32[32,120,128]{2,1,0:T(8,128)} %copy-done.1, f32[64,128]{1,0:T(8,128)} %constant.23.clone.mix_ref, ...), custom_call_target="tpu_custom_call" | custom-call | tf_op jit(solution)/shard_map/pictures/pallas_call | solution.py:248
  84.9 1.0 slice_bitcast_fusion.9
  85.9 3.1 %collective-permute-start = (f32[2,64,128]{2,1,0:T(8,128)S(1)}, f32[2,64,128]{2,1,0:T(8,128)S(1)}, u32[]{:S(2)}, u32[]{:S(2)}) collective-permute-start(f32[2,64,128]{2,1,0:T(8,128)S(1)} %get-tuple-element.9), channel_id=1, source_target_pairs={{0,1},{1,2},{2,3},{3,4},{4,5},{5,6},{6,7},{7,0},{8,9},{9,10},{10,1... | collective-permute-start | bytes 196616 | tf_op jit(solution)/shard_map/ppermute | solution.py:277
  89.0 1.9 %collective-permute-done = f32[2,64,128]{2,1,0:T(8,128)S(1)} collective-permute-done((f32[2,64,128]{2,1,0:T(8,128)S(1)}, f32[2,64,128]{2,1,0:T(8,128)S(1)}, u32[]{:S(2)}, u32[]{:S(2)}) %collective-permute-start) | collective-permute-done | bytes 65568 | tf_op jit(solution)/shard_map/ppermute | solution.py:277
  90.9 3.6 %collective-permute-done.4 = f32[2,64,128]{2,1,0:T(8,128)S(1)} collective-permute-done((f32[2,64,128]{2,1,0:T(8,128)S(1)}, f32[2,64,128]{2,1,0:T(8,128)S(1)}, u32[]{:S(2)}, u32[]{:S(2)}) %collective-permute-start.4) | collective-permute-done | bytes 65568 | tf_op jit(solution)/shard_map/ppermute | solution.py:278
  94.5 0.9 fusion.7
  95.4 0.1 collective-permute-start.1
  95.5 2.1 %collective-permute-start.5 = (f32[4,64,128]{2,1,0:T(8,128)S(1)}, f32[4,64,128]{2,1,0:T(8,128)S(1)}, u32[]{:S(2)}, u32[]{:S(2)}) collective-permute-start(f32[4,64,128]{2,1,0:T(8,128)S(1)} %pad_maximum_fusion.1), channel_id=1, source_target_pairs={{0,7},{1,0},{2,1},{3,2},{4,3},{5,4},{6,5},{7,6},{8,15},{9,8},{10,9... | collective-permute-start | bytes 393224 | tf_op jit(solution)/shard_map/ppermute | solution.py:287
  97.6 2.9 %collective-permute-done.1 = f32[4,64,128]{2,1,0:T(8,128)S(1)} collective-permute-done((f32[4,64,128]{2,1,0:T(8,128)S(1)}, f32[4,64,128]{2,1,0:T(8,128)S(1)}, u32[]{:S(2)}, u32[]{:S(2)}) %collective-permute-start.1) | collective-permute-done | bytes 131104 | tf_op jit(solution)/shard_map/ppermute | solution.py:286
  100.4 0.9 fusion.2
  101.4 1.3 %collective-permute-start.2 = (f32[4,64,128]{2,1,0:T(8,128)S(1)}, f32[4,64,128]{2,1,0:T(8,128)S(1)}, u32[]{:S(2)}, u32[]{:S(2)}) collective-permute-start(f32[4,64,128]{2,1,0:T(8,128)S(1)} %fusion.2), channel_id=1, source_target_pairs={{0,1},{1,2},{2,3},{3,4},{4,5},{5,6},{6,7},{7,0},{8,9},{9,10},{10,1... | collective-permute-start | bytes 393224 | tf_op jit(solution)/shard_map/ppermute | solution.py:286
  102.7 4.8 %collective-permute-done.2 = f32[4,64,128]{2,1,0:T(8,128)S(1)} collective-permute-done((f32[4,64,128]{2,1,0:T(8,128)S(1)}, f32[4,64,128]{2,1,0:T(8,128)S(1)}, u32[]{:S(2)}, u32[]{:S(2)}) %collective-permute-start.2) | collective-permute-done | bytes 131104 | tf_op jit(solution)/shard_map/ppermute | solution.py:286
  107.5 0.1 collective-permute-start.6
  107.6 3.2 %collective-permute-start.3 = (f32[4,64,128]{2,1,0:T(8,128)S(1)}, f32[4,64,128]{2,1,0:T(8,128)S(1)}, u32[]{:S(2)}, u32[]{:S(2)}) collective-permute-start(f32[4,64,128]{2,1,0:T(8,128)S(1)} %get-tuple-element.5), channel_id=1, source_target_pairs={{0,1},{1,2},{2,3},{3,4},{4,5},{5,6},{6,7},{7,0},{8,9},{9,10},{10,1... | collective-permute-start | bytes 393224 | tf_op jit(solution)/shard_map/ppermute | solution.py:286
  110.8 2.9 %collective-permute-done.6 = f32[4,64,128]{2,1,0:T(8,128)S(1)} collective-permute-done((f32[4,64,128]{2,1,0:T(8,128)S(1)}, f32[4,64,128]{2,1,0:T(8,128)S(1)}, u32[]{:S(2)}, u32[]{:S(2)}) %collective-permute-start.6) | collective-permute-done | bytes 131104 | tf_op jit(solution)/shard_map/ppermute | solution.py:287
  113.9 6.2 %collective-permute-done.7 = f32[4,64,128]{2,1,0:T(8,128)S(1)} collective-permute-done((f32[4,64,128]{2,1,0:T(8,128)S(1)}, f32[4,64,128]{2,1,0:T(8,128)S(1)}, u32[]{:S(2)}, u32[]{:S(2)}) %collective-permute-start.7) | collective-permute-done | bytes 131104 | tf_op jit(solution)/shard_map/ppermute | solution.py:287
  120.0 0.7 fusion.5
  (16 shorter events, 0.4 us)
Async XLA Ops:
  0.0 11.9 %copy-start = (s32[512,2]{0,1:T(2,128)S(1)}, s32[512,2]{0,1:T(2,128)}, u32[]{:S(2)}) copy-start(s32[512,2]{0,1:T(2,128)} %param.12) | copy-start | bytes 12292
  4.6 35.8 %all-to-all-start = ((f32[32,120,128]{2,1,0:T(8,128)}), f32[32,120,128]{2,1,0:T(8,128)S(1)}, u32[]{:S(2)}, u32[]{:S(2)}) async-start(f32[32,120,128]{2,1,0:T(8,128)} %pack.1), calls=%async_computation | async-start | bytes 3932160 | tf_op jit(solution)/shard_map/all_to_all | solution.py:297
  40.4 1.3 %copy-start.1 = (f32[32,120,128]{2,1,0:T(8,128)}, f32[32,120,128]{2,1,0:T(8,128)S(1)}, u32[]{:S(2)}) copy-start(f32[32,120,128]{2,1,0:T(8,128)S(1)} %all-to-all-done.x_ref) | copy-start | bytes 5898244
  84.9 22.6 %copy-start.2 = (f32[8,4,64,128]{3,2,1,0:T(8,128)S(1)}, f32[8,4,64,128]{3,2,1,0:T(8,128)}, u32[]{:S(2)}) copy-start(f32[8,4,64,128]{3,2,1,0:T(8,128)} %pictures.1) | copy-start | bytes 3145732
  85.9 5.0 %collective-permute-start = (f32[2,64,128]{2,1,0:T(8,128)S(1)}, f32[2,64,128]{2,1,0:T(8,128)S(1)}, u32[]{:S(2)}, u32[]{:S(2)}) collective-permute-start(f32[2,64,128]{2,1,0:T(8,128)S(1)} %get-tuple-element.9), channel_id=1, source_target_pairs={{0,1},{1,2},{2,3},{3,4},{4,5},{5,6},{6,7},{7,0},{8,9},{9,10},{10,1... | collective-permute-start | bytes 196616 | tf_op jit(solution)/shard_map/ppermute | solution.py:277
  89.0 5.5 %collective-permute-start.4 = (f32[2,64,128]{2,1,0:T(8,128)S(1)}, f32[2,64,128]{2,1,0:T(8,128)S(1)}, u32[]{:S(2)}, u32[]{:S(2)}) collective-permute-start(f32[2,64,128]{2,1,0:T(8,128)S(1)} %get-tuple-element.10), channel_id=1, source_target_pairs={{0,7},{1,0},{2,1},{3,2},{4,3},{5,4},{6,5},{7,6},{8,15},{9,8},{10,9... | collective-permute-start | bytes 196616 | tf_op jit(solution)/shard_map/ppermute | solution.py:278
  95.4 5.0 %collective-permute-start.1 = (f32[4,64,128]{2,1,0:T(8,128)S(1)}, f32[4,64,128]{2,1,0:T(8,128)S(1)}, u32[]{:S(2)}, u32[]{:S(2)}) collective-permute-start(f32[4,64,128]{2,1,0:T(8,128)S(1)} %pad_maximum_fusion), channel_id=1, source_target_pairs={{0,1},{1,2},{2,3},{3,4},{4,5},{5,6},{6,7},{7,0},{8,9},{9,10},{10,1... | collective-permute-start | bytes 393224 | tf_op jit(solution)/shard_map/ppermute | solution.py:286
  95.5 7.2 %collective-permute-start.5 = (f32[4,64,128]{2,1,0:T(8,128)S(1)}, f32[4,64,128]{2,1,0:T(8,128)S(1)}, u32[]{:S(2)}, u32[]{:S(2)}) collective-permute-start(f32[4,64,128]{2,1,0:T(8,128)S(1)} %pad_maximum_fusion.1), channel_id=1, source_target_pairs={{0,7},{1,0},{2,1},{3,2},{4,3},{5,4},{6,5},{7,6},{8,15},{9,8},{10,9... | collective-permute-start | bytes 393224 | tf_op jit(solution)/shard_map/ppermute | solution.py:287
  101.4 6.1 %collective-permute-start.2 = (f32[4,64,128]{2,1,0:T(8,128)S(1)}, f32[4,64,128]{2,1,0:T(8,128)S(1)}, u32[]{:S(2)}, u32[]{:S(2)}) collective-permute-start(f32[4,64,128]{2,1,0:T(8,128)S(1)} %fusion.2), channel_id=1, source_target_pairs={{0,1},{1,2},{2,3},{3,4},{4,5},{5,6},{6,7},{7,0},{8,9},{9,10},{10,1... | collective-permute-start | bytes 393224 | tf_op jit(solution)/shard_map/ppermute | solution.py:286
  107.5 6.3 %collective-permute-start.6 = (f32[4,64,128]{2,1,0:T(8,128)S(1)}, f32[4,64,128]{2,1,0:T(8,128)S(1)}, u32[]{:S(2)}, u32[]{:S(2)}) collective-permute-start(f32[4,64,128]{2,1,0:T(8,128)S(1)} %get-tuple-element.6), channel_id=1, source_target_pairs={{0,7},{1,0},{2,1},{3,2},{4,3},{5,4},{6,5},{7,6},{8,15},{9,8},{10,9... | collective-permute-start | bytes 393224 | tf_op jit(solution)/shard_map/ppermute | solution.py:287
  107.6 6.3 %collective-permute-start.3 = (f32[4,64,128]{2,1,0:T(8,128)S(1)}, f32[4,64,128]{2,1,0:T(8,128)S(1)}, u32[]{:S(2)}, u32[]{:S(2)}) collective-permute-start(f32[4,64,128]{2,1,0:T(8,128)S(1)} %get-tuple-element.5), channel_id=1, source_target_pairs={{0,1},{1,2},{2,3},{3,4},{4,5},{5,6},{6,7},{7,0},{8,9},{9,10},{10,1... | collective-permute-start | bytes 393224 | tf_op jit(solution)/shard_map/ppermute | solution.py:286
  113.8 6.3 %collective-permute-start.7 = (f32[4,64,128]{2,1,0:T(8,128)S(1)}, f32[4,64,128]{2,1,0:T(8,128)S(1)}, u32[]{:S(2)}, u32[]{:S(2)}) collective-permute-start(f32[4,64,128]{2,1,0:T(8,128)S(1)} %fusion.1), channel_id=1, source_target_pairs={{0,7},{1,0},{2,1},{3,2},{4,3},{5,4},{6,5},{7,6},{8,15},{9,8},{10,9... | collective-permute-start | bytes 393224 | tf_op jit(solution)/shard_map/ppermute | solution.py:287

commit v3 on v2

v3 whole, which is shorter than its diff:
```python
import functools
import math

import jax
import jax.numpy as jnp
import numpy as np
from jax import lax
from jax.experimental import pallas as pl
from jax.experimental.pallas import tpu as pltpu
from jax.sharding import PartitionSpec as P

CH = 2
SUB = 32
HALF = SUB // 2
ROWS = 128
TR = 64
GCW = 128
SUBW = 16
FIELDS = 3 + 2 * CH
TERMS = 4 * HALF
GROUP = 8
SPAN = 2
UNROLL = 8

def pack_kernel(label_ref, live_ref, coords_ref, waves_ref, out_ref, count_ref):
    workers, capacity = out_ref.shape[0], SUBW
    out_ref[...] = jnp.zeros_like(out_ref)

    def clear(worker, carry):
        count_ref[worker] = 0
        return carry

    lax.fori_loop(0, workers, clear, 0)
    lane = lax.broadcasted_iota(jnp.int32, (1, ROWS), 1)

    live = live_ref[0]

    def move(group, carry):
        for offset in range(UNROLL):
            block = group * UNROLL + offset
            label = label_ref[block]
            worker = label // SUBW
            slot = count_ref[worker]
            count_ref[worker] = slot + 1
            kept = jnp.where(block < live, 1.0, 0.0)
            for field in range(3):
                out_ref[worker, pl.ds(field * capacity + slot, 1), :] = coords_ref[
                    field, pl.ds(block, 1), :
                ]
            for field in range(2 * CH):
                out_ref[worker, pl.ds((3 + field) * capacity + slot, 1), :] = (
                    waves_ref[block, pl.ds(field, 1), :] * kept
                )
            row = pl.ds(FIELDS * capacity, 1)
            inside = (label - worker * SUBW).astype(jnp.float32)
            out_ref[worker, row, :] = jnp.where(lane == slot, inside, out_ref[worker, row, :])
        return carry

    lax.fori_loop(0, label_ref.shape[0] // UNROLL, move, 0)


def pack(labels, live, coords, waves, workers):
    smem = pl.BlockSpec(memory_space=pltpu.SMEM)
    vmem = pl.BlockSpec(memory_space=pltpu.VMEM)
    return pl.pallas_call(
        pack_kernel,
        name="pack",
        out_shape=jax.ShapeDtypeStruct((workers, FIELDS * SUBW + 8, ROWS), jnp.float32),
        in_specs=[smem, smem, vmem, vmem],
        out_specs=vmem,
        scratch_shapes=[pltpu.SMEM((workers,), jnp.int32)],
        compiler_params=pltpu.CompilerParams(vmem_limit_bytes=8 << 20),
    )(labels, live, coords, waves)


def series(square, first, count):
    terms = [(-1.0) ** n / math.factorial(2 * n + first) for n in range(count)]
    total = square * terms[-1] + terms[-2]
    for term in terms[-3::-1]:
        total = total * square + term
    return total


def sin_cos(theta, sin_terms, cos_terms):
    square = theta * theta
    return series(square, 0, cos_terms), series(square, 1, sin_terms) * theta


def times(a, b):
    return a[0] * b[0] - a[1] * b[1], a[0] * b[1] + a[1] * b[0]


def split(value):
    high = value.astype(jnp.bfloat16)
    low = (value - high.astype(jnp.float32)).astype(jnp.bfloat16)
    return high, low


def advance(current, previous, twice_sine):
    return (
        previous[0] - twice_sine * current[1],
        previous[1] + twice_sine * current[0],
    )


def exchange(value):
    return pltpu.roll(value, GROUP // 2, 0)


def interleave(even, odd, low):
    return (
        jnp.where(low, even, exchange(odd)),
        jnp.where(low, exchange(even), odd),
    )


def interleave_pair(even, odd, low):
    real, imag = interleave(even[0], odd[0], low), interleave(even[1], odd[1], low)
    return (real[0], imag[0]), (real[1], imag[1])


def factor_rows(fields, factor, low, put_left, put_right):
    u, v, w = fields[:3]
    first = u * (factor * (2.0 * math.pi / (2 * SUB)))
    second = v * (factor * (2.0 * math.pi / (2 * SUB)))
    depth = w * (factor * (math.pi / (SUB * SUB)))
    along_u = sin_cos(first - depth, 5, 5)
    along_v = sin_cos(second - depth, 5, 5)
    turn = sin_cos(depth * 4.0, 3, 3)
    whole_u, whole_v = times(along_u, along_u), times(along_v, along_v)
    turn2 = times(turn, turn)
    turn3 = times(turn2, turn)
    both = times(along_u, along_v)
    wave = times(fields[3:], (both[0], -both[1]))
    one, zero = jnp.ones_like(u), jnp.zeros_like(u)
    all_u = interleave_pair(along_u, times(whole_u, along_u), low)
    all_v = interleave_pair(along_v, times(whole_v, along_v), low)
    all_wave = interleave_pair(wave, times(wave, turn), low)
    all_chirp = interleave_pair((one, zero), turn, low)
    all_grown = interleave_pair(turn3, times(turn3, turn2), low)
    all_before = interleave_pair((turn[0], -turn[1]), turn, low)
    twice_u = interleave(*[whole_u[0] * whole_u[1] * 4.0] * 2, low)
    twice_v = interleave(*[whole_v[0] * whole_v[1] * 4.0] * 2, low)
    twice_w = interleave(*[turn2[0] * turn2[1] * 4.0] * 2, low)
    for half in range(2):
        along_u, along_v = all_u[half], all_v[half]
        wave, chirp = all_wave[half], all_chirp[half]
        grown, before_grown = all_grown[half], all_before[half]
        before_u = (exchange(along_u[0]), -exchange(along_u[1]))
        before_v = (exchange(along_v[0]), -exchange(along_v[1]))
        for k in range(HALF // 2):
            if k > 0:
                chirp = times(chirp, grown)
                wave = times(wave, grown)
                along_u, before_u = advance(along_u, before_u, twice_u[half]), along_u
                along_v, before_v = advance(along_v, before_v, twice_v[half]), along_v
                grown, before_grown = advance(grown, before_grown, twice_w[half]), grown
            put_left(half, 0, k, wave[0] * along_u[0])
            put_left(half, 1, k, wave[1] * along_u[0])
            put_left(half, 2, k, wave[0] * along_u[1])
            put_left(half, 3, k, wave[1] * along_u[1])
            put_right(half, 0, k, chirp[0] * along_v[0])
            put_right(half, 1, k, chirp[1] * along_v[0])
            put_right(half, 2, k, chirp[0] * along_v[1])
            put_right(half, 3, k, chirp[1] * along_v[1])


def product(left, right, contract):
    left_high, left_low = split(left)
    right_high, right_low = split(right)
    return lax.dot_general(
        jnp.concatenate([left_high, left_high, left_low], axis=1),
        jnp.concatenate([right_high, right_low, right_high], axis=contract),
        (((1,), (contract,)), ((), ())),
        preferred_element_type=jnp.float32,
    )


def picture_kernel(
    ch,
    label_ref,
    scale_ref,
    corner_ref,
    x_ref,
    mix_ref,
    spread_ref,
    out_ref,
    left,
    right,
    sums,
    mixed,
    wide,
    strip,
):
    step = pl.program_id(0)
    capacity = SUBW
    tiles = out_ref.shape[0]
    part = GROUP // 2

    @pl.when(step == 0)
    def _():
        sums[...] = jnp.zeros_like(sums)

    low = lax.broadcasted_iota(jnp.int32, (GROUP, ROWS), 0) < part
    units = [
        (source, group) for source in range(x_ref.shape[0]) for group in range(capacity // GROUP)
    ]

    def factors(unit):
        source, group = units[unit]

        def field(index):
            start = index * capacity + group * GROUP
            return x_ref[source, start : start + GROUP, :]

        def put(ref, half, kind, k, value):
            ref[unit, half, pl.ds(kind * HALF * part + k * GROUP, GROUP), :] = value

        chosen = [field(index) for index in (0, 1, 2, 3 + 2 * ch, 4 + 2 * ch)]
        factor_rows(
            chosen, scale_ref[ch], low, functools.partial(put, left), functools.partial(put, right)
        )

    def gather(unit):
        for slot in range(GROUP):
            label = label_ref[(step * len(units) + unit) * GROUP + slot]
            rows = pl.ds(slot % part, TERMS, stride=part)
            half = slot // part
            sums[label] += product(left[unit, half, rows, :], right[unit, half, rows, :], 1)

    factors(0)
    for unit in range(1, len(units)):
        factors(unit)
        gather(unit - 1)
    gather(len(units) - 1)

    @pl.when(step == pl.num_programs(0) - 1)
    def _():
        strip[...] = jnp.zeros_like(strip)
        for subgrid in range(SUBW):
            mixed[subgrid * 2 * SUB : (subgrid + 1) * 2 * SUB, :] = product(
                mix_ref[...], sums[subgrid], 0
            )
        wide[...] = product(mixed[...], spread_ref[...], 0)
        for subgrid in range(SUBW):
            shift = corner_ref[subgrid, 1]
            rows = pl.ds(corner_ref[subgrid, 0], SUB)
            top = pl.ds(subgrid * 2 * SUB, SUB)
            bottom = pl.ds(subgrid * 2 * SUB + SUB, SUB)
            real = wide[top, :GCW] - wide[bottom, GCW:]
            imag = wide[top, GCW:] + wide[bottom, :GCW]
            strip[0, rows, :] += pltpu.roll(real, shift, 1)
            strip[1, rows, :] += pltpu.roll(imag, shift, 1)
        for tile in range(tiles):
            for plane in range(2):
                out_ref[tile, plane] = strip[plane, tile * TR : (tile + 1) * TR, :]


def transform_tables():
    k = np.arange(SUB)[:, None]
    h = np.arange(HALF)[None, :]

    def tapered(x):
        return np.sin(np.pi * (x + 0.5) / SUB) ** 2 * np.exp(-2j * np.pi * k * x / SUB)

    upper, lower = tapered(HALF + h), tapered(HALF - 1 - h)
    even, odd = upper + lower, upper - lower
    table = np.concatenate([even, 1j * even, 1j * odd, -odd], axis=1)
    real, imag = table.real, table.imag
    mix = np.concatenate([real, imag], axis=0) / (ROWS * SUB)
    spread = np.zeros((TERMS, 2 * GCW))
    spread[:, :SUB] = real.T
    spread[:, GCW : GCW + SUB] = imag.T
    return mix.astype(np.float32), spread.astype(np.float32)


def channel_strip(ch, labels, scale, corners, arrived, tiles):
    sources = arrived.shape[0]
    mix, spread = transform_tables()
    parts = (SPAN * SUBW // GROUP, 2, TERMS * GROUP // 2, ROWS)
    return pl.pallas_call(
        functools.partial(picture_kernel, ch),
        name="pictures",
        out_shape=jax.ShapeDtypeStruct((tiles, 2, TR, GCW), jnp.float32),
        grid_spec=pltpu.PrefetchScalarGridSpec(
            num_scalar_prefetch=3,
            grid=(sources // SPAN,),
            in_specs=[
                pl.BlockSpec((SPAN, arrived.shape[1], ROWS), lambda i, *_: (i, 0, 0)),
                pl.BlockSpec(mix.shape, lambda i, *_: (0, 0)),
                pl.BlockSpec(spread.shape, lambda i, *_: (0, 0)),
            ],
            out_specs=pl.BlockSpec((tiles, 2, TR, GCW), lambda i, *_: (0, 0, 0, 0)),
            scratch_shapes=[
                pltpu.VMEM(parts, jnp.float32),
                pltpu.VMEM(parts, jnp.float32),
                pltpu.VMEM((SUBW, TERMS, TERMS), jnp.float32),
                pltpu.VMEM((SUBW * 2 * SUB, TERMS), jnp.float32),
                pltpu.VMEM((SUBW * 2 * SUB, 2 * GCW), jnp.float32),
                pltpu.VMEM((2, TR * tiles, GCW), jnp.float32),
            ],
        ),
        compiler_params=pltpu.CompilerParams(
            dimension_semantics=("arbitrary",), vmem_limit_bytes=20 << 20
        ),
        cost_estimate=pl.CostEstimate(
            flops=3 * 2 * sources * SUBW * TERMS * TERMS * ROWS,
            bytes_accessed=4 * (arrived.size + tiles * 2 * TR * GCW),
            transcendentals=0,
        ),
    )(labels, scale, corners, arrived, jnp.asarray(mix), jnp.asarray(spread))


def local(block_coords, block_visibilities, subgrid_of_block, live_blocks, corners, channel_scale):
    workers = lax.axis_size("work")
    tiles = lax.axis_size("tile")
    worker = lax.axis_index("work")
    coords = jnp.swapaxes(block_coords, 0, 1)
    packed = pack(subgrid_of_block, live_blocks, coords, block_visibilities, workers)
    arrived = lax.all_to_all(packed, "work", split_axis=0, concat_axis=0, tiled=True)
    labels = arrived[:, FIELDS * SUBW, :SUBW].astype(jnp.int32).reshape(workers * SUBW)
    local_corners = lax.dynamic_slice_in_dim(corners, worker * SUBW, SUBW, 0)
    local_corners = local_corners - jnp.stack([0 * worker, worker * GCW])[None, :]
    planes = []
    for ch in range(CH):
        strip = channel_strip(ch, labels, channel_scale, local_corners, arrived, tiles)
        gathered = lax.all_to_all(strip, "tile", split_axis=0, concat_axis=0, tiled=True)
        planes.append(gathered.sum(axis=0))
    return jnp.concatenate(planes, axis=0)


def solution(mesh):
    return jax.shard_map(
        local,
        mesh=mesh,
        in_specs=(
            P(("work", "tile"), None, None),
            P(("work", "tile"), None, None),
            P(("work", "tile")),
            P(("work", "tile")),
            P(),
            P(),
        ),
        out_specs=P(None, "tile", "work"),
        check_vma=False,
    )
```

time: 121 us -> 110 us (0.909)
  the two profiles are of different devices: /device:TPU:96 before, /device:TPU:2 now
where the time goes in v3:
time: 110 us; the launch traced here: 109 us
  waiting for transfers between devices  42.9 us (39%)
  Pallas kernels  38.6 us (35%)
  starting transfers between devices  23.5 us (21%)
  local copies, waits for them, and re-layouts  2.78 us (3%)
    pallas_call x2, Pallas kernels, channel_strip(): pl.pallas_call(functools.partial(picture_kernel, ch), name='pictures', ou...  35.3 us
    all_to_all x1, waiting for transfers between devices, local(): lax.all_to_all(packed, 'work', split_axis=0, concat_axis=0, tiled=True)  26.2 us
    all_to_all x2, waiting for transfers between devices, local(): lax.all_to_all(strip, 'tile', split_axis=0, concat_axis=0, tiled=True)  16.7 us
    all_to_all x2, starting transfers between devices, local(): lax.all_to_all(strip, 'tile', split_axis=0, concat_axis=0, tiled=True)  15.8 us
    all_to_all x1, starting transfers between devices, local(): lax.all_to_all(packed, 'work', split_axis=0, concat_axis=0, tiled=True)  7.75 us
    pallas_call x1, Pallas kernels, pack(): pl.pallas_call(pack_kernel, name='pack', out_shape=jax.ShapeDtypeStruct((...  3.37 us
    unnamed x15, local copies, waits for them, and re-layouts  2.63 us
  transfers between devices with their start and end apart: 3, of which 2 were waited for; matrix products, arithmetic and copies ran while one was open for 0% of the time, Pallas kernels for 16%

profile of v3, /device:TPU:2, one launch (start us, length us, event | category | flops | bytes accessed | tf_op | source)
XLA Modules:
  0.0 109.4 jit_solution(3165294959988501082)
XLA Ops:
  0.0 0.0 copy-start
  0.7 0.0 copy-start.1
  0.7 0.9 copy-done.1
  1.6 0.9 copy-done.2
  2.5 0.7 copy-done.3
  3.2 3.4 %pack.1 = f32[32,120,128]{2,1,0:T(8,128)} custom-call(s32[128]{0:T(128)S(1)} %copy-done.3, s32[1]{0:T(128)S(6)} %copy.14.live_ref, f32[3,128,128]{2,1,0:T(8,128)S(1)} %bitcast.2, f32[128,4,128]{2,1,0:T(4,128)S(1)} %copy-done.1), custom_call_target="tpu_custom_call" | custom-call | tf_op jit(solution)/shard_map/pack/pallas_call | solution.py:65
  6.6 7.8 %all-to-all-start = ((f32[32,120,128]{2,1,0:T(8,128)}), f32[32,120,128]{2,1,0:T(8,128)S(1)}, u32[]{:S(2)}, u32[]{:S(2)}) async-start(f32[32,120,128]{2,1,0:T(8,128)} %pack.1), calls=%async_computation | async-start | bytes 3932160 | tf_op jit(solution)/shard_map/all_to_all | solution.py:320
  14.3 0.0 copy-done
  14.4 0.1 constant_dynamic-slice_fusion
  14.4 0.1 copy.13
  14.5 0.1 pad_add_fusion
  14.6 26.2 %all-to-all-done.x_ref = f32[32,120,128]{2,1,0:T(8,128)S(1)} async-done(((f32[32,120,128]{2,1,0:T(8,128)}), f32[32,120,128]{2,1,0:T(8,128)S(1)}, u32[]{:S(2)}, u32[]{:S(2)}) %all-to-all-start) | async-done | bytes 1966112 | tf_op jit(solution)/shard_map/all_to_all | solution.py:320
  40.8 0.1 fusion
  40.9 0.1 convert_element_type.8.label_ref
  40.9 0.0 copy-done.4
  41.0 0.0 copy-done.5
  41.0 0.0 copy-done.6
  41.0 17.6 %pictures.3 = f32[8,2,64,128]{3,2,1,0:T(8,128)} custom-call(s32[512]{0:T(512)S(1)} %convert_element_type.8.label_ref, f32[2]{0:T(128)S(1)} %copy-done.4, s32[16,2]{1,0:T(8,128)S(1)} %broadcast_subtract_fusion.corner_ref, f32[32,120,128]{2,1,0:T(8,128)S(1)} %all-to-all-done.x_ref, f32[64,64]{1,0:T(8,128)S(1)} %copy-done.6, f32[64,256]{1,0:T(8,128)S(1)} %copy-done.5), custom_call_target="tpu_custom_call" | custom-call | flops 1610612736 | bytes 2490368 | tf_op jit(solution)/shard_map/pictures/pallas_call | solution.py:281
  58.6 8.6 %all-to-all-start.2 = ((f32[8,2,64,128]{3,2,1,0:T(8,128)}), f32[8,2,64,128]{3,2,1,0:T(8,128)S(1)}, u32[]{:S(2)}, u32[]{:S(2)}) async-start(f32[8,2,64,128]{3,2,1,0:T(8,128)} %pictures.3), calls=%async_computation.2 | async-start | bytes 1048576 | tf_op jit(solution)/shard_map/all_to_all | solution.py:327
  67.2 17.6 %pictures.2 = f32[8,2,64,128]{3,2,1,0:T(8,128)} custom-call(s32[512]{0:T(512)S(1)} %convert_element_type.8.label_ref, f32[2]{0:T(128)S(1)} %copy-done.4, s32[16,2]{1,0:T(8,128)S(1)} %broadcast_subtract_fusion.corner_ref, f32[32,120,128]{2,1,0:T(8,128)S(1)} %all-to-all-done.x_ref, f32[64,64]{1,0:T(8,128)S(1)} %copy-done.6, f32[64,256]{1,0:T(8,128)S(1)} %copy-done.5), custom_call_target="tpu_custom_call" | custom-call | flops 1610612736 | bytes 2490368 | tf_op jit(solution)/shard_map/pictures/pallas_call | solution.py:281
  84.8 0.0 all-to-all-done.2
  84.8 7.2 %all-to-all-start.1 = ((f32[8,2,64,128]{3,2,1,0:T(8,128)}), f32[8,2,64,128]{3,2,1,0:T(8,128)S(1)}, u32[]{:S(2)}, u32[]{:S(2)}) async-start(f32[8,2,64,128]{3,2,1,0:T(8,128)} %pictures.2), calls=%async_computation.1 | async-start | bytes 1048576 | tf_op jit(solution)/shard_map/all_to_all | solution.py:327
  92.0 16.7 %all-to-all-done.1 = f32[8,2,64,128]{3,2,1,0:T(8,128)S(1)} async-done(((f32[8,2,64,128]{3,2,1,0:T(8,128)}), f32[8,2,64,128]{3,2,1,0:T(8,128)S(1)}, u32[]{:S(2)}, u32[]{:S(2)}) %all-to-all-start.1) | async-done | bytes 524320 | tf_op jit(solution)/shard_map/all_to_all | solution.py:327
  108.7 0.7 pad_maximum_fusion
  (8 shorter events, 0.1 us)
Async XLA Ops:
  0.0 14.3 %copy-start = (s32[512,2]{0,1:T(2,128)S(1)}, s32[512,2]{0,1:T(2,128)}, u32[]{:S(2)}) copy-start(s32[512,2]{0,1:T(2,128)} %param.14) | copy-start | bytes 12292
  0.7 1.0 copy-start.1
  1.6 0.9 copy-start.2
  2.5 0.7 copy-start.3
  6.6 34.4 %copy-start.4 = (f32[2]{0:T(128)S(1)}, f32[2]{0:T(128)}, u32[]{:S(2)}) copy-start(f32[2]{0:T(128)} %scale_ref.3) | copy-start | bytes 28
  6.6 34.4 %copy-start.5 = (f32[64,256]{1,0:T(8,128)S(1)}, f32[64,256]{1,0:T(8,128)}, u32[]{:S(2)}) copy-start(f32[64,256]{1,0:T(8,128)} %constant.23.clone.spread_ref) | copy-start | bytes 196612
  6.6 34.4 %copy-start.6 = (f32[64,64]{1,0:T(8,128)S(1)}, f32[64,64]{1,0:T(8,128)}, u32[]{:S(2)}) copy-start(f32[64,64]{1,0:T(8,128)} %constant.22.clone.mix_ref) | copy-start | bytes 49156
  6.6 34.2 %all-to-all-start = ((f32[32,120,128]{2,1,0:T(8,128)}), f32[32,120,128]{2,1,0:T(8,128)S(1)}, u32[]{:S(2)}, u32[]{:S(2)}) async-start(f32[32,120,128]{2,1,0:T(8,128)} %pack.1), calls=%async_computation | async-start | bytes 3932160 | tf_op jit(solution)/shard_map/all_to_all | solution.py:320
  58.6 26.2 %all-to-all-start.2 = ((f32[8,2,64,128]{3,2,1,0:T(8,128)}), f32[8,2,64,128]{3,2,1,0:T(8,128)S(1)}, u32[]{:S(2)}, u32[]{:S(2)}) async-start(f32[8,2,64,128]{3,2,1,0:T(8,128)} %pictures.3), calls=%async_computation.2 | async-start | bytes 1048576 | tf_op jit(solution)/shard_map/all_to_all | solution.py:327
  84.8 23.9 %all-to-all-start.1 = ((f32[8,2,64,128]{3,2,1,0:T(8,128)}), f32[8,2,64,128]{3,2,1,0:T(8,128)S(1)}, u32[]{:S(2)}, u32[]{:S(2)}) async-start(f32[8,2,64,128]{3,2,1,0:T(8,128)} %pictures.2), calls=%async_computation.1 | async-start | bytes 1048576 | tf_op jit(solution)/shard_map/all_to_all | solution.py:327

commit v4 on v3

--- a/solution.py
+++ b/solution.py
@@ -52,7 +52,7 @@
                     waves_ref[block, pl.ds(field, 1), :] * kept
                 )
             row = pl.ds(FIELDS * capacity, 1)
-            inside = (label - worker * SUBW).astype(jnp.float32)
+            inside = (label - worker * SUBW + 1).astype(jnp.float32) * kept
             out_ref[worker, row, :] = jnp.where(lane == slot, inside, out_ref[worker, row, :])
         return carry
 
@@ -69,7 +69,6 @@
         in_specs=[smem, smem, vmem, vmem],
         out_specs=vmem,
         scratch_shapes=[pltpu.SMEM((workers,), jnp.int32)],
-        compiler_params=pltpu.CompilerParams(vmem_limit_bytes=8 << 20),
     )(labels, live, coords, waves)
 
 
@@ -223,16 +222,32 @@
 
     def gather(unit):
         for slot in range(GROUP):
-            label = label_ref[(step * len(units) + unit) * GROUP + slot]
+            label = jnp.maximum(label_ref[(step * len(units) + unit) * GROUP + slot], 0)
             rows = pl.ds(slot % part, TERMS, stride=part)
             half = slot // part
             sums[label] += product(left[unit, half, rows, :], right[unit, half, rows, :], 1)
 
-    factors(0)
-    for unit in range(1, len(units)):
-        factors(unit)
-        gather(unit - 1)
-    gather(len(units) - 1)
+    def run(chosen):
+        factors(chosen[0])
+        for before, unit in zip(chosen[:-1], chosen[1:]):
+            factors(unit)
+            gather(before)
+        gather(chosen[-1])
+
+    first_units = [unit for unit in range(len(units)) if units[unit][1] == 0]
+    later_units = [unit for unit in range(len(units)) if units[unit][1] > 0]
+    crowded = functools.reduce(
+        jnp.logical_or,
+        [label_ref[(step * len(units) + unit) * GROUP] >= 0 for unit in later_units],
+    )
+
+    @pl.when(crowded)
+    def _():
+        run(list(range(len(units))))
+
+    @pl.when(jnp.logical_not(crowded))
+    def _():
+        run(first_units)
 
     @pl.when(step == pl.num_programs(0) - 1)
     def _():
@@ -318,7 +333,7 @@
     coords = jnp.swapaxes(block_coords, 0, 1)
     packed = pack(subgrid_of_block, live_blocks, coords, block_visibilities, workers)
     arrived = lax.all_to_all(packed, "work", split_axis=0, concat_axis=0, tiled=True)
-    labels = arrived[:, FIELDS * SUBW, :SUBW].astype(jnp.int32).reshape(workers * SUBW)
+    labels = arrived[:, FIELDS * SUBW, :SUBW].astype(jnp.int32).reshape(workers * SUBW) - 1
     local_corners = lax.dynamic_slice_in_dim(corners, worker * SUBW, SUBW, 0)
     local_corners = local_corners - jnp.stack([0 * worker, worker * GCW])[None, :]
     planes = []

time: 110 us -> 104 us (0.945); the launches traced: 109 us -> 105 us
  waiting for transfers between devices: 42.9 us -> 39.5 us
  local copies, waits for them, and re-layouts: 2.78 us -> 0.26 us
  Pallas kernels: 38.6 us -> 40 us
    all_to_all x2, waiting for transfers between devices: 16.7 us -> 13.3 us  [local(): lax.all_to_all(strip, 'tile', split_axis=0, concat_axis=0, tiled=True)]
    unnamed x15 -> x9, local copies, waits for them, and re-layouts: 2.63 us -> 0.1 us
  transfers between devices with their start and end apart: 3 -> 3, of which waited for: 2 -> 2; matrix products, arithmetic and copies ran while one was open for 0% -> 0% of each run, Pallas kernels for 16% -> 17%
where the time goes in v4:
time: 104 us; the launch traced here: 105 us
  Pallas kernels  40 us (38%)
  waiting for transfers between devices  39.5 us (38%)
  starting transfers between devices  23.4 us (22%)
    pallas_call x2, Pallas kernels, channel_strip(): pl.pallas_call(functools.partial(picture_kernel, ch), name='pictures', ou...  36 us
    all_to_all x1, waiting for transfers between devices, local(): lax.all_to_all(packed, 'work', split_axis=0, concat_axis=0, tiled=True)  26.2 us
    all_to_all x2, starting transfers between devices, local(): lax.all_to_all(strip, 'tile', split_axis=0, concat_axis=0, tiled=True)  15.7 us
    all_to_all x2, waiting for transfers between devices, local(): lax.all_to_all(strip, 'tile', split_axis=0, concat_axis=0, tiled=True)  13.3 us
    all_to_all x1, starting transfers between devices, local(): lax.all_to_all(packed, 'work', split_axis=0, concat_axis=0, tiled=True)  7.76 us
    pallas_call x1, Pallas kernels, pack(): pl.pallas_call(pack_kernel, name='pack', out_shape=jax.ShapeDtypeStruct((...  3.98 us
  transfers between devices with their start and end apart: 3, of which 2 were waited for; matrix products, arithmetic and copies ran while one was open for 0% of the time, Pallas kernels for 17%

profile of v4, /device:TPU:2, one launch (start us, length us, event | category | flops | bytes accessed | tf_op | source)
XLA Modules:
  0.0 104.7 jit_solution(6952127570016501619)
XLA Ops:
  0.0 0.0 copy-start
  0.7 4.0 %pack.1 = f32[32,120,128]{2,1,0:T(8,128)} custom-call(s32[128]{0:T(128)} %label_ref.1, s32[1]{0:T(128)S(6)} %copy.14.live_ref, f32[3,128,128]{2,1,0:T(8,128)} %bitcast.2, f32[128,4,128]{2,1,0:T(4,128)} %waves_ref.1), custom_call_target="tpu_custom_call" | custom-call | tf_op jit(solution)/shard_map/pack/pallas_call | solution.py:65
  4.6 0.0 copy-start.1
  4.6 0.0 copy-start.2
  4.7 0.0 copy-start.3
  4.7 7.8 %all-to-all-start = ((f32[32,120,128]{2,1,0:T(8,128)}), f32[32,120,128]{2,1,0:T(8,128)S(1)}, u32[]{:S(2)}, u32[]{:S(2)}) async-start(f32[32,120,128]{2,1,0:T(8,128)} %pack.1), calls=%async_computation | async-start | bytes 3932160 | tf_op jit(solution)/shard_map/all_to_all | solution.py:335
  12.4 0.0 copy-done
  12.4 0.1 constant_dynamic-slice_fusion
  12.5 0.1 copy.13
  12.6 0.1 pad_add_fusion
  12.7 26.2 %all-to-all-done.x_ref = f32[32,120,128]{2,1,0:T(8,128)S(1)} async-done(((f32[32,120,128]{2,1,0:T(8,128)}), f32[32,120,128]{2,1,0:T(8,128)S(1)}, u32[]{:S(2)}, u32[]{:S(2)}) %all-to-all-start) | async-done | bytes 1966112 | tf_op jit(solution)/shard_map/all_to_all | solution.py:335
  38.9 0.1 fusion.1
  39.0 0.1 sub.15.label_ref
  39.0 0.0 copy-done.1
  39.0 0.0 copy-done.2
  39.0 0.0 copy-done.3
  39.0 18.0 %pictures.3 = f32[8,2,64,128]{3,2,1,0:T(8,128)} custom-call(s32[512]{0:T(512)S(1)} %sub.15.label_ref, f32[2]{0:T(128)S(1)} %copy-done.1, s32[16,2]{1,0:T(8,128)S(1)} %broadcast_subtract_fusion.corner_ref, f32[32,120,128]{2,1,0:T(8,128)S(1)} %all-to-all-done.x_ref, f32[64,64]{1,0:T(8,128)S(1)} %copy-done.3, f32[64,256]{1,0:T(8,128)S(1)} %copy-done.2), custom_call_target="tpu_custom_call" | custom-call | flops 1610612736 | bytes 2490368 | tf_op jit(solution)/shard_map/pictures/pallas_call | solution.py:296
  57.1 8.5 %all-to-all-start.2 = ((f32[8,2,64,128]{3,2,1,0:T(8,128)}), f32[8,2,64,128]{3,2,1,0:T(8,128)S(1)}, u32[]{:S(2)}, u32[]{:S(2)}) async-start(f32[8,2,64,128]{3,2,1,0:T(8,128)} %pictures.3), calls=%async_computation.2 | async-start | bytes 1048576 | tf_op jit(solution)/shard_map/all_to_all | solution.py:342
  65.5 18.0 %pictures.2 = f32[8,2,64,128]{3,2,1,0:T(8,128)} custom-call(s32[512]{0:T(512)S(1)} %sub.15.label_ref, f32[2]{0:T(128)S(1)} %copy-done.1, s32[16,2]{1,0:T(8,128)S(1)} %broadcast_subtract_fusion.corner_ref, f32[32,120,128]{2,1,0:T(8,128)S(1)} %all-to-all-done.x_ref, f32[64,64]{1,0:T(8,128)S(1)} %copy-done.3, f32[64,256]{1,0:T(8,128)S(1)} %copy-done.2), custom_call_target="tpu_custom_call" | custom-call | flops 1610612736 | bytes 2490368 | tf_op jit(solution)/shard_map/pictures/pallas_call | solution.py:296
  83.6 0.0 all-to-all-done.2
  83.6 7.2 %all-to-all-start.1 = ((f32[8,2,64,128]{3,2,1,0:T(8,128)}), f32[8,2,64,128]{3,2,1,0:T(8,128)S(1)}, u32[]{:S(2)}, u32[]{:S(2)}) async-start(f32[8,2,64,128]{3,2,1,0:T(8,128)} %pictures.2), calls=%async_computation.1 | async-start | bytes 1048576 | tf_op jit(solution)/shard_map/all_to_all | solution.py:342
  90.8 13.3 %all-to-all-done.1 = f32[8,2,64,128]{3,2,1,0:T(8,128)S(1)} async-done(((f32[8,2,64,128]{3,2,1,0:T(8,128)}), f32[8,2,64,128]{3,2,1,0:T(8,128)S(1)}, u32[]{:S(2)}, u32[]{:S(2)}) %all-to-all-start.1) | async-done | bytes 524320 | tf_op jit(solution)/shard_map/all_to_all | solution.py:342
  104.1 0.7 pad_maximum_fusion
  (3 shorter events, 0.1 us)
Async XLA Ops:
  0.0 12.4 %copy-start = (s32[512,2]{0,1:T(2,128)S(1)}, s32[512,2]{0,1:T(2,128)}, u32[]{:S(2)}) copy-start(s32[512,2]{0,1:T(2,128)} %param.14) | copy-start | bytes 12292
  4.6 34.4 %copy-start.1 = (f32[2]{0:T(128)S(1)}, f32[2]{0:T(128)}, u32[]{:S(2)}) copy-start(f32[2]{0:T(128)} %scale_ref.3) | copy-start | bytes 28
  4.6 34.4 %copy-start.2 = (f32[64,256]{1,0:T(8,128)S(1)}, f32[64,256]{1,0:T(8,128)}, u32[]{:S(2)}) copy-start(f32[64,256]{1,0:T(8,128)} %constant.26.clone.spread_ref) | copy-start | bytes 196612
  4.7 34.4 %copy-start.3 = (f32[64,64]{1,0:T(8,128)S(1)}, f32[64,64]{1,0:T(8,128)}, u32[]{:S(2)}) copy-start(f32[64,64]{1,0:T(8,128)} %constant.25.clone.mix_ref) | copy-start | bytes 49156
  4.7 34.2 %all-to-all-start = ((f32[32,120,128]{2,1,0:T(8,128)}), f32[32,120,128]{2,1,0:T(8,128)S(1)}, u32[]{:S(2)}, u32[]{:S(2)}) async-start(f32[32,120,128]{2,1,0:T(8,128)} %pack.1), calls=%async_computation | async-start | bytes 3932160 | tf_op jit(solution)/shard_map/all_to_all | solution.py:335
  57.1 26.5 %all-to-all-start.2 = ((f32[8,2,64,128]{3,2,1,0:T(8,128)}), f32[8,2,64,128]{3,2,1,0:T(8,128)S(1)}, u32[]{:S(2)}, u32[]{:S(2)}) async-start(f32[8,2,64,128]{3,2,1,0:T(8,128)} %pictures.3), calls=%async_computation.2 | async-start | bytes 1048576 | tf_op jit(solution)/shard_map/all_to_all | solution.py:342
  83.6 20.5 %all-to-all-start.1 = ((f32[8,2,64,128]{3,2,1,0:T(8,128)}), f32[8,2,64,128]{3,2,1,0:T(8,128)S(1)}, u32[]{:S(2)}, u32[]{:S(2)}) async-start(f32[8,2,64,128]{3,2,1,0:T(8,128)} %pictures.2), calls=%async_computation.1 | async-start | bytes 1048576 | tf_op jit(solution)/shard_map/all_to_all | solution.py:342

commit v5 on v3

v5 whole, which is shorter than its diff:
```python
import functools
import math

import jax
import jax.numpy as jnp
import numpy as np
from jax import lax
from jax.experimental import pallas as pl
from jax.experimental.pallas import tpu as pltpu
from jax.sharding import PartitionSpec as P


CH = 2
SUB = 32
HALF = SUB // 2
ROWS = 128
TR = 64
GCW = 128
SUBW = 16
FIELDS = 3 + 2 * CH
TERMS = 4 * HALF
GROUP = 8
SPAN = 4
CHUNKS = SUBW // GROUP
UNROLL = 8


def pack_kernel(label_ref, live_ref, coords_ref, waves_ref, *refs):
    out_refs, (room, count_ref) = refs[:CHUNKS], refs[CHUNKS:]
    workers = room.shape[1]
    room[...] = jnp.zeros_like(room)

    def clear(worker, carry):
        count_ref[worker] = 0
        return carry

    lax.fori_loop(0, workers, clear, 0)
    lane = lax.broadcasted_iota(jnp.int32, (1, ROWS), 1)
    live = live_ref[0]

    def move(group, carry):
        for offset in range(UNROLL):
            block = group * UNROLL + offset
            label = label_ref[block]
            worker = label // SUBW
            count = count_ref[worker]
            count_ref[worker] = count + 1
            chunk, slot = count // GROUP, count % GROUP
            kept = jnp.where(block < live, 1.0, 0.0)
            for field in range(3):
                room[chunk, worker, pl.ds(field * GROUP + slot, 1), :] = coords_ref[
                    field, pl.ds(block, 1), :
                ]
            for field in range(2 * CH):
                room[chunk, worker, pl.ds((3 + field) * GROUP + slot, 1), :] = (
                    waves_ref[block, pl.ds(field, 1), :] * kept
                )
            row = pl.ds(FIELDS * GROUP, 1)
            inside = (label - worker * SUBW + 1).astype(jnp.float32) * kept
            room[chunk, worker, row, :] = jnp.where(
                lane == slot, inside, room[chunk, worker, row, :]
            )
        return carry

    lax.fori_loop(0, label_ref.shape[0] // UNROLL, move, 0)
    for chunk in range(CHUNKS):
        out_refs[chunk][...] = room[chunk]


def pack(labels, live, coords, waves, workers):
    smem = pl.BlockSpec(memory_space=pltpu.SMEM)
    vmem = pl.BlockSpec(memory_space=pltpu.VMEM)
    shape = (workers, (FIELDS + 1) * GROUP, ROWS)
    return pl.pallas_call(
        pack_kernel,
        name="pack",
        out_shape=[jax.ShapeDtypeStruct(shape, jnp.float32)] * CHUNKS,
        in_specs=[smem, smem, vmem, vmem],
        out_specs=[vmem] * CHUNKS,
        scratch_shapes=[
            pltpu.VMEM((CHUNKS,) + shape, jnp.float32),
            pltpu.SMEM((workers,), jnp.int32),
        ],
    )(labels, live, coords, waves)


def series(square, first, count):
    terms = [(-1.0) ** n / math.factorial(2 * n + first) for n in range(count)]
    total = square * terms[-1] + terms[-2]
    for term in terms[-3::-1]:
        total = total * square + term
    return total


def sin_cos(theta, sin_terms, cos_terms):
    square = theta * theta
    return series(square, 0, cos_terms), series(square, 1, sin_terms) * theta


def times(a, b):
    return a[0] * b[0] - a[1] * b[1], a[0] * b[1] + a[1] * b[0]


def split(value):
    high = value.astype(jnp.bfloat16)
    low = (value - high.astype(jnp.float32)).astype(jnp.bfloat16)
    return high, low


def advance(current, previous, twice_sine):
    return (
        previous[0] - twice_sine * current[1],
        previous[1] + twice_sine * current[0],
    )


def exchange(value):
    return pltpu.roll(value, GROUP // 2, 0)


def interleave(even, odd, low):
    return (
        jnp.where(low, even, exchange(odd)),
        jnp.where(low, exchange(even), odd),
    )


def interleave_pair(even, odd, low):
    real, imag = interleave(even[0], odd[0], low), interleave(even[1], odd[1], low)
    return (real[0], imag[0]), (real[1], imag[1])


def factor_rows(fields, factor, low, put_left, put_right):
    u, v, w = fields[:3]
    first = u * (factor * (2.0 * math.pi / (2 * SUB)))
    second = v * (factor * (2.0 * math.pi / (2 * SUB)))
    depth = w * (factor * (math.pi / (SUB * SUB)))
    along_u = sin_cos(first - depth, 5, 5)
    along_v = sin_cos(second - depth, 5, 5)
    turn = sin_cos(depth * 4.0, 3, 3)
    whole_u, whole_v = times(along_u, along_u), times(along_v, along_v)
    turn2 = times(turn, turn)
    turn3 = times(turn2, turn)
    both = times(along_u, along_v)
    wave = times(fields[3:], (both[0], -both[1]))
    one, zero = jnp.ones_like(u), jnp.zeros_like(u)
    all_u = interleave_pair(along_u, times(whole_u, along_u), low)
    all_v = interleave_pair(along_v, times(whole_v, along_v), low)
    all_wave = interleave_pair(wave, times(wave, turn), low)
    all_chirp = interleave_pair((one, zero), turn, low)
    all_grown = interleave_pair(turn3, times(turn3, turn2), low)
    all_before = interleave_pair((turn[0], -turn[1]), turn, low)
    twice_u = interleave(*[whole_u[0] * whole_u[1] * 4.0] * 2, low)
    twice_v = interleave(*[whole_v[0] * whole_v[1] * 4.0] * 2, low)
    twice_w = interleave(*[turn2[0] * turn2[1] * 4.0] * 2, low)
    for half in range(2):
        along_u, along_v = all_u[half], all_v[half]
        wave, chirp = all_wave[half], all_chirp[half]
        grown, before_grown = all_grown[half], all_before[half]
        before_u = (exchange(along_u[0]), -exchange(along_u[1]))
        before_v = (exchange(along_v[0]), -exchange(along_v[1]))
        for k in range(HALF // 2):
            if k > 0:
                chirp = times(chirp, grown)
                wave = times(wave, grown)
                along_u, before_u = advance(along_u, before_u, twice_u[half]), along_u
                along_v, before_v = advance(along_v, before_v, twice_v[half]), along_v
                grown, before_grown = advance(grown, before_grown, twice_w[half]), grown
            put_left(half, 0, k, wave[0] * along_u[0])
            put_left(half, 1, k, wave[1] * along_u[0])
            put_left(half, 2, k, wave[0] * along_u[1])
            put_left(half, 3, k, wave[1] * along_u[1])
            put_right(half, 0, k, chirp[0] * along_v[0])
            put_right(half, 1, k, chirp[1] * along_v[0])
            put_right(half, 2, k, chirp[0] * along_v[1])
            put_right(half, 3, k, chirp[1] * along_v[1])


def product(left, right, contract):
    left_high, left_low = split(left)
    right_high, right_low = split(right)
    return lax.dot_general(
        jnp.concatenate([left_high, left_high, left_low], axis=1),
        jnp.concatenate([right_high, right_low, right_high], axis=contract),
        (((1,), (contract,)), ((), ())),
        preferred_element_type=jnp.float32,
    )


def accumulate(label_ref, scale_ref, x_ref, left, right, sums):
    step = pl.program_id(0)
    part = GROUP // 2
    sources = x_ref.shape[0]
    low = lax.broadcasted_iota(jnp.int32, (GROUP, ROWS), 0) < part

    def factors(source, ch):
        def field(index):
            return x_ref[source, index * GROUP : (index + 1) * GROUP, :]

        def put(ref, half, kind, k, value):
            ref[source, ch, half, pl.ds(kind * HALF * part + k * GROUP, GROUP), :] = value

        chosen = [field(index) for index in (0, 1, 2, 3 + 2 * ch, 4 + 2 * ch)]
        factor_rows(
            chosen, scale_ref[ch], low, functools.partial(put, left), functools.partial(put, right)
        )

    def gather(source, ch):
        for slot in range(GROUP):
            label = jnp.maximum(label_ref[(step * sources + source) * GROUP + slot], 0)
            rows = pl.ds(slot % part, TERMS, stride=part)
            half = slot // part
            sums[ch, label] += product(
                left[source, ch, half, rows, :], right[source, ch, half, rows, :], 1
            )

    live = functools.reduce(
        jnp.logical_or,
        [label_ref[(step * sources + source) * GROUP] >= 0 for source in range(sources)],
    )

    @pl.when(live)
    def _():
        units = [(source, ch) for source in range(sources) for ch in range(CH)]
        factors(*units[0])
        for before, unit in zip(units[:-1], units[1:]):
            factors(*unit)
            gather(*before)
        gather(*units[-1])


def first_kernel(label_ref, scale_ref, x_ref, sums, left, right):
    @pl.when(pl.program_id(0) == 0)
    def _():
        sums[...] = jnp.zeros_like(sums)

    accumulate(label_ref, scale_ref, x_ref, left, right, sums)


def last_kernel(
    label_ref,
    scale_ref,
    corner_ref,
    x_ref,
    prior_ref,
    mix_ref,
    spread_ref,
    out_ref,
    left,
    right,
    sums,
    mixed,
    wide,
    strip,
):
    tiles = out_ref.shape[0]

    @pl.when(pl.program_id(0) == 0)
    def _():
        sums[...] = prior_ref[...]

    accumulate(label_ref, scale_ref, x_ref, left, right, sums)

    @pl.when(pl.program_id(0) == pl.num_programs(0) - 1)
    def _():
        strip[...] = jnp.zeros_like(strip)
        for ch in range(CH):
            for subgrid in range(SUBW):
                mixed[ch, subgrid * 2 * SUB : (subgrid + 1) * 2 * SUB, :] = product(
                    mix_ref[...], sums[ch, subgrid], 0
                )
            wide[ch] = product(mixed[ch], spread_ref[...], 0)
            for subgrid in range(SUBW):
                shift = corner_ref[subgrid, 1]
                rows = pl.ds(corner_ref[subgrid, 0], SUB)
                top = pl.ds(subgrid * 2 * SUB, SUB)
                bottom = pl.ds(subgrid * 2 * SUB + SUB, SUB)
                real = wide[ch, top, :GCW] - wide[ch, bottom, GCW:]
                imag = wide[ch, top, GCW:] + wide[ch, bottom, :GCW]
                strip[2 * ch, rows, :] += pltpu.roll(real, shift, 1)
                strip[2 * ch + 1, rows, :] += pltpu.roll(imag, shift, 1)
        for tile in range(tiles):
            for plane in range(2 * CH):
                out_ref[tile, plane] = strip[plane, tile * TR : (tile + 1) * TR, :]


def transform_tables():
    k = np.arange(SUB)[:, None]
    h = np.arange(HALF)[None, :]

    def tapered(x):
        return np.sin(np.pi * (x + 0.5) / SUB) ** 2 * np.exp(-2j * np.pi * k * x / SUB)

    upper, lower = tapered(HALF + h), tapered(HALF - 1 - h)
    even, odd = upper + lower, upper - lower
    table = np.concatenate([even, 1j * even, 1j * odd, -odd], axis=1)
    real, imag = table.real, table.imag
    mix = np.concatenate([real, imag], axis=0) / (ROWS * SUB)
    spread = np.zeros((TERMS, 2 * GCW))
    spread[:, :SUB] = real.T
    spread[:, GCW : GCW + SUB] = imag.T
    return mix.astype(np.float32), spread.astype(np.float32)


SUMS = (CH, SUBW, TERMS, TERMS)
ROOM = (SPAN, CH, 2, TERMS * GROUP // 2, ROWS)


def chunk_call(kernel, prefetched, arrived, extra, out_shape, scratch):
    sources = arrived.shape[0]
    whole = [pl.BlockSpec(x.shape, lambda i, *_, n=x.ndim: (0,) * n) for x in extra]
    return pl.pallas_call(
        kernel,
        out_shape=jax.ShapeDtypeStruct(out_shape, jnp.float32),
        grid_spec=pltpu.PrefetchScalarGridSpec(
            num_scalar_prefetch=len(prefetched),
            grid=(sources // SPAN,),
            in_specs=[pl.BlockSpec((SPAN, arrived.shape[1], ROWS), lambda i, *_: (i, 0, 0))]
            + whole,
            out_specs=pl.BlockSpec(out_shape, lambda i, *_: (0,) * len(out_shape)),
            scratch_shapes=[pltpu.VMEM(shape, jnp.float32) for shape in [ROOM, ROOM] + scratch],
        ),
        compiler_params=pltpu.CompilerParams(
            dimension_semantics=("arbitrary",), vmem_limit_bytes=28 << 20
        ),
        cost_estimate=pl.CostEstimate(
            flops=3 * 2 * CH * sources * GROUP * TERMS * TERMS * ROWS,
            bytes_accessed=4 * (arrived.size + math.prod(out_shape)),
            transcendentals=0,
        ),
    )(*prefetched, arrived, *extra)


def local(block_coords, block_visibilities, subgrid_of_block, live_blocks, corners, channel_scale):
    workers = lax.axis_size("work")
    tiles = lax.axis_size("tile")
    worker = lax.axis_index("work")
    coords = jnp.swapaxes(block_coords, 0, 1)
    packed = pack(subgrid_of_block, live_blocks, coords, block_visibilities, workers)
    local_corners = lax.dynamic_slice_in_dim(corners, worker * SUBW, SUBW, 0)
    local_corners = local_corners - jnp.stack([0 * worker, worker * GCW])[None, :]
    sums = None
    for chunk in range(CHUNKS):
        arrived = lax.all_to_all(packed[chunk], "work", split_axis=0, concat_axis=0, tiled=True)
        labels = arrived[:, FIELDS * GROUP, :GROUP].astype(jnp.int32).reshape(workers * GROUP) - 1
        if chunk == 0:
            sums = chunk_call(first_kernel, (labels, channel_scale), arrived, (), SUMS, [])
    mix, spread = transform_tables()
    strip = chunk_call(
        last_kernel,
        (labels, channel_scale, local_corners),
        arrived,
        (sums, jnp.asarray(mix), jnp.asarray(spread)),
        (tiles, 2 * CH, TR, GCW),
        [
            SUMS,
            (CH, SUBW * 2 * SUB, TERMS),
            (CH, SUBW * 2 * SUB, 2 * GCW),
            (2 * CH, TR * tiles, GCW),
        ],
    )
    gathered = lax.all_to_all(strip, "tile", split_axis=0, concat_axis=0, tiled=True)
    return gathered.sum(axis=0)


def solution(mesh):
    return jax.shard_map(
        local,
        mesh=mesh,
        in_specs=(
            P(("work", "tile"), None, None),
            P(("work", "tile"), None, None),
            P(("work", "tile")),
            P(("work", "tile")),
            P(),
            P(),
        ),
        out_specs=P(None, "tile", "work"),
        check_vma=False,
    )
```

time: 110 us -> 118 us (1.073)
  the two profiles are of different devices: /device:TPU:2 before, /device:TPU:7 now
where the time goes in v5:
time: 118 us
  blocking collectives  58.4 us (49%)
  Pallas kernels  35.9 us (30%)
  waiting for transfers between devices  15.5 us (13%)
  starting transfers between devices  5.19 us (4%)
    all_to_all x1, blocking collectives, local(): lax.all_to_all(strip, 'tile', split_axis=0, concat_axis=0, tiled=True)  34.7 us
    pallas_call x2, Pallas kernels, chunk_call(): pl.pallas_call(kernel, out_shape=jax.ShapeDtypeStruct(out_shape, jnp.floa...  31 us
    all_to_all x1, blocking collectives, local(): lax.all_to_all(packed[chunk], 'work', split_axis=0, concat_axis=0, tiled=...  23.7 us
    all_to_all x1, waiting for transfers between devices, local(): lax.all_to_all(packed[chunk], 'work', split_axis=0, concat_axis=0, tiled=...  15.5 us
    all_to_all x1, starting transfers between devices, local(): lax.all_to_all(packed[chunk], 'work', split_axis=0, concat_axis=0, tiled=...  5.19 us
    pallas_call x1, Pallas kernels, pack(): pl.pallas_call(pack_kernel, name='pack', out_shape=[jax.ShapeDtypeStruct(...  4.89 us
  transfers between devices with their start and end apart: 1, of which 1 were waited for; matrix products, arithmetic and copies ran while one was open for 0% of the time, Pallas kernels for 0%

profile of v5, /device:TPU:7, one launch (start us, length us, event | category | flops | bytes accessed | tf_op | source)
XLA Modules:
  0.0 117.6 jit_solution(3413142760343850940)
XLA Ops:
  0.0 0.0 copy-start
  0.7 4.9 %pack.1 = (f32[32,64,128]{2,1,0:T(8,128)}, f32[32,64,128]{2,1,0:T(8,128)}) custom-call(s32[128]{0:T(128)} %label_ref.1, s32[1]{0:T(128)S(6)} %copy.12.live_ref, f32[3,128,128]{2,1,0:T(8,128)} %bitcast.2, f32[128,4,128]{2,1,0:T(4,128)} %waves_ref.1), custom_call_target="tpu_custom_call" | custom-call | tf_op jit(solution)/shard_map/pack/pallas_call | solution.py:74
  5.6 23.7 %all_to_all.15.x_ref = f32[32,64,128]{2,1,0:T(8,128)S(1)} all-to-all(f32[32,64,128]{2,1,0:T(8,128)} %get-tuple-element.8), channel_id=1, replica_groups=mesh['work'=32,'tile'=8] {'work'}, dimensions={0} | all-to-all | bytes 2097152 | tf_op jit(solution)/shard_map/all_to_all | solution.py:344
  29.3 5.2 %all-to-all-start = ((f32[32,64,128]{2,1,0:T(8,128)}), f32[32,64,128]{2,1,0:T(8,128)S(1)}, u32[]{:S(2)}, u32[]{:S(2)}) async-start(f32[32,64,128]{2,1,0:T(8,128)} %get-tuple-element.7), calls=%async_computation | async-start | bytes 2097152 | tf_op jit(solution)/shard_map/all_to_all | solution.py:344
  34.5 0.0 copy-done
  34.5 0.1 constant_dynamic-slice_fusion
  34.6 0.1 copy.11
  34.7 0.1 pad_add_fusion
  34.7 0.1 fusion.1
  34.8 0.1 sub.23.label_ref
  34.9 15.5 %all-to-all-done.x_ref = f32[32,64,128]{2,1,0:T(8,128)S(1)} async-done(((f32[32,64,128]{2,1,0:T(8,128)}), f32[32,64,128]{2,1,0:T(8,128)S(1)}, u32[]{:S(2)}, u32[]{:S(2)}) %all-to-all-start) | async-done | bytes 1048608 | tf_op jit(solution)/shard_map/all_to_all | solution.py:344
  50.4 0.1 fusion.3
  50.5 0.0 copy-start.1
  50.5 0.1 sub.19.label_ref
  50.6 0.6 copy-done.1
  51.1 0.0 copy-start.2
  51.1 0.0 copy-start.3
  51.2 14.6 %shard_map.82.prior_ref = f32[2,16,64,64]{3,2,1,0:T(8,128)S(1)} custom-call(s32[256]{0:T(256)S(1)} %sub.23.label_ref, f32[2]{0:T(128)S(1)} %copy-done.1, f32[32,64,128]{2,1,0:T(8,128)S(1)} %all_to_all.15.x_ref), custom_call_target="tpu_custom_call" | custom-call | flops 1610612736 | bytes 1572864 | tf_op jit(solution)/shard_map/pallas_call | solution.py:312
  65.8 0.0 copy-done.2
  65.8 0.0 copy-done.3
  65.8 16.4 %shard_map.83 = f32[8,4,64,128]{3,2,1,0:T(8,128)S(1)} custom-call(s32[256]{0:T(256)S(1)} %sub.19.label_ref, f32[2]{0:T(128)S(1)} %copy-done.1, s32[16,2]{1,0:T(8,128)S(1)} %broadcast_subtract_fusion.corner_ref, f32[32,64,128]{2,1,0:T(8,128)S(1)} %all-to-all-done.x_ref, f32[2,16,64,64]{3,2,1,0:T(8,128)S(1)} %shard_map.82.prior_ref, f32[64,64]{1,0:T(8,128)S(1)} %copy-done.3, ...), custom_call_target="tpu_custom_call" | custom-call | flops 1610612736 | bytes 2097152 | tf_op jit(solution)/shard_map/pallas_call | solution.py:312
  82.2 34.7 %all_to_all.16 = f32[8,4,64,128]{3,2,1,0:T(8,128)S(1)} all-to-all(f32[8,4,64,128]{3,2,1,0:T(8,128)S(1)} %shard_map.83), channel_id=1, replica_groups=mesh['work'=32,'tile'=8] {'tile'}, dimensions={0} | all-to-all | bytes 2097152 | tf_op jit(solution)/shard_map/all_to_all | solution.py:362
  116.9 0.7 reduce_sum.9
  (1 shorter events, 0.0 us)
Async XLA Ops:
  0.0 34.5 %copy-start = (s32[512,2]{0,1:T(2,128)S(1)}, s32[512,2]{0,1:T(2,128)}, u32[]{:S(2)}) copy-start(s32[512,2]{0,1:T(2,128)} %param.12) | copy-start | bytes 12292
  29.3 21.1 %all-to-all-start = ((f32[32,64,128]{2,1,0:T(8,128)}), f32[32,64,128]{2,1,0:T(8,128)S(1)}, u32[]{:S(2)}, u32[]{:S(2)}) async-start(f32[32,64,128]{2,1,0:T(8,128)} %get-tuple-element.7), calls=%async_computation | async-start | bytes 2097152 | tf_op jit(solution)/shard_map/all_to_all | solution.py:344
  50.5 0.7 copy-start.1
  51.1 14.7 %copy-start.2 = (f32[64,256]{1,0:T(8,128)S(1)}, f32[64,256]{1,0:T(8,128)}, u32[]{:S(2)}) copy-start(f32[64,256]{1,0:T(8,128)} %constant.27.clone.spread_ref) | copy-start | bytes 196612
  51.1 14.7 %copy-start.3 = (f32[64,64]{1,0:T(8,128)S(1)}, f32[64,64]{1,0:T(8,128)}, u32[]{:S(2)}) copy-start(f32[64,64]{1,0:T(8,128)} %constant.26.clone.mix_ref) | copy-start | bytes 49156

commit v6 on v5

--- a/solution.py
+++ b/solution.py
@@ -241,6 +241,7 @@
     label_ref,
     scale_ref,
     corner_ref,
+    tile_ref,
     x_ref,
     prior_ref,
     mix_ref,
@@ -279,9 +280,11 @@
                 imag = wide[ch, top, GCW:] + wide[ch, bottom, :GCW]
                 strip[2 * ch, rows, :] += pltpu.roll(real, shift, 1)
                 strip[2 * ch + 1, rows, :] += pltpu.roll(imag, shift, 1)
-        for tile in range(tiles):
+        for distance in range(tiles):
+            tile = lax.rem(tile_ref[0] + distance, tiles)
+            rows = pl.ds(pl.multiple_of(tile * TR, TR), TR)
             for plane in range(2 * CH):
-                out_ref[tile, plane] = strip[plane, tile * TR : (tile + 1) * TR, :]
+                out_ref[distance, plane] = strip[plane, rows, :]
 
 
 def transform_tables():
@@ -331,6 +334,25 @@
     )(*prefetched, arrived, *extra)
 
 
+def summed_around(parts, axis):
+    size = lax.axis_size(axis)
+    far = size // 2
+    up = [(i, (i + 1) % size) for i in range(size)]
+    down = [(i, (i - 1) % size) for i in range(size)]
+    rising = lax.ppermute(parts[far, :CH], axis, up)
+    falling = lax.ppermute(parts[far, CH:], axis, down)
+    for distance in range(far - 1, 0, -1):
+        near, opposite = parts[distance], parts[size - distance]
+        if distance == far - 1:
+            rising = jnp.concatenate([near[:CH] + rising, near[CH:]])
+            falling = jnp.concatenate([opposite[:CH], opposite[CH:] + falling])
+        else:
+            rising, falling = near + rising, opposite + falling
+        rising = lax.ppermute(rising, axis, up)
+        falling = lax.ppermute(falling, axis, down)
+    return parts[0] + rising + falling
+
+
 def local(block_coords, block_visibilities, subgrid_of_block, live_blocks, corners, channel_scale):
     workers = lax.axis_size("work")
     tiles = lax.axis_size("tile")
@@ -346,9 +368,10 @@
         if chunk == 0:
             sums = chunk_call(first_kernel, (labels, channel_scale), arrived, (), SUMS, [])
     mix, spread = transform_tables()
-    strip = chunk_call(
+    tile = lax.axis_index("tile").astype(jnp.int32).reshape(1)
+    parts = chunk_call(
         last_kernel,
-        (labels, channel_scale, local_corners),
+        (labels, channel_scale, local_corners, tile),
         arrived,
         (sums, jnp.asarray(mix), jnp.asarray(spread)),
         (tiles, 2 * CH, TR, GCW),
@@ -359,8 +382,7 @@
             (2 * CH, TR * tiles, GCW),
         ],
     )
-    gathered = lax.all_to_all(strip, "tile", split_axis=0, concat_axis=0, tiled=True)
-    return gathered.sum(axis=0)
+    return summed_around(parts, "tile")
 
 
 def solution(mesh):

time: 118 us -> 113 us (0.958)
  the two profiles are of different devices: /device:TPU:7 before, /device:TPU:120 now
where the time goes in v6:
time: 113 us
  waiting for transfers between devices  35.5 us (31%)
  Pallas kernels  28.9 us (26%)
  starting transfers between devices  23.4 us (21%)
  blocking collectives  22.3 us (20%)
    pallas_call x2, Pallas kernels, chunk_call(): pl.pallas_call(kernel, out_shape=jax.ShapeDtypeStruct(out_shape, jnp.floa...  24 us
    all_to_all x1, blocking collectives, local(): lax.all_to_all(packed[chunk], 'work', split_axis=0, concat_axis=0, tiled=...  22.3 us
    all_to_all x1, waiting for transfers between devices, local(): lax.all_to_all(packed[chunk], 'work', split_axis=0, concat_axis=0, tiled=...  14.6 us
    ppermute x1, starting transfers between devices, summed_around(): rising = lax.ppermute(parts[far, :CH], axis, up)  10.2 us
    ppermute x3, waiting for transfers between devices, summed_around(): falling = lax.ppermute(falling, axis, down)  9.1 us
    ppermute x3, waiting for transfers between devices, summed_around(): rising = lax.ppermute(rising, axis, up)  6.41 us
    all_to_all x1, starting transfers between devices, local(): lax.all_to_all(packed[chunk], 'work', split_axis=0, concat_axis=0, tiled=...  6.18 us
    ppermute x3, starting transfers between devices, summed_around(): rising = lax.ppermute(rising, axis, up)  4.97 us
  transfers between devices with their start and end apart: 9, of which 7 were waited for; matrix products, arithmetic and copies ran while one was open for 0% of the time, Pallas kernels for 0%

profile of v6, /device:TPU:120, one launch (start us, length us, event | category | flops | bytes accessed | tf_op | source)
XLA Modules:
  0.0 112.8 jit_solution(12116623992224008387)
XLA Ops:
  0.7 4.8 %pack.1 = (f32[32,64,128]{2,1,0:T(8,128)}, f32[32,64,128]{2,1,0:T(8,128)}) custom-call(s32[128]{0:T(128)} %label_ref.1, s32[1]{0:T(128)S(6)} %copy.12.live_ref, f32[3,128,128]{2,1,0:T(8,128)} %bitcast.41, f32[128,4,128]{2,1,0:T(4,128)} %waves_ref.1), custom_call_target="tpu_custom_call" | custom-call | tf_op jit(solution)/shard_map/pack/pallas_call | solution.py:74
  5.5 22.3 %all_to_all.10.x_ref = f32[32,64,128]{2,1,0:T(8,128)S(1)} all-to-all(f32[32,64,128]{2,1,0:T(8,128)} %get-tuple-element.8), channel_id=1, replica_groups=mesh['work'=32,'tile'=8] {'work'}, dimensions={0} | all-to-all | bytes 2097152 | tf_op jit(solution)/shard_map/all_to_all | solution.py:366
  27.8 6.2 %all-to-all-start = ((f32[32,64,128]{2,1,0:T(8,128)}), f32[32,64,128]{2,1,0:T(8,128)S(1)}, u32[]{:S(2)}, u32[]{:S(2)}) async-start(f32[32,64,128]{2,1,0:T(8,128)} %get-tuple-element.7), calls=%async_computation | async-start | bytes 2097152 | tf_op jit(solution)/shard_map/all_to_all | solution.py:366
  34.1 0.1 copy.11
  34.3 0.1 sub.23.label_ref
  34.4 14.6 %all-to-all-done.x_ref = f32[32,64,128]{2,1,0:T(8,128)S(1)} async-done(((f32[32,64,128]{2,1,0:T(8,128)}), f32[32,64,128]{2,1,0:T(8,128)S(1)}, u32[]{:S(2)}, u32[]{:S(2)}) %all-to-all-start) | async-done | bytes 1048608 | tf_op jit(solution)/shard_map/all_to_all | solution.py:366
  49.0 0.1 sub.19.label_ref
  49.1 0.6 copy-done.1
  49.7 14.6 %shard_map.82.prior_ref = f32[2,16,64,64]{3,2,1,0:T(8,128)S(1)} custom-call(s32[256]{0:T(256)S(1)} %sub.23.label_ref, f32[2]{0:T(128)S(1)} %copy-done.1, f32[32,64,128]{2,1,0:T(8,128)S(1)} %all_to_all.10.x_ref), custom_call_target="tpu_custom_call" | custom-call | flops 1610612736 | bytes 1572864 | tf_op jit(solution)/shard_map/pallas_call | solution.py:315
  64.4 9.4 %shard_map.83 = f32[8,4,64,128]{3,2,1,0:T(8,128)S(1)} custom-call(s32[256]{0:T(256)S(1)} %sub.19.label_ref, f32[2]{0:T(128)S(1)} %copy-done.1, s32[16,2]{1,0:T(8,128)S(1)} %broadcast_subtract_fusion.corner_ref, s32[1]{0:T(128)} %bitcast.2.tile_ref, f32[32,64,128]{2,1,0:T(8,128)S(1)} %all-to-all-done.x_ref, f32[2,16,64,64]{3,2,1,0:T(8,128)S(1)} %shard_map.82.prior_ref, ...), custom_call_target="tpu_custom_call" | custom-call | flops 1610612736 | bytes 2097152 | tf_op jit(solution)/shard_map/pallas_call | solution.py:315
  73.8 10.2 %collective-permute-start = (f32[2,64,128]{2,1,0:T(8,128)S(1)}, f32[2,64,128]{2,1,0:T(8,128)S(1)}, u32[]{:S(2)}, u32[]{:S(2)}) collective-permute-start(f32[2,64,128]{2,1,0:T(8,128)S(1)} %get-tuple-element.13), channel_id=1, source_target_pairs={{0,1},{1,2},{2,3},{3,4},{4,5},{5,6},{6,7},{7,0},{8,9},{9,10},{10,1... | collective-permute-start | bytes 196616 | tf_op jit(solution)/shard_map/ppermute | solution.py:342
  84.0 2.0 %collective-permute-done = f32[2,64,128]{2,1,0:T(8,128)S(1)} collective-permute-done((f32[2,64,128]{2,1,0:T(8,128)S(1)}, f32[2,64,128]{2,1,0:T(8,128)S(1)}, u32[]{:S(2)}, u32[]{:S(2)}) %collective-permute-start) | collective-permute-done | bytes 65568 | tf_op jit(solution)/shard_map/ppermute | solution.py:342
  86.0 3.5 %collective-permute-done.4 = f32[2,64,128]{2,1,0:T(8,128)S(1)} collective-permute-done((f32[2,64,128]{2,1,0:T(8,128)S(1)}, f32[2,64,128]{2,1,0:T(8,128)S(1)}, u32[]{:S(2)}, u32[]{:S(2)}) %collective-permute-start.4) | collective-permute-done | bytes 65568 | tf_op jit(solution)/shard_map/ppermute | solution.py:343
  89.5 0.3 collective-permute-start.1
  89.8 1.9 %collective-permute-start.5 = (f32[4,64,128]{2,1,0:T(8,128)S(1)}, f32[4,64,128]{2,1,0:T(8,128)S(1)}, u32[]{:S(2)}, u32[]{:S(2)}) collective-permute-start(f32[4,64,128]{2,1,0:T(8,128)S(1)} %pad_maximum_fusion.1), channel_id=1, source_target_pairs={{0,7},{1,0},{2,1},{3,2},{4,3},{5,4},{6,5},{7,6},{8,15},{9,8},{10,9... | collective-permute-start | bytes 393224 | tf_op jit(solution)/shard_map/ppermute | solution.py:352
  91.7 2.9 %collective-permute-done.1 = f32[4,64,128]{2,1,0:T(8,128)S(1)} collective-permute-done((f32[4,64,128]{2,1,0:T(8,128)S(1)}, f32[4,64,128]{2,1,0:T(8,128)S(1)}, u32[]{:S(2)}, u32[]{:S(2)}) %collective-permute-start.1) | collective-permute-done | bytes 131104 | tf_op jit(solution)/shard_map/ppermute | solution.py:351
  94.6 1.5 %collective-permute-start.2 = (f32[4,64,128]{2,1,0:T(8,128)S(1)}, f32[4,64,128]{2,1,0:T(8,128)S(1)}, u32[]{:S(2)}, u32[]{:S(2)}) collective-permute-start(f32[4,64,128]{2,1,0:T(8,128)S(1)} %fusion.2), channel_id=1, source_target_pairs={{0,1},{1,2},{2,3},{3,4},{4,5},{5,6},{6,7},{7,0},{8,9},{9,10},{10,1... | collective-permute-start | bytes 393224 | tf_op jit(solution)/shard_map/ppermute | solution.py:351
  96.0 3.6 %collective-permute-done.2 = f32[4,64,128]{2,1,0:T(8,128)S(1)} collective-permute-done((f32[4,64,128]{2,1,0:T(8,128)S(1)}, f32[4,64,128]{2,1,0:T(8,128)S(1)}, u32[]{:S(2)}, u32[]{:S(2)}) %collective-permute-start.2) | collective-permute-done | bytes 131104 | tf_op jit(solution)/shard_map/ppermute | solution.py:351
  99.6 0.1 collective-permute-start.6
  99.7 3.2 %collective-permute-start.3 = (f32[4,64,128]{2,1,0:T(8,128)S(1)}, f32[4,64,128]{2,1,0:T(8,128)S(1)}, u32[]{:S(2)}, u32[]{:S(2)}) collective-permute-start(f32[4,64,128]{2,1,0:T(8,128)S(1)} %get-tuple-element.9), channel_id=1, source_target_pairs={{0,1},{1,2},{2,3},{3,4},{4,5},{5,6},{6,7},{7,0},{8,9},{9,10},{10,1... | collective-permute-start | bytes 393224 | tf_op jit(solution)/shard_map/ppermute | solution.py:351
  102.9 2.9 %collective-permute-done.6 = f32[4,64,128]{2,1,0:T(8,128)S(1)} collective-permute-done((f32[4,64,128]{2,1,0:T(8,128)S(1)}, f32[4,64,128]{2,1,0:T(8,128)S(1)}, u32[]{:S(2)}, u32[]{:S(2)}) %collective-permute-start.6) | collective-permute-done | bytes 131104 | tf_op jit(solution)/shard_map/ppermute | solution.py:352
  105.9 0.1 collective-permute-start.7
  106.0 6.2 %collective-permute-done.7 = f32[4,64,128]{2,1,0:T(8,128)S(1)} collective-permute-done((f32[4,64,128]{2,1,0:T(8,128)S(1)}, f32[4,64,128]{2,1,0:T(8,128)S(1)}, u32[]{:S(2)}, u32[]{:S(2)}) %collective-permute-start.7) | collective-permute-done | bytes 131104 | tf_op jit(solution)/shard_map/ppermute | solution.py:352
  112.2 0.7 fusion.5
  (22 shorter events, 0.4 us)
Async XLA Ops:
  0.0 34.0 %copy-start = (s32[512,2]{0,1:T(2,128)S(1)}, s32[512,2]{0,1:T(2,128)}, u32[]{:S(2)}) copy-start(s32[512,2]{0,1:T(2,128)} %param.12) | copy-start | bytes 12292
  27.8 21.1 %all-to-all-start = ((f32[32,64,128]{2,1,0:T(8,128)}), f32[32,64,128]{2,1,0:T(8,128)S(1)}, u32[]{:S(2)}, u32[]{:S(2)}) async-start(f32[32,64,128]{2,1,0:T(8,128)} %get-tuple-element.7), calls=%async_computation | async-start | bytes 2097152 | tf_op jit(solution)/shard_map/all_to_all | solution.py:366
  49.0 0.7 copy-start.1
  49.7 14.7 %copy-start.2 = (f32[64,256]{1,0:T(8,128)S(1)}, f32[64,256]{1,0:T(8,128)}, u32[]{:S(2)}) copy-start(f32[64,256]{1,0:T(8,128)} %constant.28.clone.spread_ref) | copy-start | bytes 196612
  49.7 14.7 %copy-start.3 = (f32[64,64]{1,0:T(8,128)S(1)}, f32[64,64]{1,0:T(8,128)}, u32[]{:S(2)}) copy-start(f32[64,64]{1,0:T(8,128)} %constant.27.clone.mix_ref) | copy-start | bytes 49156
  73.8 12.2 %collective-permute-start = (f32[2,64,128]{2,1,0:T(8,128)S(1)}, f32[2,64,128]{2,1,0:T(8,128)S(1)}, u32[]{:S(2)}, u32[]{:S(2)}) collective-permute-start(f32[2,64,128]{2,1,0:T(8,128)S(1)} %get-tuple-element.13), channel_id=1, source_target_pairs={{0,1},{1,2},{2,3},{3,4},{4,5},{5,6},{6,7},{7,0},{8,9},{9,10},{10,1... | collective-permute-start | bytes 196616 | tf_op jit(solution)/shard_map/ppermute | solution.py:342
  84.0 5.5 %collective-permute-start.4 = (f32[2,64,128]{2,1,0:T(8,128)S(1)}, f32[2,64,128]{2,1,0:T(8,128)S(1)}, u32[]{:S(2)}, u32[]{:S(2)}) collective-permute-start(f32[2,64,128]{2,1,0:T(8,128)S(1)} %get-tuple-element.14), channel_id=1, source_target_pairs={{0,7},{1,0},{2,1},{3,2},{4,3},{5,4},{6,5},{7,6},{8,15},{9,8},{10,9... | collective-permute-start | bytes 196616 | tf_op jit(solution)/shard_map/ppermute | solution.py:343
  89.5 5.0 %collective-permute-start.1 = (f32[4,64,128]{2,1,0:T(8,128)S(1)}, f32[4,64,128]{2,1,0:T(8,128)S(1)}, u32[]{:S(2)}, u32[]{:S(2)}) collective-permute-start(f32[4,64,128]{2,1,0:T(8,128)S(1)} %pad_maximum_fusion), channel_id=1, source_target_pairs={{0,1},{1,2},{2,3},{3,4},{4,5},{5,6},{6,7},{7,0},{8,9},{9,10},{10,1... | collective-permute-start | bytes 393224 | tf_op jit(solution)/shard_map/ppermute | solution.py:351
  89.8 6.3 %collective-permute-start.5 = (f32[4,64,128]{2,1,0:T(8,128)S(1)}, f32[4,64,128]{2,1,0:T(8,128)S(1)}, u32[]{:S(2)}, u32[]{:S(2)}) collective-permute-start(f32[4,64,128]{2,1,0:T(8,128)S(1)} %pad_maximum_fusion.1), channel_id=1, source_target_pairs={{0,7},{1,0},{2,1},{3,2},{4,3},{5,4},{6,5},{7,6},{8,15},{9,8},{10,9... | collective-permute-start | bytes 393224 | tf_op jit(solution)/shard_map/ppermute | solution.py:352
  94.6 5.0 %collective-permute-start.2 = (f32[4,64,128]{2,1,0:T(8,128)S(1)}, f32[4,64,128]{2,1,0:T(8,128)S(1)}, u32[]{:S(2)}, u32[]{:S(2)}) collective-permute-start(f32[4,64,128]{2,1,0:T(8,128)S(1)} %fusion.2), channel_id=1, source_target_pairs={{0,1},{1,2},{2,3},{3,4},{4,5},{5,6},{6,7},{7,0},{8,9},{9,10},{10,1... | collective-permute-start | bytes 393224 | tf_op jit(solution)/shard_map/ppermute | solution.py:351
  99.6 6.3 %collective-permute-start.6 = (f32[4,64,128]{2,1,0:T(8,128)S(1)}, f32[4,64,128]{2,1,0:T(8,128)S(1)}, u32[]{:S(2)}, u32[]{:S(2)}) collective-permute-start(f32[4,64,128]{2,1,0:T(8,128)S(1)} %get-tuple-element.10), channel_id=1, source_target_pairs={{0,7},{1,0},{2,1},{3,2},{4,3},{5,4},{6,5},{7,6},{8,15},{9,8},{10,9... | collective-permute-start | bytes 393224 | tf_op jit(solution)/shard_map/ppermute | solution.py:352
  99.7 6.3 %collective-permute-start.3 = (f32[4,64,128]{2,1,0:T(8,128)S(1)}, f32[4,64,128]{2,1,0:T(8,128)S(1)}, u32[]{:S(2)}, u32[]{:S(2)}) collective-permute-start(f32[4,64,128]{2,1,0:T(8,128)S(1)} %get-tuple-element.9), channel_id=1, source_target_pairs={{0,1},{1,2},{2,3},{3,4},{4,5},{5,6},{6,7},{7,0},{8,9},{9,10},{10,1... | collective-permute-start | bytes 393224 | tf_op jit(solution)/shard_map/ppermute | solution.py:351
  105.9 6.3 %collective-permute-start.7 = (f32[4,64,128]{2,1,0:T(8,128)S(1)}, f32[4,64,128]{2,1,0:T(8,128)S(1)}, u32[]{:S(2)}, u32[]{:S(2)}) collective-permute-start(f32[4,64,128]{2,1,0:T(8,128)S(1)} %fusion.1), channel_id=1, source_target_pairs={{0,7},{1,0},{2,1},{3,2},{4,3},{5,4},{6,5},{7,6},{8,15},{9,8},{10,9... | collective-permute-start | bytes 393224 | tf_op jit(solution)/shard_map/ppermute | solution.py:352

commit v7 on v6

--- a/solution.py
+++ b/solution.py
@@ -20,15 +20,14 @@
 FIELDS = 3 + 2 * CH
 TERMS = 4 * HALF
 GROUP = 8
-SPAN = 4
+SPAN = 8
 CHUNKS = SUBW // GROUP
 UNROLL = 8
 
 
-def pack_kernel(label_ref, live_ref, coords_ref, waves_ref, *refs):
-    out_refs, (room, count_ref) = refs[:CHUNKS], refs[CHUNKS:]
-    workers = room.shape[1]
-    room[...] = jnp.zeros_like(room)
+def pack_kernel(chunk, label_ref, live_ref, coords_ref, waves_ref, out_ref, count_ref):
+    workers = out_ref.shape[0]
+    out_ref[...] = jnp.zeros_like(out_ref)
 
     def clear(worker, carry):
         count_ref[worker] = 0
@@ -43,44 +42,42 @@
             block = group * UNROLL + offset
             label = label_ref[block]
             worker = label // SUBW
-            count = count_ref[worker]
-            count_ref[worker] = count + 1
-            chunk, slot = count // GROUP, count % GROUP
-            kept = jnp.where(block < live, 1.0, 0.0)
-            for field in range(3):
-                room[chunk, worker, pl.ds(field * GROUP + slot, 1), :] = coords_ref[
-                    field, pl.ds(block, 1), :
-                ]
-            for field in range(2 * CH):
-                room[chunk, worker, pl.ds((3 + field) * GROUP + slot, 1), :] = (
-                    waves_ref[block, pl.ds(field, 1), :] * kept
-                )
-            row = pl.ds(FIELDS * GROUP, 1)
-            inside = (label - worker * SUBW + 1).astype(jnp.float32) * kept
-            room[chunk, worker, row, :] = jnp.where(
-                lane == slot, inside, room[chunk, worker, row, :]
-            )
+            slot = count_ref[worker] - chunk * GROUP
+            count_ref[worker] = slot + chunk * GROUP + 1
+
+            @pl.when((slot >= 0) & (slot < GROUP) & (block < live))
+            def _():
+                for field in range(3):
+                    out_ref[worker, pl.ds(field * GROUP + slot, 1), :] = coords_ref[
+                        field, pl.ds(block, 1), :
+                    ]
+                for field in range(2 * CH):
+                    out_ref[worker, pl.ds((3 + field) * GROUP + slot, 1), :] = waves_ref[
+                        block, pl.ds(field, 1), :
+                    ]
+                row = pl.ds(FIELDS * GROUP, 1)
+                inside = (label - worker * SUBW + 1).astype(jnp.float32)
+                out_ref[worker, row, :] = jnp.where(lane == slot, inside, out_ref[worker, row, :])
+
         return carry
 
     lax.fori_loop(0, label_ref.shape[0] // UNROLL, move, 0)
-    for chunk in range(CHUNKS):
-        out_refs[chunk][...] = room[chunk]
-
-
-def pack(labels, live, coords, waves, workers):
+
+
+def pack(chunk, labels, live, coords, waves, workers):
     smem = pl.BlockSpec(memory_space=pltpu.SMEM)
     vmem = pl.BlockSpec(memory_space=pltpu.VMEM)
     shape = (workers, (FIELDS + 1) * GROUP, ROWS)
     return pl.pallas_call(
-        pack_kernel,
+        functools.partial(pack_kernel, chunk),
         name="pack",
-        out_shape=[jax.ShapeDtypeStruct(shape, jnp.float32)] * CHUNKS,
+        out_shape=jax.ShapeDtypeStruct(shape, jnp.float32),
         in_specs=[smem, smem, vmem, vmem],
-        out_specs=[vmem] * CHUNKS,
-        scratch_shapes=[
-            pltpu.VMEM((CHUNKS,) + shape, jnp.float32),
-            pltpu.SMEM((workers,), jnp.int32),
-        ],
+        out_specs=vmem,
+        scratch_shapes=[pltpu.SMEM((workers,), jnp.int32)],
+        cost_estimate=pl.CostEstimate(
+            flops=0, bytes_accessed=4 * math.prod(shape), transcendentals=0
+        ),
     )(labels, live, coords, waves)
 
 
@@ -324,7 +321,7 @@
             scratch_shapes=[pltpu.VMEM(shape, jnp.float32) for shape in [ROOM, ROOM] + scratch],
         ),
         compiler_params=pltpu.CompilerParams(
-            dimension_semantics=("arbitrary",), vmem_limit_bytes=28 << 20
+            dimension_semantics=("arbitrary",), vmem_limit_bytes=36 << 20
         ),
         cost_estimate=pl.CostEstimate(
             flops=3 * 2 * CH * sources * GROUP * TERMS * TERMS * ROWS,
@@ -358,12 +355,14 @@
     tiles = lax.axis_size("tile")
     worker = lax.axis_index("work")
     coords = jnp.swapaxes(block_coords, 0, 1)
-    packed = pack(subgrid_of_block, live_blocks, coords, block_visibilities, workers)
     local_corners = lax.dynamic_slice_in_dim(corners, worker * SUBW, SUBW, 0)
     local_corners = local_corners - jnp.stack([0 * worker, worker * GCW])[None, :]
     sums = None
     for chunk in range(CHUNKS):
-        arrived = lax.all_to_all(packed[chunk], "work", split_axis=0, concat_axis=0, tiled=True)
+        packed = pack(
+            chunk, subgrid_of_block, live_blocks, coords, block_visibilities, workers
+        )
+        arrived = lax.all_to_all(packed, "work", split_axis=0, concat_axis=0, tiled=True)
         labels = arrived[:, FIELDS * GROUP, :GROUP].astype(jnp.int32).reshape(workers * GROUP) - 1
         if chunk == 0:
             sums = chunk_call(first_kernel, (labels, channel_scale), arrived, (), SUMS, [])

time: 113 us -> 114 us (level)
  the two profiles are of different devices: /device:TPU:120 before, /device:TPU:2 now
where the time goes in v7:
time: 114 us
  waiting for transfers between devices  43.8 us (38%)
  Pallas kernels  37 us (32%)
  starting transfers between devices  30.4 us (27%)
    pallas_call x2, Pallas kernels, chunk_call(): pl.pallas_call(kernel, out_shape=jax.ShapeDtypeStruct(out_shape, jnp.floa...  26.7 us
    all_to_all x2, waiting for transfers between devices, local(): lax.all_to_all(packed, 'work', split_axis=0, concat_axis=0, tiled=True)  26.6 us
    all_to_all x2, starting transfers between devices, local(): lax.all_to_all(packed, 'work', split_axis=0, concat_axis=0, tiled=True)  12.6 us
    pallas_call x2, Pallas kernels, pack(): pl.pallas_call(functools.partial(pack_kernel, chunk), name='pack', out_sh...  10.3 us
    ppermute x3, waiting for transfers between devices, summed_around(): rising = lax.ppermute(rising, axis, up)  8.81 us
    ppermute x3, starting transfers between devices, summed_around(): falling = lax.ppermute(falling, axis, down)  6.92 us
    ppermute x3, waiting for transfers between devices, summed_around(): falling = lax.ppermute(falling, axis, down)  5.89 us
    ppermute x1, starting transfers between devices, summed_around(): rising = lax.ppermute(parts[far, :CH], axis, up)  5.36 us
  transfers between devices with their start and end apart: 10, of which 8 were waited for; matrix products, arithmetic and copies ran while one was open for 0% of the time, Pallas kernels for 4%

profile of v7, /device:TPU:2, one launch (start us, length us, event | category | flops | bytes accessed | tf_op | source)
XLA Modules:
  0.0 113.9 jit_solution(7690238271577952888)
XLA Ops:
  0.7 5.3 %pack.3 = f32[32,64,128]{2,1,0:T(8,128)} custom-call(s32[128]{0:T(128)} %label_ref.3, s32[1]{0:T(128)S(6)} %copy.12.live_ref, f32[3,128,128]{2,1,0:T(8,128)} %bitcast.41, f32[128,4,128]{2,1,0:T(4,128)} %waves_ref.3), custom_call_target="tpu_custom_call" | custom-call | bytes 1048576 | tf_op jit(solution)/shard_map/pack/pallas_call | solution.py:71
  5.9 7.6 %all-to-all-start.1 = ((f32[32,64,128]{2,1,0:T(8,128)}), f32[32,64,128]{2,1,0:T(8,128)S(1)}, u32[]{:S(2)}, u32[]{:S(2)}) async-start(f32[32,64,128]{2,1,0:T(8,128)} %pack.3), calls=%async_computation.1 | async-start | bytes 2097152 | tf_op jit(solution)/shard_map/all_to_all | solution.py:365
  13.5 5.0 %pack.2 = f32[32,64,128]{2,1,0:T(8,128)} custom-call(s32[128]{0:T(128)} %label_ref.3, s32[1]{0:T(128)S(6)} %copy.12.live_ref, f32[3,128,128]{2,1,0:T(8,128)} %bitcast.42, f32[128,4,128]{2,1,0:T(4,128)} %waves_ref.3), custom_call_target="tpu_custom_call" | custom-call | bytes 1048576 | tf_op jit(solution)/shard_map/pack/pallas_call | solution.py:71
  18.6 11.0 %all-to-all-done.1.x_ref = f32[32,64,128]{2,1,0:T(8,128)S(1)} async-done(((f32[32,64,128]{2,1,0:T(8,128)}), f32[32,64,128]{2,1,0:T(8,128)S(1)}, u32[]{:S(2)}, u32[]{:S(2)}) %all-to-all-start.1) | async-done | bytes 1048608 | tf_op jit(solution)/shard_map/all_to_all | solution.py:365
  29.5 5.0 %all-to-all-start = ((f32[32,64,128]{2,1,0:T(8,128)}), f32[32,64,128]{2,1,0:T(8,128)S(1)}, u32[]{:S(2)}, u32[]{:S(2)}) async-start(f32[32,64,128]{2,1,0:T(8,128)} %pack.2), calls=%async_computation | async-start | bytes 2097152 | tf_op jit(solution)/shard_map/all_to_all | solution.py:365
  34.7 0.1 copy.11
  35.0 15.7 %all-to-all-done.x_ref = f32[32,64,128]{2,1,0:T(8,128)S(1)} async-done(((f32[32,64,128]{2,1,0:T(8,128)}), f32[32,64,128]{2,1,0:T(8,128)S(1)}, u32[]{:S(2)}, u32[]{:S(2)}) %all-to-all-start) | async-done | bytes 1048608 | tf_op jit(solution)/shard_map/all_to_all | solution.py:365
  50.8 0.1 sub.19.label_ref
  50.8 0.6 copy-done.1
  51.4 14.2 %shard_map.82.prior_ref = f32[2,16,64,64]{3,2,1,0:T(8,128)S(1)} custom-call(s32[256]{0:T(256)S(1)} %sub.23.label_ref, f32[2]{0:T(128)S(1)} %copy-done.1, f32[32,64,128]{2,1,0:T(8,128)S(1)} %all-to-all-done.1.x_ref), custom_call_target="tpu_custom_call" | custom-call | flops 1610612736 | bytes 1572864 | tf_op jit(solution)/shard_map/pallas_call | solution.py:312
  65.7 12.4 %shard_map.83 = f32[8,4,64,128]{3,2,1,0:T(8,128)S(1)} custom-call(s32[256]{0:T(256)S(1)} %sub.19.label_ref, f32[2]{0:T(128)S(1)} %copy-done.1, s32[16,2]{1,0:T(8,128)S(1)} %broadcast_subtract_fusion.corner_ref, s32[1]{0:T(128)} %bitcast.2.tile_ref, f32[32,64,128]{2,1,0:T(8,128)S(1)} %all-to-all-done.x_ref, f32[2,16,64,64]{3,2,1,0:T(8,128)S(1)} %shard_map.82.prior_ref, ...), custom_call_target="tpu_custom_call" | custom-call | flops 1610612736 | bytes 2097152 | tf_op jit(solution)/shard_map/pallas_call | solution.py:312
  78.2 5.4 %collective-permute-start = (f32[2,64,128]{2,1,0:T(8,128)S(1)}, f32[2,64,128]{2,1,0:T(8,128)S(1)}, u32[]{:S(2)}, u32[]{:S(2)}) collective-permute-start(f32[2,64,128]{2,1,0:T(8,128)S(1)} %get-tuple-element.9), channel_id=1, source_target_pairs={{0,1},{1,2},{2,3},{3,4},{4,5},{5,6},{6,7},{7,0},{8,9},{9,10},{10,1... | collective-permute-start | bytes 196616 | tf_op jit(solution)/shard_map/ppermute | solution.py:339
  83.5 4.0 %collective-permute-start.4 = (f32[2,64,128]{2,1,0:T(8,128)S(1)}, f32[2,64,128]{2,1,0:T(8,128)S(1)}, u32[]{:S(2)}, u32[]{:S(2)}) collective-permute-start(f32[2,64,128]{2,1,0:T(8,128)S(1)} %get-tuple-element.10), channel_id=1, source_target_pairs={{0,7},{1,0},{2,1},{3,2},{4,3},{5,4},{6,5},{7,6},{8,15},{9,8},{10,9... | collective-permute-start | bytes 196616 | tf_op jit(solution)/shard_map/ppermute | solution.py:340
  87.6 2.2 %collective-permute-done = f32[2,64,128]{2,1,0:T(8,128)S(1)} collective-permute-done((f32[2,64,128]{2,1,0:T(8,128)S(1)}, f32[2,64,128]{2,1,0:T(8,128)S(1)}, u32[]{:S(2)}, u32[]{:S(2)}) %collective-permute-start) | collective-permute-done | bytes 65568 | tf_op jit(solution)/shard_map/ppermute | solution.py:339
  89.7 0.3 collective-permute-done.4
  90.2 3.9 %collective-permute-start.5 = (f32[4,64,128]{2,1,0:T(8,128)S(1)}, f32[4,64,128]{2,1,0:T(8,128)S(1)}, u32[]{:S(2)}, u32[]{:S(2)}) collective-permute-start(f32[4,64,128]{2,1,0:T(8,128)S(1)} %pad_maximum_fusion.1), channel_id=1, source_target_pairs={{0,7},{1,0},{2,1},{3,2},{4,3},{5,4},{6,5},{7,6},{8,15},{9,8},{10,9... | collective-permute-start | bytes 393224 | tf_op jit(solution)/shard_map/ppermute | solution.py:349
  94.1 2.7 %collective-permute-done.1 = f32[4,64,128]{2,1,0:T(8,128)S(1)} collective-permute-done((f32[4,64,128]{2,1,0:T(8,128)S(1)}, f32[4,64,128]{2,1,0:T(8,128)S(1)}, u32[]{:S(2)}, u32[]{:S(2)}) %collective-permute-start.1) | collective-permute-done | bytes 131104 | tf_op jit(solution)/shard_map/ppermute | solution.py:348
  96.9 6.2 %collective-permute-done.2 = f32[4,64,128]{2,1,0:T(8,128)S(1)} collective-permute-done((f32[4,64,128]{2,1,0:T(8,128)S(1)}, f32[4,64,128]{2,1,0:T(8,128)S(1)}, u32[]{:S(2)}, u32[]{:S(2)}) %collective-permute-start.2) | collective-permute-done | bytes 131104 | tf_op jit(solution)/shard_map/ppermute | solution.py:348
  103.1 0.9 collective-permute-start.6
  104.0 1.2 %collective-permute-start.3 = (f32[4,64,128]{2,1,0:T(8,128)S(1)}, f32[4,64,128]{2,1,0:T(8,128)S(1)}, u32[]{:S(2)}, u32[]{:S(2)}) collective-permute-start(f32[4,64,128]{2,1,0:T(8,128)S(1)} %get-tuple-element.5), channel_id=1, source_target_pairs={{0,1},{1,2},{2,3},{3,4},{4,5},{5,6},{6,7},{7,0},{8,9},{9,10},{10,1... | collective-permute-start | bytes 393224 | tf_op jit(solution)/shard_map/ppermute | solution.py:348
  105.2 2.9 %collective-permute-done.6 = f32[4,64,128]{2,1,0:T(8,128)S(1)} collective-permute-done((f32[4,64,128]{2,1,0:T(8,128)S(1)}, f32[4,64,128]{2,1,0:T(8,128)S(1)}, u32[]{:S(2)}, u32[]{:S(2)}) %collective-permute-start.6) | collective-permute-done | bytes 131104 | tf_op jit(solution)/shard_map/ppermute | solution.py:349
  108.2 2.1 %collective-permute-start.7 = (f32[4,64,128]{2,1,0:T(8,128)S(1)}, f32[4,64,128]{2,1,0:T(8,128)S(1)}, u32[]{:S(2)}, u32[]{:S(2)}) collective-permute-start(f32[4,64,128]{2,1,0:T(8,128)S(1)} %fusion.1), channel_id=1, source_target_pairs={{0,7},{1,0},{2,1},{3,2},{4,3},{5,4},{6,5},{7,6},{8,15},{9,8},{10,9... | collective-permute-start | bytes 393224 | tf_op jit(solution)/shard_map/ppermute | solution.py:349
  110.3 2.9 %collective-permute-done.7 = f32[4,64,128]{2,1,0:T(8,128)S(1)} collective-permute-done((f32[4,64,128]{2,1,0:T(8,128)S(1)}, f32[4,64,128]{2,1,0:T(8,128)S(1)}, u32[]{:S(2)}, u32[]{:S(2)}) %collective-permute-start.7) | collective-permute-done | bytes 131104 | tf_op jit(solution)/shard_map/ppermute | solution.py:349
  113.2 0.7 fusion.5
  (24 shorter events, 0.7 us)
Async XLA Ops:
  0.0 34.6 %copy-start = (s32[512,2]{0,1:T(2,128)S(1)}, s32[512,2]{0,1:T(2,128)}, u32[]{:S(2)}) copy-start(s32[512,2]{0,1:T(2,128)} %param.12) | copy-start | bytes 12292
  5.9 23.6 %all-to-all-start.1 = ((f32[32,64,128]{2,1,0:T(8,128)}), f32[32,64,128]{2,1,0:T(8,128)S(1)}, u32[]{:S(2)}, u32[]{:S(2)}) async-start(f32[32,64,128]{2,1,0:T(8,128)} %pack.3), calls=%async_computation.1 | async-start | bytes 2097152 | tf_op jit(solution)/shard_map/all_to_all | solution.py:365
  29.5 21.1 %all-to-all-start = ((f32[32,64,128]{2,1,0:T(8,128)}), f32[32,64,128]{2,1,0:T(8,128)S(1)}, u32[]{:S(2)}, u32[]{:S(2)}) async-start(f32[32,64,128]{2,1,0:T(8,128)} %pack.2), calls=%async_computation | async-start | bytes 2097152 | tf_op jit(solution)/shard_map/all_to_all | solution.py:365
  50.7 0.7 copy-start.1
  51.4 14.3 %copy-start.2 = (f32[64,256]{1,0:T(8,128)S(1)}, f32[64,256]{1,0:T(8,128)}, u32[]{:S(2)}) copy-start(f32[64,256]{1,0:T(8,128)} %constant.28.clone.spread_ref) | copy-start | bytes 196612
  51.4 14.3 %copy-start.3 = (f32[64,64]{1,0:T(8,128)S(1)}, f32[64,64]{1,0:T(8,128)}, u32[]{:S(2)}) copy-start(f32[64,64]{1,0:T(8,128)} %constant.27.clone.mix_ref) | copy-start | bytes 49156
  78.2 11.6 %collective-permute-start = (f32[2,64,128]{2,1,0:T(8,128)S(1)}, f32[2,64,128]{2,1,0:T(8,128)S(1)}, u32[]{:S(2)}, u32[]{:S(2)}) collective-permute-start(f32[2,64,128]{2,1,0:T(8,128)S(1)} %get-tuple-element.9), channel_id=1, source_target_pairs={{0,1},{1,2},{2,3},{3,4},{4,5},{5,6},{6,7},{7,0},{8,9},{9,10},{10,1... | collective-permute-start | bytes 196616 | tf_op jit(solution)/shard_map/ppermute | solution.py:339
  83.5 6.5 %collective-permute-start.4 = (f32[2,64,128]{2,1,0:T(8,128)S(1)}, f32[2,64,128]{2,1,0:T(8,128)S(1)}, u32[]{:S(2)}, u32[]{:S(2)}) collective-permute-start(f32[2,64,128]{2,1,0:T(8,128)S(1)} %get-tuple-element.10), channel_id=1, source_target_pairs={{0,7},{1,0},{2,1},{3,2},{4,3},{5,4},{6,5},{7,6},{8,15},{9,8},{10,9... | collective-permute-start | bytes 196616 | tf_op jit(solution)/shard_map/ppermute | solution.py:340
  90.1 6.7 %collective-permute-start.1 = (f32[4,64,128]{2,1,0:T(8,128)S(1)}, f32[4,64,128]{2,1,0:T(8,128)S(1)}, u32[]{:S(2)}, u32[]{:S(2)}) collective-permute-start(f32[4,64,128]{2,1,0:T(8,128)S(1)} %pad_maximum_fusion), channel_id=1, source_target_pairs={{0,1},{1,2},{2,3},{3,4},{4,5},{5,6},{6,7},{7,0},{8,9},{9,10},{10,1... | collective-permute-start | bytes 393224 | tf_op jit(solution)/shard_map/ppermute | solution.py:348
  90.2 6.7 %collective-permute-start.5 = (f32[4,64,128]{2,1,0:T(8,128)S(1)}, f32[4,64,128]{2,1,0:T(8,128)S(1)}, u32[]{:S(2)}, u32[]{:S(2)}) collective-permute-start(f32[4,64,128]{2,1,0:T(8,128)S(1)} %pad_maximum_fusion.1), channel_id=1, source_target_pairs={{0,7},{1,0},{2,1},{3,2},{4,3},{5,4},{6,5},{7,6},{8,15},{9,8},{10,9... | collective-permute-start | bytes 393224 | tf_op jit(solution)/shard_map/ppermute | solution.py:349
  96.8 6.3 %collective-permute-start.2 = (f32[4,64,128]{2,1,0:T(8,128)S(1)}, f32[4,64,128]{2,1,0:T(8,128)S(1)}, u32[]{:S(2)}, u32[]{:S(2)}) collective-permute-start(f32[4,64,128]{2,1,0:T(8,128)S(1)} %fusion.2), channel_id=1, source_target_pairs={{0,1},{1,2},{2,3},{3,4},{4,5},{5,6},{6,7},{7,0},{8,9},{9,10},{10,1... | collective-permute-start | bytes 393224 | tf_op jit(solution)/shard_map/ppermute | solution.py:348
  103.1 5.0 %collective-permute-start.6 = (f32[4,64,128]{2,1,0:T(8,128)S(1)}, f32[4,64,128]{2,1,0:T(8,128)S(1)}, u32[]{:S(2)}, u32[]{:S(2)}) collective-permute-start(f32[4,64,128]{2,1,0:T(8,128)S(1)} %get-tuple-element.6), channel_id=1, source_target_pairs={{0,7},{1,0},{2,1},{3,2},{4,3},{5,4},{6,5},{7,6},{8,15},{9,8},{10,9... | collective-permute-start | bytes 393224 | tf_op jit(solution)/shard_map/ppermute | solution.py:349
  104.0 6.3 %collective-permute-start.3 = (f32[4,64,128]{2,1,0:T(8,128)S(1)}, f32[4,64,128]{2,1,0:T(8,128)S(1)}, u32[]{:S(2)}, u32[]{:S(2)}) collective-permute-start(f32[4,64,128]{2,1,0:T(8,128)S(1)} %get-tuple-element.5), channel_id=1, source_target_pairs={{0,1},{1,2},{2,3},{3,4},{4,5},{5,6},{6,7},{7,0},{8,9},{9,10},{10,1... | collective-permute-start | bytes 393224 | tf_op jit(solution)/shard_map/ppermute | solution.py:348
  108.2 5.0 %collective-permute-start.7 = (f32[4,64,128]{2,1,0:T(8,128)S(1)}, f32[4,64,128]{2,1,0:T(8,128)S(1)}, u32[]{:S(2)}, u32[]{:S(2)}) collective-permute-start(f32[4,64,128]{2,1,0:T(8,128)S(1)} %fusion.1), channel_id=1, source_target_pairs={{0,7},{1,0},{2,1},{3,2},{4,3},{5,4},{6,5},{7,6},{8,15},{9,8},{10,9... | collective-permute-start | bytes 393224 | tf_op jit(solution)/shard_map/ppermute | solution.py:349

commit v8 on v7

--- a/solution.py
+++ b/solution.py
@@ -25,9 +25,9 @@
 UNROLL = 8
 
 
-def pack_kernel(chunk, label_ref, live_ref, coords_ref, waves_ref, out_ref, count_ref):
+def pack_kernel(chunk, label_ref, live_ref, coords_ref, waves_ref, out_ref, room, count_ref):
     workers = out_ref.shape[0]
-    out_ref[...] = jnp.zeros_like(out_ref)
+    room[...] = jnp.zeros_like(room)
 
     def clear(worker, carry):
         count_ref[worker] = 0
@@ -41,27 +41,25 @@
         for offset in range(UNROLL):
             block = group * UNROLL + offset
             label = label_ref[block]
-            worker = label // SUBW
-            slot = count_ref[worker] - chunk * GROUP
-            count_ref[worker] = slot + chunk * GROUP + 1
-
-            @pl.when((slot >= 0) & (slot < GROUP) & (block < live))
-            def _():
-                for field in range(3):
-                    out_ref[worker, pl.ds(field * GROUP + slot, 1), :] = coords_ref[
-                        field, pl.ds(block, 1), :
-                    ]
-                for field in range(2 * CH):
-                    out_ref[worker, pl.ds((3 + field) * GROUP + slot, 1), :] = waves_ref[
-                        block, pl.ds(field, 1), :
-                    ]
-                row = pl.ds(FIELDS * GROUP, 1)
-                inside = (label - worker * SUBW + 1).astype(jnp.float32)
-                out_ref[worker, row, :] = jnp.where(lane == slot, inside, out_ref[worker, row, :])
-
+            worker = label >> (SUBW.bit_length() - 1)
+            count = count_ref[worker]
+            count_ref[worker] = count + 1
+            inside = ((count >> (GROUP.bit_length() - 1)) == chunk) & (block < live)
+            place = jnp.where(inside, worker, workers)
+            slot = count & (GROUP - 1)
+            for field in range(FIELDS):
+                if field < 3:
+                    value = coords_ref[field, pl.ds(block, 1), :]
+                else:
+                    value = waves_ref[block, pl.ds(field - 3, 1), :]
+                room[place, pl.ds(field * GROUP + slot, 1), :] = value
+            row = pl.ds(FIELDS * GROUP, 1)
+            mark = ((label & (SUBW - 1)) + 1).astype(jnp.float32)
+            room[place, row, :] = jnp.where(lane == slot, mark, room[place, row, :])
         return carry
 
     lax.fori_loop(0, label_ref.shape[0] // UNROLL, move, 0)
+    out_ref[...] = room[:workers]
 
 
 def pack(chunk, labels, live, coords, waves, workers):
@@ -74,7 +72,10 @@
         out_shape=jax.ShapeDtypeStruct(shape, jnp.float32),
         in_specs=[smem, smem, vmem, vmem],
         out_specs=vmem,
-        scratch_shapes=[pltpu.SMEM((workers,), jnp.int32)],
+        scratch_shapes=[
+            pltpu.VMEM((workers + 1,) + shape[1:], jnp.float32),
+            pltpu.SMEM((workers,), jnp.int32),
+        ],
         cost_estimate=pl.CostEstimate(
             flops=0, bytes_accessed=4 * math.prod(shape), transcendentals=0
         ),

time: 114 us -> 112 us (0.982)
  Pallas kernels: 37 us -> 33.4 us
  waiting for transfers between devices: 43.8 us -> 45.5 us
    pallas_call x2, Pallas kernels: 10.3 us -> 6.73 us  [pack(): pl.pallas_call(functools.partial(pack_kernel, chunk), name='pack', out_sh...]
    all_to_all x2, waiting for transfers between devices: 26.6 us -> 28.3 us  [local(): lax.all_to_all(packed, 'work', split_axis=0, concat_axis=0, tiled=True)]
  transfers between devices with their start and end apart: 10 -> 10, of which waited for: 8 -> 8; matrix products, arithmetic and copies ran while one was open for 0% -> 0% of each run, Pallas kernels for 4% -> 3%
where the time goes in v8:
time: 112 us
  waiting for transfers between devices  45.5 us (41%)
  Pallas kernels  33.4 us (30%)
  starting transfers between devices  30.3 us (27%)
    all_to_all x2, waiting for transfers between devices, local(): lax.all_to_all(packed, 'work', split_axis=0, concat_axis=0, tiled=True)  28.3 us
    pallas_call x2, Pallas kernels, chunk_call(): pl.pallas_call(kernel, out_shape=jax.ShapeDtypeStruct(out_shape, jnp.floa...  26.7 us
    all_to_all x2, starting transfers between devices, local(): lax.all_to_all(packed, 'work', split_axis=0, concat_axis=0, tiled=True)  12.7 us
    ppermute x3, waiting for transfers between devices, summed_around(): rising = lax.ppermute(rising, axis, up)  8.81 us
    ppermute x3, starting transfers between devices, summed_around(): falling = lax.ppermute(falling, axis, down)  6.92 us
    pallas_call x2, Pallas kernels, pack(): pl.pallas_call(functools.partial(pack_kernel, chunk), name='pack', out_sh...  6.73 us
    ppermute x3, waiting for transfers between devices, summed_around(): falling = lax.ppermute(falling, axis, down)  5.89 us
    ppermute x1, starting transfers between devices, summed_around(): rising = lax.ppermute(parts[far, :CH], axis, up)  5.35 us
  transfers between devices with their start and end apart: 10, of which 8 were waited for; matrix products, arithmetic and copies ran while one was open for 0% of the time, Pallas kernels for 3%

profile of v8, /device:TPU:2, one launch (start us, length us, event | category | flops | bytes accessed | tf_op | source)
XLA Modules:
  0.0 112.0 jit_solution(17265630149399532780)
XLA Ops:
  0.7 3.4 %pack.3 = f32[32,64,128]{2,1,0:T(8,128)} custom-call(s32[128]{0:T(128)} %label_ref.3, s32[1]{0:T(128)S(6)} %copy.12.live_ref, f32[3,128,128]{2,1,0:T(8,128)} %bitcast.41, f32[128,4,128]{2,1,0:T(4,128)} %waves_ref.3), custom_call_target="tpu_custom_call" | custom-call | bytes 1048576 | tf_op jit(solution)/shard_map/pack/pallas_call | solution.py:69
  4.0 7.6 %all-to-all-start.1 = ((f32[32,64,128]{2,1,0:T(8,128)}), f32[32,64,128]{2,1,0:T(8,128)S(1)}, u32[]{:S(2)}, u32[]{:S(2)}) async-start(f32[32,64,128]{2,1,0:T(8,128)} %pack.3), calls=%async_computation.1 | async-start | bytes 2097152 | tf_op jit(solution)/shard_map/all_to_all | solution.py:366
  11.7 3.4 %pack.2 = f32[32,64,128]{2,1,0:T(8,128)} custom-call(s32[128]{0:T(128)} %label_ref.3, s32[1]{0:T(128)S(6)} %copy.12.live_ref, f32[3,128,128]{2,1,0:T(8,128)} %bitcast.42, f32[128,4,128]{2,1,0:T(4,128)} %waves_ref.3), custom_call_target="tpu_custom_call" | custom-call | bytes 1048576 | tf_op jit(solution)/shard_map/pack/pallas_call | solution.py:69
  15.0 12.6 %all-to-all-done.1.x_ref = f32[32,64,128]{2,1,0:T(8,128)S(1)} async-done(((f32[32,64,128]{2,1,0:T(8,128)}), f32[32,64,128]{2,1,0:T(8,128)S(1)}, u32[]{:S(2)}, u32[]{:S(2)}) %all-to-all-start.1) | async-done | bytes 1048608 | tf_op jit(solution)/shard_map/all_to_all | solution.py:366
  27.7 5.0 %all-to-all-start = ((f32[32,64,128]{2,1,0:T(8,128)}), f32[32,64,128]{2,1,0:T(8,128)S(1)}, u32[]{:S(2)}, u32[]{:S(2)}) async-start(f32[32,64,128]{2,1,0:T(8,128)} %pack.2), calls=%async_computation | async-start | bytes 2097152 | tf_op jit(solution)/shard_map/all_to_all | solution.py:366
  32.8 0.1 copy.11
  33.0 0.1 sub.23.label_ref
  33.1 15.7 %all-to-all-done.x_ref = f32[32,64,128]{2,1,0:T(8,128)S(1)} async-done(((f32[32,64,128]{2,1,0:T(8,128)}), f32[32,64,128]{2,1,0:T(8,128)S(1)}, u32[]{:S(2)}, u32[]{:S(2)}) %all-to-all-start) | async-done | bytes 1048608 | tf_op jit(solution)/shard_map/all_to_all | solution.py:366
  49.0 0.6 copy-done.1
  49.5 14.2 %shard_map.82.prior_ref = f32[2,16,64,64]{3,2,1,0:T(8,128)S(1)} custom-call(s32[256]{0:T(256)S(1)} %sub.23.label_ref, f32[2]{0:T(128)S(1)} %copy-done.1, f32[32,64,128]{2,1,0:T(8,128)S(1)} %all-to-all-done.1.x_ref), custom_call_target="tpu_custom_call" | custom-call | flops 1610612736 | bytes 1572864 | tf_op jit(solution)/shard_map/pallas_call | solution.py:313
  63.8 12.4 %shard_map.83 = f32[8,4,64,128]{3,2,1,0:T(8,128)S(1)} custom-call(s32[256]{0:T(256)S(1)} %sub.19.label_ref, f32[2]{0:T(128)S(1)} %copy-done.1, s32[16,2]{1,0:T(8,128)S(1)} %broadcast_subtract_fusion.corner_ref, s32[1]{0:T(128)} %bitcast.2.tile_ref, f32[32,64,128]{2,1,0:T(8,128)S(1)} %all-to-all-done.x_ref, f32[2,16,64,64]{3,2,1,0:T(8,128)S(1)} %shard_map.82.prior_ref, ...), custom_call_target="tpu_custom_call" | custom-call | flops 1610612736 | bytes 2097152 | tf_op jit(solution)/shard_map/pallas_call | solution.py:313
  76.3 5.4 %collective-permute-start = (f32[2,64,128]{2,1,0:T(8,128)S(1)}, f32[2,64,128]{2,1,0:T(8,128)S(1)}, u32[]{:S(2)}, u32[]{:S(2)}) collective-permute-start(f32[2,64,128]{2,1,0:T(8,128)S(1)} %get-tuple-element.9), channel_id=1, source_target_pairs={{0,1},{1,2},{2,3},{3,4},{4,5},{5,6},{6,7},{7,0},{8,9},{9,10},{10,1... | collective-permute-start | bytes 196616 | tf_op jit(solution)/shard_map/ppermute | solution.py:340
  81.6 4.0 %collective-permute-start.4 = (f32[2,64,128]{2,1,0:T(8,128)S(1)}, f32[2,64,128]{2,1,0:T(8,128)S(1)}, u32[]{:S(2)}, u32[]{:S(2)}) collective-permute-start(f32[2,64,128]{2,1,0:T(8,128)S(1)} %get-tuple-element.10), channel_id=1, source_target_pairs={{0,7},{1,0},{2,1},{3,2},{4,3},{5,4},{6,5},{7,6},{8,15},{9,8},{10,9... | collective-permute-start | bytes 196616 | tf_op jit(solution)/shard_map/ppermute | solution.py:341
  85.7 2.2 %collective-permute-done = f32[2,64,128]{2,1,0:T(8,128)S(1)} collective-permute-done((f32[2,64,128]{2,1,0:T(8,128)S(1)}, f32[2,64,128]{2,1,0:T(8,128)S(1)}, u32[]{:S(2)}, u32[]{:S(2)}) %collective-permute-start) | collective-permute-done | bytes 65568 | tf_op jit(solution)/shard_map/ppermute | solution.py:340
  87.8 0.3 collective-permute-done.4
  88.3 3.9 %collective-permute-start.5 = (f32[4,64,128]{2,1,0:T(8,128)S(1)}, f32[4,64,128]{2,1,0:T(8,128)S(1)}, u32[]{:S(2)}, u32[]{:S(2)}) collective-permute-start(f32[4,64,128]{2,1,0:T(8,128)S(1)} %pad_maximum_fusion.1), channel_id=1, source_target_pairs={{0,7},{1,0},{2,1},{3,2},{4,3},{5,4},{6,5},{7,6},{8,15},{9,8},{10,9... | collective-permute-start | bytes 393224 | tf_op jit(solution)/shard_map/ppermute | solution.py:350
  92.2 2.7 %collective-permute-done.1 = f32[4,64,128]{2,1,0:T(8,128)S(1)} collective-permute-done((f32[4,64,128]{2,1,0:T(8,128)S(1)}, f32[4,64,128]{2,1,0:T(8,128)S(1)}, u32[]{:S(2)}, u32[]{:S(2)}) %collective-permute-start.1) | collective-permute-done | bytes 131104 | tf_op jit(solution)/shard_map/ppermute | solution.py:349
  95.0 6.2 %collective-permute-done.2 = f32[4,64,128]{2,1,0:T(8,128)S(1)} collective-permute-done((f32[4,64,128]{2,1,0:T(8,128)S(1)}, f32[4,64,128]{2,1,0:T(8,128)S(1)}, u32[]{:S(2)}, u32[]{:S(2)}) %collective-permute-start.2) | collective-permute-done | bytes 131104 | tf_op jit(solution)/shard_map/ppermute | solution.py:349
  101.2 0.9 collective-permute-start.6
  102.1 1.2 %collective-permute-start.3 = (f32[4,64,128]{2,1,0:T(8,128)S(1)}, f32[4,64,128]{2,1,0:T(8,128)S(1)}, u32[]{:S(2)}, u32[]{:S(2)}) collective-permute-start(f32[4,64,128]{2,1,0:T(8,128)S(1)} %get-tuple-element.5), channel_id=1, source_target_pairs={{0,1},{1,2},{2,3},{3,4},{4,5},{5,6},{6,7},{7,0},{8,9},{9,10},{10,1... | collective-permute-start | bytes 393224 | tf_op jit(solution)/shard_map/ppermute | solution.py:349
  103.3 2.9 %collective-permute-done.6 = f32[4,64,128]{2,1,0:T(8,128)S(1)} collective-permute-done((f32[4,64,128]{2,1,0:T(8,128)S(1)}, f32[4,64,128]{2,1,0:T(8,128)S(1)}, u32[]{:S(2)}, u32[]{:S(2)}) %collective-permute-start.6) | collective-permute-done | bytes 131104 | tf_op jit(solution)/shard_map/ppermute | solution.py:350
  106.3 2.1 %collective-permute-start.7 = (f32[4,64,128]{2,1,0:T(8,128)S(1)}, f32[4,64,128]{2,1,0:T(8,128)S(1)}, u32[]{:S(2)}, u32[]{:S(2)}) collective-permute-start(f32[4,64,128]{2,1,0:T(8,128)S(1)} %fusion.1), channel_id=1, source_target_pairs={{0,7},{1,0},{2,1},{3,2},{4,3},{5,4},{6,5},{7,6},{8,15},{9,8},{10,9... | collective-permute-start | bytes 393224 | tf_op jit(solution)/shard_map/ppermute | solution.py:350
  108.4 2.9 %collective-permute-done.7 = f32[4,64,128]{2,1,0:T(8,128)S(1)} collective-permute-done((f32[4,64,128]{2,1,0:T(8,128)S(1)}, f32[4,64,128]{2,1,0:T(8,128)S(1)}, u32[]{:S(2)}, u32[]{:S(2)}) %collective-permute-start.7) | collective-permute-done | bytes 131104 | tf_op jit(solution)/shard_map/ppermute | solution.py:350
  111.3 0.7 fusion.5
  (24 shorter events, 0.7 us)
Async XLA Ops:
  0.0 32.7 %copy-start = (s32[512,2]{0,1:T(2,128)S(1)}, s32[512,2]{0,1:T(2,128)}, u32[]{:S(2)}) copy-start(s32[512,2]{0,1:T(2,128)} %param.12) | copy-start | bytes 12292
  4.0 23.6 %all-to-all-start.1 = ((f32[32,64,128]{2,1,0:T(8,128)}), f32[32,64,128]{2,1,0:T(8,128)S(1)}, u32[]{:S(2)}, u32[]{:S(2)}) async-start(f32[32,64,128]{2,1,0:T(8,128)} %pack.3), calls=%async_computation.1 | async-start | bytes 2097152 | tf_op jit(solution)/shard_map/all_to_all | solution.py:366
  27.7 21.1 %all-to-all-start = ((f32[32,64,128]{2,1,0:T(8,128)}), f32[32,64,128]{2,1,0:T(8,128)S(1)}, u32[]{:S(2)}, u32[]{:S(2)}) async-start(f32[32,64,128]{2,1,0:T(8,128)} %pack.2), calls=%async_computation | async-start | bytes 2097152 | tf_op jit(solution)/shard_map/all_to_all | solution.py:366
  48.9 0.7 copy-start.1
  49.5 14.3 %copy-start.2 = (f32[64,256]{1,0:T(8,128)S(1)}, f32[64,256]{1,0:T(8,128)}, u32[]{:S(2)}) copy-start(f32[64,256]{1,0:T(8,128)} %constant.28.clone.spread_ref) | copy-start | bytes 196612
  49.5 14.3 %copy-start.3 = (f32[64,64]{1,0:T(8,128)S(1)}, f32[64,64]{1,0:T(8,128)}, u32[]{:S(2)}) copy-start(f32[64,64]{1,0:T(8,128)} %constant.27.clone.mix_ref) | copy-start | bytes 49156
  76.3 11.5 %collective-permute-start = (f32[2,64,128]{2,1,0:T(8,128)S(1)}, f32[2,64,128]{2,1,0:T(8,128)S(1)}, u32[]{:S(2)}, u32[]{:S(2)}) collective-permute-start(f32[2,64,128]{2,1,0:T(8,128)S(1)} %get-tuple-element.9), channel_id=1, source_target_pairs={{0,1},{1,2},{2,3},{3,4},{4,5},{5,6},{6,7},{7,0},{8,9},{9,10},{10,1... | collective-permute-start | bytes 196616 | tf_op jit(solution)/shard_map/ppermute | solution.py:340
  81.6 6.5 %collective-permute-start.4 = (f32[2,64,128]{2,1,0:T(8,128)S(1)}, f32[2,64,128]{2,1,0:T(8,128)S(1)}, u32[]{:S(2)}, u32[]{:S(2)}) collective-permute-start(f32[2,64,128]{2,1,0:T(8,128)S(1)} %get-tuple-element.10), channel_id=1, source_target_pairs={{0,7},{1,0},{2,1},{3,2},{4,3},{5,4},{6,5},{7,6},{8,15},{9,8},{10,9... | collective-permute-start | bytes 196616 | tf_op jit(solution)/shard_map/ppermute | solution.py:341
  88.2 6.7 %collective-permute-start.1 = (f32[4,64,128]{2,1,0:T(8,128)S(1)}, f32[4,64,128]{2,1,0:T(8,128)S(1)}, u32[]{:S(2)}, u32[]{:S(2)}) collective-permute-start(f32[4,64,128]{2,1,0:T(8,128)S(1)} %pad_maximum_fusion), channel_id=1, source_target_pairs={{0,1},{1,2},{2,3},{3,4},{4,5},{5,6},{6,7},{7,0},{8,9},{9,10},{10,1... | collective-permute-start | bytes 393224 | tf_op jit(solution)/shard_map/ppermute | solution.py:349
  88.3 6.7 %collective-permute-start.5 = (f32[4,64,128]{2,1,0:T(8,128)S(1)}, f32[4,64,128]{2,1,0:T(8,128)S(1)}, u32[]{:S(2)}, u32[]{:S(2)}) collective-permute-start(f32[4,64,128]{2,1,0:T(8,128)S(1)} %pad_maximum_fusion.1), channel_id=1, source_target_pairs={{0,7},{1,0},{2,1},{3,2},{4,3},{5,4},{6,5},{7,6},{8,15},{9,8},{10,9... | collective-permute-start | bytes 393224 | tf_op jit(solution)/shard_map/ppermute | solution.py:350
  94.9 6.3 %collective-permute-start.2 = (f32[4,64,128]{2,1,0:T(8,128)S(1)}, f32[4,64,128]{2,1,0:T(8,128)S(1)}, u32[]{:S(2)}, u32[]{:S(2)}) collective-permute-start(f32[4,64,128]{2,1,0:T(8,128)S(1)} %fusion.2), channel_id=1, source_target_pairs={{0,1},{1,2},{2,3},{3,4},{4,5},{5,6},{6,7},{7,0},{8,9},{9,10},{10,1... | collective-permute-start | bytes 393224 | tf_op jit(solution)/shard_map/ppermute | solution.py:349
  101.2 5.0 %collective-permute-start.6 = (f32[4,64,128]{2,1,0:T(8,128)S(1)}, f32[4,64,128]{2,1,0:T(8,128)S(1)}, u32[]{:S(2)}, u32[]{:S(2)}) collective-permute-start(f32[4,64,128]{2,1,0:T(8,128)S(1)} %get-tuple-element.6), channel_id=1, source_target_pairs={{0,7},{1,0},{2,1},{3,2},{4,3},{5,4},{6,5},{7,6},{8,15},{9,8},{10,9... | collective-permute-start | bytes 393224 | tf_op jit(solution)/shard_map/ppermute | solution.py:350
  102.1 6.3 %collective-permute-start.3 = (f32[4,64,128]{2,1,0:T(8,128)S(1)}, f32[4,64,128]{2,1,0:T(8,128)S(1)}, u32[]{:S(2)}, u32[]{:S(2)}) collective-permute-start(f32[4,64,128]{2,1,0:T(8,128)S(1)} %get-tuple-element.5), channel_id=1, source_target_pairs={{0,1},{1,2},{2,3},{3,4},{4,5},{5,6},{6,7},{7,0},{8,9},{9,10},{10,1... | collective-permute-start | bytes 393224 | tf_op jit(solution)/shard_map/ppermute | solution.py:349
  106.3 5.0 %collective-permute-start.7 = (f32[4,64,128]{2,1,0:T(8,128)S(1)}, f32[4,64,128]{2,1,0:T(8,128)S(1)}, u32[]{:S(2)}, u32[]{:S(2)}) collective-permute-start(f32[4,64,128]{2,1,0:T(8,128)S(1)} %fusion.1), channel_id=1, source_target_pairs={{0,7},{1,0},{2,1},{3,2},{4,3},{5,4},{6,5},{7,6},{8,15},{9,8},{10,9... | collective-permute-start | bytes 393224 | tf_op jit(solution)/shard_map/ppermute | solution.py:350

commit v9 on v8

--- a/solution.py
+++ b/solution.py
@@ -334,21 +334,20 @@
 
 def summed_around(parts, axis):
     size = lax.axis_size(axis)
-    far = size // 2
-    up = [(i, (i + 1) % size) for i in range(size)]
-    down = [(i, (i - 1) % size) for i in range(size)]
-    rising = lax.ppermute(parts[far, :CH], axis, up)
-    falling = lax.ppermute(parts[far, CH:], axis, down)
-    for distance in range(far - 1, 0, -1):
-        near, opposite = parts[distance], parts[size - distance]
-        if distance == far - 1:
-            rising = jnp.concatenate([near[:CH] + rising, near[CH:]])
-            falling = jnp.concatenate([opposite[:CH], opposite[CH:] + falling])
-        else:
-            rising, falling = near + rising, opposite + falling
-        rising = lax.ppermute(rising, axis, up)
-        falling = lax.ppermute(falling, axis, down)
-    return parts[0] + rising + falling
+
+    def sent(value, hops):
+        return lax.ppermute(value, axis, [(i, (i + hops) % size) for i in range(size)])
+
+    rising = sent(jnp.concatenate([parts[3], parts[4, :CH]]), 2)
+    falling = sent(jnp.concatenate([parts[5], parts[4, CH:]]), -2)
+    planes = 2 * CH
+    pieces = [
+        sent(jnp.concatenate([parts[2, :CH] + rising[planes:], parts[2, CH:]]), 2),
+        sent(jnp.concatenate([parts[6, :CH], parts[6, CH:] + falling[planes:]]), -2),
+        sent(parts[1] + rising[:planes], 1),
+        sent(parts[7] + falling[:planes], -1),
+    ]
+    return sum(pieces, parts[0])
 
 
 def local(block_coords, block_visibilities, subgrid_of_block, live_blocks, corners, channel_scale):

time: 112 us -> 113 us (level)
  the two profiles are of different devices: /device:TPU:2 before, /device:TPU:7 now
where the time goes in v9:
time: 113 us
  waiting for transfers between devices  48.5 us (43%)
  Pallas kernels  36.8 us (33%)
  starting transfers between devices  24.5 us (22%)
    pallas_call x2, Pallas kernels, chunk_call(): pl.pallas_call(kernel, out_shape=jax.ShapeDtypeStruct(out_shape, jnp.floa...  30 us
    all_to_all x2, waiting for transfers between devices, local(): lax.all_to_all(packed, 'work', split_axis=0, concat_axis=0, tiled=True)  28.1 us
    ppermute x6, waiting for transfers between devices, sent(): lax.ppermute(value, axis, [(i, (i + hops) % size) for i in range(size)])  20.5 us
    all_to_all x2, starting transfers between devices, local(): lax.all_to_all(packed, 'work', split_axis=0, concat_axis=0, tiled=True)  13 us
    ppermute x6, starting transfers between devices, sent(): lax.ppermute(value, axis, [(i, (i + hops) % size) for i in range(size)])  11.4 us
    pallas_call x2, Pallas kernels, pack(): pl.pallas_call(functools.partial(pack_kernel, chunk), name='pack', out_sh...  6.73 us
  transfers between devices with their start and end apart: 8, of which 7 were waited for; matrix products, arithmetic and copies ran while one was open for 0% of the time, Pallas kernels for 3%

profile of v9, /device:TPU:7, one launch (start us, length us, event | category | flops | bytes accessed | tf_op | source)
XLA Modules:
  0.0 112.5 jit_solution(1108866355142690974)
XLA Ops:
  0.7 3.4 %pack.3 = f32[32,64,128]{2,1,0:T(8,128)} custom-call(s32[128]{0:T(128)} %label_ref.3, s32[1]{0:T(128)S(6)} %copy.12.live_ref, f32[3,128,128]{2,1,0:T(8,128)} %bitcast.41, f32[128,4,128]{2,1,0:T(4,128)} %waves_ref.3), custom_call_target="tpu_custom_call" | custom-call | bytes 1048576 | tf_op jit(solution)/shard_map/pack/pallas_call | solution.py:69
  4.1 7.8 %all-to-all-start.1 = ((f32[32,64,128]{2,1,0:T(8,128)}), f32[32,64,128]{2,1,0:T(8,128)S(1)}, u32[]{:S(2)}, u32[]{:S(2)}) async-start(f32[32,64,128]{2,1,0:T(8,128)} %pack.3), calls=%async_computation.1 | async-start | bytes 2097152 | tf_op jit(solution)/shard_map/all_to_all | solution.py:365
  11.9 3.4 %pack.2 = f32[32,64,128]{2,1,0:T(8,128)} custom-call(s32[128]{0:T(128)} %label_ref.3, s32[1]{0:T(128)S(6)} %copy.12.live_ref, f32[3,128,128]{2,1,0:T(8,128)} %bitcast.42, f32[128,4,128]{2,1,0:T(4,128)} %waves_ref.3), custom_call_target="tpu_custom_call" | custom-call | bytes 1048576 | tf_op jit(solution)/shard_map/pack/pallas_call | solution.py:69
  15.3 12.5 %all-to-all-done.1.x_ref = f32[32,64,128]{2,1,0:T(8,128)S(1)} async-done(((f32[32,64,128]{2,1,0:T(8,128)}), f32[32,64,128]{2,1,0:T(8,128)S(1)}, u32[]{:S(2)}, u32[]{:S(2)}) %all-to-all-start.1) | async-done | bytes 1048608 | tf_op jit(solution)/shard_map/all_to_all | solution.py:365
  27.8 5.2 %all-to-all-start = ((f32[32,64,128]{2,1,0:T(8,128)}), f32[32,64,128]{2,1,0:T(8,128)S(1)}, u32[]{:S(2)}, u32[]{:S(2)}) async-start(f32[32,64,128]{2,1,0:T(8,128)} %pack.2), calls=%async_computation | async-start | bytes 2097152 | tf_op jit(solution)/shard_map/all_to_all | solution.py:365
  33.1 0.1 copy.11
  33.3 0.1 sub.23.label_ref
  33.4 15.5 %all-to-all-done.x_ref = f32[32,64,128]{2,1,0:T(8,128)S(1)} async-done(((f32[32,64,128]{2,1,0:T(8,128)}), f32[32,64,128]{2,1,0:T(8,128)S(1)}, u32[]{:S(2)}, u32[]{:S(2)}) %all-to-all-start) | async-done | bytes 1048608 | tf_op jit(solution)/shard_map/all_to_all | solution.py:365
  49.0 0.1 sub.19.label_ref
  49.1 0.6 copy-done.1
  49.6 14.2 %shard_map.82.prior_ref = f32[2,16,64,64]{3,2,1,0:T(8,128)S(1)} custom-call(s32[256]{0:T(256)S(1)} %sub.23.label_ref, f32[2]{0:T(128)S(1)} %copy-done.1, f32[32,64,128]{2,1,0:T(8,128)S(1)} %all-to-all-done.1.x_ref), custom_call_target="tpu_custom_call" | custom-call | flops 1610612736 | bytes 1572864 | tf_op jit(solution)/shard_map/pallas_call | solution.py:313
  63.9 15.8 %shard_map.83 = f32[8,4,64,128]{3,2,1,0:T(8,128)S(1)} custom-call(s32[256]{0:T(256)S(1)} %sub.19.label_ref, f32[2]{0:T(128)S(1)} %copy-done.1, s32[16,2]{1,0:T(8,128)S(1)} %broadcast_subtract_fusion.corner_ref, s32[1]{0:T(128)} %bitcast.2.tile_ref, f32[32,64,128]{2,1,0:T(8,128)S(1)} %all-to-all-done.x_ref, f32[2,16,64,64]{3,2,1,0:T(8,128)S(1)} %shard_map.82.prior_ref, ...), custom_call_target="tpu_custom_call" | custom-call | flops 1610612736 | bytes 2097152 | tf_op jit(solution)/shard_map/pallas_call | solution.py:313
  79.8 6.1 %collective-permute-start.2 = (f32[6,64,128]{2,1,0:T(8,128)S(1)}, f32[6,64,128]{2,1,0:T(8,128)S(1)}, u32[]{:S(2)}, u32[]{:S(2)}) collective-permute-start(f32[6,64,128]{2,1,0:T(8,128)S(1)} %pad_maximum_fusion.1), channel_id=1, source_target_pairs={{0,6},{1,7},{2,0},{3,1},{4,2},{5,3},{6,4},{7,5},{8,14},{9,15},{10,... | collective-permute-start | bytes 589832 | tf_op jit(solution)/shard_map/ppermute | solution.py:339
  85.9 0.1 collective-permute-start
  86.0 8.4 %collective-permute-done.2 = f32[6,64,128]{2,1,0:T(8,128)S(1)} collective-permute-done((f32[6,64,128]{2,1,0:T(8,128)S(1)}, f32[6,64,128]{2,1,0:T(8,128)S(1)}, u32[]{:S(2)}, u32[]{:S(2)}) %collective-permute-start.2) | collective-permute-done | bytes 196640 | tf_op jit(solution)/shard_map/ppermute | solution.py:339
  94.4 4.0 %collective-permute-done = f32[6,64,128]{2,1,0:T(8,128)S(1)} collective-permute-done((f32[6,64,128]{2,1,0:T(8,128)S(1)}, f32[6,64,128]{2,1,0:T(8,128)S(1)}, u32[]{:S(2)}, u32[]{:S(2)}) %collective-permute-start) | collective-permute-done | bytes 196640 | tf_op jit(solution)/shard_map/ppermute | solution.py:339
  98.5 0.1 collective-permute-start.3
  98.6 2.4 %collective-permute-start.1 = (f32[4,64,128]{2,1,0:T(8,128)S(1)}, f32[4,64,128]{2,1,0:T(8,128)S(1)}, u32[]{:S(2)}, u32[]{:S(2)}) collective-permute-start(f32[4,64,128]{2,1,0:T(8,128)S(1)} %pad_maximum_fusion.2), channel_id=1, source_target_pairs={{0,2},{1,3},{2,4},{3,5},{4,6},{5,7},{6,0},{7,1},{8,10},{9,11},{10,... | collective-permute-start | bytes 393224 | tf_op jit(solution)/shard_map/ppermute | solution.py:339
  101.1 1.2 %collective-permute-start.4 = (f32[4,64,128]{2,1,0:T(8,128)S(1)}, f32[4,64,128]{2,1,0:T(8,128)S(1)}, u32[]{:S(2)}, u32[]{:S(2)}) collective-permute-start(f32[4,64,128]{2,1,0:T(8,128)S(1)} %get-tuple-element.11), channel_id=1, source_target_pairs={{0,1},{1,2},{2,3},{3,4},{4,5},{5,6},{6,7},{7,0},{8,9},{9,10},{10,1... | collective-permute-start | bytes 393224 | tf_op jit(solution)/shard_map/ppermute | solution.py:339
  102.3 1.6 %collective-permute-start.5 = (f32[4,64,128]{2,1,0:T(8,128)S(1)}, f32[4,64,128]{2,1,0:T(8,128)S(1)}, u32[]{:S(2)}, u32[]{:S(2)}) collective-permute-start(f32[4,64,128]{2,1,0:T(8,128)S(1)} %get-tuple-element.12), channel_id=1, source_target_pairs={{0,7},{1,0},{2,1},{3,2},{4,3},{5,4},{6,5},{7,6},{8,15},{9,8},{10,9... | collective-permute-start | bytes 393224 | tf_op jit(solution)/shard_map/ppermute | solution.py:339
  103.8 3.1 %collective-permute-done.3 = f32[4,64,128]{2,1,0:T(8,128)S(1)} collective-permute-done((f32[4,64,128]{2,1,0:T(8,128)S(1)}, f32[4,64,128]{2,1,0:T(8,128)S(1)}, u32[]{:S(2)}, u32[]{:S(2)}) %collective-permute-start.3) | collective-permute-done | bytes 131104 | tf_op jit(solution)/shard_map/ppermute | solution.py:339
  106.9 1.3 %collective-permute-done.1 = f32[4,64,128]{2,1,0:T(8,128)S(1)} collective-permute-done((f32[4,64,128]{2,1,0:T(8,128)S(1)}, f32[4,64,128]{2,1,0:T(8,128)S(1)}, u32[]{:S(2)}, u32[]{:S(2)}) %collective-permute-start.1) | collective-permute-done | bytes 131104 | tf_op jit(solution)/shard_map/ppermute | solution.py:339
  108.2 3.6 %collective-permute-done.4 = f32[4,64,128]{2,1,0:T(8,128)S(1)} collective-permute-done((f32[4,64,128]{2,1,0:T(8,128)S(1)}, f32[4,64,128]{2,1,0:T(8,128)S(1)}, u32[]{:S(2)}, u32[]{:S(2)}) %collective-permute-start.4) | collective-permute-done | bytes 131104 | tf_op jit(solution)/shard_map/ppermute | solution.py:339
  111.8 0.7 fusion.3
  (21 shorter events, 0.4 us)
Async XLA Ops:
  0.0 33.0 %copy-start = (s32[512,2]{0,1:T(2,128)S(1)}, s32[512,2]{0,1:T(2,128)}, u32[]{:S(2)}) copy-start(s32[512,2]{0,1:T(2,128)} %param.12) | copy-start | bytes 12292
  4.1 23.7 %all-to-all-start.1 = ((f32[32,64,128]{2,1,0:T(8,128)}), f32[32,64,128]{2,1,0:T(8,128)S(1)}, u32[]{:S(2)}, u32[]{:S(2)}) async-start(f32[32,64,128]{2,1,0:T(8,128)} %pack.3), calls=%async_computation.1 | async-start | bytes 2097152 | tf_op jit(solution)/shard_map/all_to_all | solution.py:365
  27.8 21.1 %all-to-all-start = ((f32[32,64,128]{2,1,0:T(8,128)}), f32[32,64,128]{2,1,0:T(8,128)S(1)}, u32[]{:S(2)}, u32[]{:S(2)}) async-start(f32[32,64,128]{2,1,0:T(8,128)} %pack.2), calls=%async_computation | async-start | bytes 2097152 | tf_op jit(solution)/shard_map/all_to_all | solution.py:365
  49.0 0.7 copy-start.1
  49.6 14.2 %copy-start.2 = (f32[64,256]{1,0:T(8,128)S(1)}, f32[64,256]{1,0:T(8,128)}, u32[]{:S(2)}) copy-start(f32[64,256]{1,0:T(8,128)} %constant.28.clone.spread_ref) | copy-start | bytes 196612
  49.6 14.2 %copy-start.3 = (f32[64,64]{1,0:T(8,128)S(1)}, f32[64,64]{1,0:T(8,128)}, u32[]{:S(2)}) copy-start(f32[64,64]{1,0:T(8,128)} %constant.27.clone.mix_ref) | copy-start | bytes 49156
  79.8 14.6 %collective-permute-start.2 = (f32[6,64,128]{2,1,0:T(8,128)S(1)}, f32[6,64,128]{2,1,0:T(8,128)S(1)}, u32[]{:S(2)}, u32[]{:S(2)}) collective-permute-start(f32[6,64,128]{2,1,0:T(8,128)S(1)} %pad_maximum_fusion.1), channel_id=1, source_target_pairs={{0,6},{1,7},{2,0},{3,1},{4,2},{5,3},{6,4},{7,5},{8,14},{9,15},{10,... | collective-permute-start | bytes 589832 | tf_op jit(solution)/shard_map/ppermute | solution.py:339
  85.9 12.6 %collective-permute-start = (f32[6,64,128]{2,1,0:T(8,128)S(1)}, f32[6,64,128]{2,1,0:T(8,128)S(1)}, u32[]{:S(2)}, u32[]{:S(2)}) collective-permute-start(f32[6,64,128]{2,1,0:T(8,128)S(1)} %pad_maximum_fusion), channel_id=1, source_target_pairs={{0,2},{1,3},{2,4},{3,5},{4,6},{5,7},{6,0},{7,1},{8,10},{9,11},{10,... | collective-permute-start | bytes 589832 | tf_op jit(solution)/shard_map/ppermute | solution.py:339
  98.5 8.4 %collective-permute-start.3 = (f32[4,64,128]{2,1,0:T(8,128)S(1)}, f32[4,64,128]{2,1,0:T(8,128)S(1)}, u32[]{:S(2)}, u32[]{:S(2)}) collective-permute-start(f32[4,64,128]{2,1,0:T(8,128)S(1)} %pad_maximum_fusion.3), channel_id=1, source_target_pairs={{0,6},{1,7},{2,0},{3,1},{4,2},{5,3},{6,4},{7,5},{8,14},{9,15},{10,... | collective-permute-start | bytes 393224 | tf_op jit(solution)/shard_map/ppermute | solution.py:339
  98.6 9.6 %collective-permute-start.1 = (f32[4,64,128]{2,1,0:T(8,128)S(1)}, f32[4,64,128]{2,1,0:T(8,128)S(1)}, u32[]{:S(2)}, u32[]{:S(2)}) collective-permute-start(f32[4,64,128]{2,1,0:T(8,128)S(1)} %pad_maximum_fusion.2), channel_id=1, source_target_pairs={{0,2},{1,3},{2,4},{3,5},{4,6},{5,7},{6,0},{7,1},{8,10},{9,11},{10,... | collective-permute-start | bytes 393224 | tf_op jit(solution)/shard_map/ppermute | solution.py:339
  101.1 10.8 %collective-permute-start.4 = (f32[4,64,128]{2,1,0:T(8,128)S(1)}, f32[4,64,128]{2,1,0:T(8,128)S(1)}, u32[]{:S(2)}, u32[]{:S(2)}) collective-permute-start(f32[4,64,128]{2,1,0:T(8,128)S(1)} %get-tuple-element.11), channel_id=1, source_target_pairs={{0,1},{1,2},{2,3},{3,4},{4,5},{5,6},{6,7},{7,0},{8,9},{9,10},{10,1... | collective-permute-start | bytes 393224 | tf_op jit(solution)/shard_map/ppermute | solution.py:339
  102.3 9.6 %collective-permute-start.5 = (f32[4,64,128]{2,1,0:T(8,128)S(1)}, f32[4,64,128]{2,1,0:T(8,128)S(1)}, u32[]{:S(2)}, u32[]{:S(2)}) collective-permute-start(f32[4,64,128]{2,1,0:T(8,128)S(1)} %get-tuple-element.12), channel_id=1, source_target_pairs={{0,7},{1,0},{2,1},{3,2},{4,3},{5,4},{6,5},{7,6},{8,15},{9,8},{10,9... | collective-permute-start | bytes 393224 | tf_op jit(solution)/shard_map/ppermute | solution.py:339

commit v10 on v9

--- a/solution.py
+++ b/solution.py
@@ -128,11 +128,11 @@
     return (real[0], imag[0]), (real[1], imag[1])
 
 
-def factor_rows(fields, factor, low, put_left, put_right):
+def factor_rows(fields, factor, depth_factor, low, put_left, put_right):
     u, v, w = fields[:3]
-    first = u * (factor * (2.0 * math.pi / (2 * SUB)))
-    second = v * (factor * (2.0 * math.pi / (2 * SUB)))
-    depth = w * (factor * (math.pi / (SUB * SUB)))
+    first = u * factor
+    second = v * factor
+    depth = w * depth_factor
     along_u = sin_cos(first - depth, 5, 5)
     along_v = sin_cos(second - depth, 5, 5)
     turn = sin_cos(depth * 4.0, 3, 3)
@@ -200,7 +200,12 @@
 
         chosen = [field(index) for index in (0, 1, 2, 3 + 2 * ch, 4 + 2 * ch)]
         factor_rows(
-            chosen, scale_ref[ch], low, functools.partial(put, left), functools.partial(put, right)
+            chosen,
+            scale_ref[ch],
+            scale_ref[CH + ch],
+            low,
+            functools.partial(put, left),
+            functools.partial(put, right),
         )
 
     def gather(source, ch):
@@ -357,6 +362,9 @@
     coords = jnp.swapaxes(block_coords, 0, 1)
     local_corners = lax.dynamic_slice_in_dim(corners, worker * SUBW, SUBW, 0)
     local_corners = local_corners - jnp.stack([0 * worker, worker * GCW])[None, :]
+    factors = jnp.concatenate(
+        [channel_scale * (2.0 * math.pi / (2 * SUB)), channel_scale * (math.pi / (SUB * SUB))]
+    )
     sums = None
     for chunk in range(CHUNKS):
         packed = pack(
@@ -365,12 +373,12 @@
         arrived = lax.all_to_all(packed, "work", split_axis=0, concat_axis=0, tiled=True)
         labels = arrived[:, FIELDS * GROUP, :GROUP].astype(jnp.int32).reshape(workers * GROUP) - 1
         if chunk == 0:
-            sums = chunk_call(first_kernel, (labels, channel_scale), arrived, (), SUMS, [])
+            sums = chunk_call(first_kernel, (labels, factors), arrived, (), SUMS, [])
     mix, spread = transform_tables()
     tile = lax.axis_index("tile").astype(jnp.int32).reshape(1)
     parts = chunk_call(
         last_kernel,
-        (labels, channel_scale, local_corners, tile),
+        (labels, factors, local_corners, tile),
         arrived,
         (sums, jnp.asarray(mix), jnp.asarray(spread)),
         (tiles, 2 * CH, TR, GCW),

time: 113 us -> 112 us (level)
  no operation moved by 1% of the time
where the time goes in v10:
time: 112 us
  waiting for transfers between devices  47.8 us (43%)
  Pallas kernels  36.8 us (33%)
  starting transfers between devices  24.5 us (22%)
    pallas_call x2, Pallas kernels, chunk_call(): pl.pallas_call(kernel, out_shape=jax.ShapeDtypeStruct(out_shape, jnp.floa...  30 us
    all_to_all x2, waiting for transfers between devices, local(): lax.all_to_all(packed, 'work', split_axis=0, concat_axis=0, tiled=True)  27.4 us
    ppermute x6, waiting for transfers between devices, sent(): lax.ppermute(value, axis, [(i, (i + hops) % size) for i in range(size)])  20.4 us
    all_to_all x2, starting transfers between devices, local(): lax.all_to_all(packed, 'work', split_axis=0, concat_axis=0, tiled=True)  13 us
    ppermute x6, starting transfers between devices, sent(): lax.ppermute(value, axis, [(i, (i + hops) % size) for i in range(size)])  11.5 us
    pallas_call x2, Pallas kernels, pack(): pl.pallas_call(functools.partial(pack_kernel, chunk), name='pack', out_sh...  6.73 us
  transfers between devices with their start and end apart: 8, of which 7 were waited for; matrix products, arithmetic and copies ran while one was open for 0% of the time, Pallas kernels for 3%

profile of v10, /device:TPU:7, one launch (start us, length us, event | category | flops | bytes accessed | tf_op | source)
XLA Modules:
  0.0 111.9 jit_solution(1808564227597109020)
XLA Ops:
  0.7 3.4 %pack.3 = f32[32,64,128]{2,1,0:T(8,128)} custom-call(s32[128]{0:T(128)} %label_ref.3, s32[1]{0:T(128)S(6)} %copy.12.live_ref, f32[3,128,128]{2,1,0:T(8,128)} %bitcast.41, f32[128,4,128]{2,1,0:T(4,128)} %waves_ref.3), custom_call_target="tpu_custom_call" | custom-call | bytes 1048576 | tf_op jit(solution)/shard_map/pack/pallas_call | solution.py:69
  4.0 7.8 %all-to-all-start.1 = ((f32[32,64,128]{2,1,0:T(8,128)}), f32[32,64,128]{2,1,0:T(8,128)S(1)}, u32[]{:S(2)}, u32[]{:S(2)}) async-start(f32[32,64,128]{2,1,0:T(8,128)} %pack.3), calls=%async_computation.1 | async-start | bytes 2097152 | tf_op jit(solution)/shard_map/all_to_all | solution.py:373
  11.9 3.4 %pack.2 = f32[32,64,128]{2,1,0:T(8,128)} custom-call(s32[128]{0:T(128)} %label_ref.3, s32[1]{0:T(128)S(6)} %copy.12.live_ref, f32[3,128,128]{2,1,0:T(8,128)} %bitcast.42, f32[128,4,128]{2,1,0:T(4,128)} %waves_ref.3), custom_call_target="tpu_custom_call" | custom-call | bytes 1048576 | tf_op jit(solution)/shard_map/pack/pallas_call | solution.py:69
  15.3 12.5 %all-to-all-done.1.x_ref = f32[32,64,128]{2,1,0:T(8,128)S(1)} async-done(((f32[32,64,128]{2,1,0:T(8,128)}), f32[32,64,128]{2,1,0:T(8,128)S(1)}, u32[]{:S(2)}, u32[]{:S(2)}) %all-to-all-start.1) | async-done | bytes 1048608 | tf_op jit(solution)/shard_map/all_to_all | solution.py:373
  27.8 5.2 %all-to-all-start = ((f32[32,64,128]{2,1,0:T(8,128)}), f32[32,64,128]{2,1,0:T(8,128)S(1)}, u32[]{:S(2)}, u32[]{:S(2)}) async-start(f32[32,64,128]{2,1,0:T(8,128)} %pack.2), calls=%async_computation | async-start | bytes 2097152 | tf_op jit(solution)/shard_map/all_to_all | solution.py:373
  33.1 0.1 copy.11
  33.2 0.6 copy-done.3
  34.0 0.1 sub.23.label_ref
  34.0 14.9 %all-to-all-done.x_ref = f32[32,64,128]{2,1,0:T(8,128)S(1)} async-done(((f32[32,64,128]{2,1,0:T(8,128)}), f32[32,64,128]{2,1,0:T(8,128)S(1)}, u32[]{:S(2)}, u32[]{:S(2)}) %all-to-all-start) | async-done | bytes 1048608 | tf_op jit(solution)/shard_map/all_to_all | solution.py:373
  49.0 0.1 sub.19.label_ref
  49.1 14.2 %shard_map.82.prior_ref = f32[2,16,64,64]{3,2,1,0:T(8,128)S(1)} custom-call(s32[256]{0:T(256)S(1)} %sub.23.label_ref, f32[4]{0:T(128)S(1)} %pad_maximum_fusion.4.scale_ref, f32[32,64,128]{2,1,0:T(8,128)S(1)} %all-to-all-done.1.x_ref), custom_call_target="tpu_custom_call" | custom-call | flops 1610612736 | bytes 1572864 | tf_op jit(solution)/shard_map/pallas_call | solution.py:318
  63.3 15.8 %shard_map.83 = f32[8,4,64,128]{3,2,1,0:T(8,128)S(1)} custom-call(s32[256]{0:T(256)S(1)} %sub.19.label_ref, f32[4]{0:T(128)S(1)} %pad_maximum_fusion.4.scale_ref, s32[16,2]{1,0:T(8,128)S(1)} %broadcast_subtract_fusion.corner_ref, s32[1]{0:T(128)} %bitcast.2.tile_ref, f32[32,64,128]{2,1,0:T(8,128)S(1)} %all-to-all-done.x_ref, ...), custom_call_target="tpu_custom_call" | custom-call | flops 1610612736 | bytes 2097152 | tf_op jit(solution)/shard_map/pallas_call | solution.py:318
  79.2 6.1 %collective-permute-start.2 = (f32[6,64,128]{2,1,0:T(8,128)S(1)}, f32[6,64,128]{2,1,0:T(8,128)S(1)}, u32[]{:S(2)}, u32[]{:S(2)}) collective-permute-start(f32[6,64,128]{2,1,0:T(8,128)S(1)} %pad_maximum_fusion.1), channel_id=1, source_target_pairs={{0,6},{1,7},{2,0},{3,1},{4,2},{5,3},{6,4},{7,5},{8,14},{9,15},{10,... | collective-permute-start | bytes 589832 | tf_op jit(solution)/shard_map/ppermute | solution.py:344
  85.4 0.1 collective-permute-start
  85.5 8.4 %collective-permute-done.2 = f32[6,64,128]{2,1,0:T(8,128)S(1)} collective-permute-done((f32[6,64,128]{2,1,0:T(8,128)S(1)}, f32[6,64,128]{2,1,0:T(8,128)S(1)}, u32[]{:S(2)}, u32[]{:S(2)}) %collective-permute-start.2) | collective-permute-done | bytes 196640 | tf_op jit(solution)/shard_map/ppermute | solution.py:344
  93.9 3.9 %collective-permute-done = f32[6,64,128]{2,1,0:T(8,128)S(1)} collective-permute-done((f32[6,64,128]{2,1,0:T(8,128)S(1)}, f32[6,64,128]{2,1,0:T(8,128)S(1)}, u32[]{:S(2)}, u32[]{:S(2)}) %collective-permute-start) | collective-permute-done | bytes 196640 | tf_op jit(solution)/shard_map/ppermute | solution.py:344
  97.8 0.2 collective-permute-start.3
  98.0 2.3 %collective-permute-start.1 = (f32[4,64,128]{2,1,0:T(8,128)S(1)}, f32[4,64,128]{2,1,0:T(8,128)S(1)}, u32[]{:S(2)}, u32[]{:S(2)}) collective-permute-start(f32[4,64,128]{2,1,0:T(8,128)S(1)} %pad_maximum_fusion.2), channel_id=1, source_target_pairs={{0,2},{1,3},{2,4},{3,5},{4,6},{5,7},{6,0},{7,1},{8,10},{9,11},{10,... | collective-permute-start | bytes 393224 | tf_op jit(solution)/shard_map/ppermute | solution.py:344
  100.4 1.2 %collective-permute-start.4 = (f32[4,64,128]{2,1,0:T(8,128)S(1)}, f32[4,64,128]{2,1,0:T(8,128)S(1)}, u32[]{:S(2)}, u32[]{:S(2)}) collective-permute-start(f32[4,64,128]{2,1,0:T(8,128)S(1)} %get-tuple-element.11), channel_id=1, source_target_pairs={{0,1},{1,2},{2,3},{3,4},{4,5},{5,6},{6,7},{7,0},{8,9},{9,10},{10,1... | collective-permute-start | bytes 393224 | tf_op jit(solution)/shard_map/ppermute | solution.py:344
  101.6 1.5 %collective-permute-start.5 = (f32[4,64,128]{2,1,0:T(8,128)S(1)}, f32[4,64,128]{2,1,0:T(8,128)S(1)}, u32[]{:S(2)}, u32[]{:S(2)}) collective-permute-start(f32[4,64,128]{2,1,0:T(8,128)S(1)} %get-tuple-element.12), channel_id=1, source_target_pairs={{0,7},{1,0},{2,1},{3,2},{4,3},{5,4},{6,5},{7,6},{8,15},{9,8},{10,9... | collective-permute-start | bytes 393224 | tf_op jit(solution)/shard_map/ppermute | solution.py:344
  103.2 2.3 %collective-permute-done.3 = f32[4,64,128]{2,1,0:T(8,128)S(1)} collective-permute-done((f32[4,64,128]{2,1,0:T(8,128)S(1)}, f32[4,64,128]{2,1,0:T(8,128)S(1)}, u32[]{:S(2)}, u32[]{:S(2)}) %collective-permute-start.3) | collective-permute-done | bytes 131104 | tf_op jit(solution)/shard_map/ppermute | solution.py:344
  105.4 2.2 %collective-permute-done.1 = f32[4,64,128]{2,1,0:T(8,128)S(1)} collective-permute-done((f32[4,64,128]{2,1,0:T(8,128)S(1)}, f32[4,64,128]{2,1,0:T(8,128)S(1)}, u32[]{:S(2)}, u32[]{:S(2)}) %collective-permute-start.1) | collective-permute-done | bytes 131104 | tf_op jit(solution)/shard_map/ppermute | solution.py:344
  107.6 3.6 %collective-permute-done.4 = f32[4,64,128]{2,1,0:T(8,128)S(1)} collective-permute-done((f32[4,64,128]{2,1,0:T(8,128)S(1)}, f32[4,64,128]{2,1,0:T(8,128)S(1)}, u32[]{:S(2)}, u32[]{:S(2)}) %collective-permute-start.4) | collective-permute-done | bytes 131104 | tf_op jit(solution)/shard_map/ppermute | solution.py:344
  111.2 0.7 fusion.3
  (23 shorter events, 0.5 us)
Async XLA Ops:
  0.0 33.0 %copy-start = (s32[512,2]{0,1:T(2,128)S(1)}, s32[512,2]{0,1:T(2,128)}, u32[]{:S(2)}) copy-start(s32[512,2]{0,1:T(2,128)} %param.12) | copy-start | bytes 12292
  4.0 23.7 %all-to-all-start.1 = ((f32[32,64,128]{2,1,0:T(8,128)}), f32[32,64,128]{2,1,0:T(8,128)S(1)}, u32[]{:S(2)}, u32[]{:S(2)}) async-start(f32[32,64,128]{2,1,0:T(8,128)} %pack.3), calls=%async_computation.1 | async-start | bytes 2097152 | tf_op jit(solution)/shard_map/all_to_all | solution.py:373
  27.8 21.1 %all-to-all-start = ((f32[32,64,128]{2,1,0:T(8,128)}), f32[32,64,128]{2,1,0:T(8,128)S(1)}, u32[]{:S(2)}, u32[]{:S(2)}) async-start(f32[32,64,128]{2,1,0:T(8,128)} %pack.2), calls=%async_computation | async-start | bytes 2097152 | tf_op jit(solution)/shard_map/all_to_all | solution.py:373
  33.2 0.7 copy-start.3
  49.1 14.2 %copy-start.1 = (f32[64,256]{1,0:T(8,128)S(1)}, f32[64,256]{1,0:T(8,128)}, u32[]{:S(2)}) copy-start(f32[64,256]{1,0:T(8,128)} %constant.32.clone.spread_ref) | copy-start | bytes 196612
  49.1 14.2 %copy-start.2 = (f32[64,64]{1,0:T(8,128)S(1)}, f32[64,64]{1,0:T(8,128)}, u32[]{:S(2)}) copy-start(f32[64,64]{1,0:T(8,128)} %constant.31.clone.mix_ref) | copy-start | bytes 49156
  79.2 14.6 %collective-permute-start.2 = (f32[6,64,128]{2,1,0:T(8,128)S(1)}, f32[6,64,128]{2,1,0:T(8,128)S(1)}, u32[]{:S(2)}, u32[]{:S(2)}) collective-permute-start(f32[6,64,128]{2,1,0:T(8,128)S(1)} %pad_maximum_fusion.1), channel_id=1, source_target_pairs={{0,6},{1,7},{2,0},{3,1},{4,2},{5,3},{6,4},{7,5},{8,14},{9,15},{10,... | collective-permute-start | bytes 589832 | tf_op jit(solution)/shard_map/ppermute | solution.py:344
  85.4 12.4 %collective-permute-start = (f32[6,64,128]{2,1,0:T(8,128)S(1)}, f32[6,64,128]{2,1,0:T(8,128)S(1)}, u32[]{:S(2)}, u32[]{:S(2)}) collective-permute-start(f32[6,64,128]{2,1,0:T(8,128)S(1)} %pad_maximum_fusion), channel_id=1, source_target_pairs={{0,2},{1,3},{2,4},{3,5},{4,6},{5,7},{6,0},{7,1},{8,10},{9,11},{10,... | collective-permute-start | bytes 589832 | tf_op jit(solution)/shard_map/ppermute | solution.py:344
  97.8 7.6 %collective-permute-start.3 = (f32[4,64,128]{2,1,0:T(8,128)S(1)}, f32[4,64,128]{2,1,0:T(8,128)S(1)}, u32[]{:S(2)}, u32[]{:S(2)}) collective-permute-start(f32[4,64,128]{2,1,0:T(8,128)S(1)} %pad_maximum_fusion.3), channel_id=1, source_target_pairs={{0,6},{1,7},{2,0},{3,1},{4,2},{5,3},{6,4},{7,5},{8,14},{9,15},{10,... | collective-permute-start | bytes 393224 | tf_op jit(solution)/shard_map/ppermute | solution.py:344
  98.0 9.6 %collective-permute-start.1 = (f32[4,64,128]{2,1,0:T(8,128)S(1)}, f32[4,64,128]{2,1,0:T(8,128)S(1)}, u32[]{:S(2)}, u32[]{:S(2)}) collective-permute-start(f32[4,64,128]{2,1,0:T(8,128)S(1)} %pad_maximum_fusion.2), channel_id=1, source_target_pairs={{0,2},{1,3},{2,4},{3,5},{4,6},{5,7},{6,0},{7,1},{8,10},{9,11},{10,... | collective-permute-start | bytes 393224 | tf_op jit(solution)/shard_map/ppermute | solution.py:344
  100.4 10.8 %collective-permute-start.4 = (f32[4,64,128]{2,1,0:T(8,128)S(1)}, f32[4,64,128]{2,1,0:T(8,128)S(1)}, u32[]{:S(2)}, u32[]{:S(2)}) collective-permute-start(f32[4,64,128]{2,1,0:T(8,128)S(1)} %get-tuple-element.11), channel_id=1, source_target_pairs={{0,1},{1,2},{2,3},{3,4},{4,5},{5,6},{6,7},{7,0},{8,9},{9,10},{10,1... | collective-permute-start | bytes 393224 | tf_op jit(solution)/shard_map/ppermute | solution.py:344
  101.6 9.6 %collective-permute-start.5 = (f32[4,64,128]{2,1,0:T(8,128)S(1)}, f32[4,64,128]{2,1,0:T(8,128)S(1)}, u32[]{:S(2)}, u32[]{:S(2)}) collective-permute-start(f32[4,64,128]{2,1,0:T(8,128)S(1)} %get-tuple-element.12), channel_id=1, source_target_pairs={{0,7},{1,0},{2,1},{3,2},{4,3},{5,4},{6,5},{7,6},{8,15},{9,8},{10,9... | collective-permute-start | bytes 393224 | tf_op jit(solution)/shard_map/ppermute | solution.py:344
